TPU v7x, 256 devices: a whole 4x4x8 slice. The times are simulated.
256 devices in a mesh: ctx: 32 (over z, x), dp: 8 (over y, core).
Axes of the slice: x: 4, y: 4, z: 8, core: 2. Of those that a mesh axis runs over, the one named last changes fastest.
Arguments:
- query: bfloat16 [8, 32, 2, 64, 4096], P('dp', 'ctx'), may hold values from -42 to 42, as said below
- key: bfloat16 [8, 32, 2, 64, 1024], P('dp', 'ctx'), may hold values from -4 to 4, as said below
- value: bfloat16 [8, 32, 2, 64, 1024], P('dp', 'ctx'), may hold values from -6 to 6
- beacon_slot_state: bfloat16 [8, 32, 2, 8, 4096], P('dp', 'ctx'), may hold values from -6 to 6
- frozen_beacon_cache: bfloat16 [8, 32, 2, 8, 2048], P('dp', 'ctx'), may hold values from -6 to 6
- adapter_down_weight: bfloat16 [4096, 64], replicated, may hold values from -0.09375 to 0.09375
- adapter_up_weight: bfloat16 [64, 2048], replicated, may hold values from -0.75 to 0.75
- output_cotangent: bfloat16 [8, 32, 2, 64, 4096], P('dp', 'ctx'), may hold values from -6 to 6
- span_beacon_count: int32 [8, 32, 2], P('dp', 'ctx'), may hold values from 1 to 8, as said below
- span_document: int32 [8, 32, 2], P('dp', 'ctx'), may hold values from 0 to 4, as said below
- boundary: int32 [8, 32, 2], P('dp', 'ctx'), may hold values from 1 to 64, as said below
Outputs:
- attended: bfloat16 [8, 32, 2, 64, 4096], P('dp', 'ctx')
- grad_query: bfloat16 [8, 32, 2, 64, 4096], P('dp', 'ctx')
- grad_key: bfloat16 [8, 32, 2, 64, 1024], P('dp', 'ctx')
- grad_value: bfloat16 [8, 32, 2, 64, 1024], P('dp', 'ctx')
- beacon_cache_gradient: bfloat16 [8, 32, 2, 8, 2048], P('dp', 'ctx')
- adapter_gradient: float32 [64, 6144], replicated
Inputs may be any that keep to these rules, and one draw needn't show every extreme that they name: `span_beacon_count`: the two spans of one pair index hold at most 12 beacons together; in every sequence one pair holds exactly 8 and 4. `span_document`: document numbers start at 0 in span 0 and rise by 0 or 1 from span c to span c + 1 in natural span order; every sequence reaches the largest. Every span that is not the last of its document has boundary 64. `query`: queries are real values. `key`: keys are real values.
All inputs are finite; a program needn't handle non-finite values.
Results may differ from a plain program's by a relative error of at most 0.02.
Values may be sent and summed in bfloat16 or wider, within the bound.
No kernel may reach another device: no remote copies, remote signals or barrier semaphores. Data moves between devices by JAX's collectives and lax.ppermute only.
A program may use at most 128 MiB of HBM per device.

v0:
```python
import jax
import jax.numpy as jnp
from jax import lax
from jax.sharding import PartitionSpec as P

MODEL_WIDTH = 4096
KVH = 8
HD = 128
SPAN = 64
MAX_BEACONS = 8
GROUP = 4
QW = 4096
KEY_FEATURES = 1024


masked_score = -1e30


def attend(
    query,
    key,
    value,
    output_cotangent,
    beacon_states,
    own_span,
    own_doc,
    live_lengths,
    slot_span,
    slot_doc,
):
    score_scale = HD ** (-0.5)
    positions = jnp.arange(SPAN)
    live_rows = positions[None, :] < live_lengths[:, None]
    near_mask = (positions[None, None, :] <= positions[None, :, None]) & (
        live_rows[:, :, None] == live_rows[:, None, :]
    )
    far_mask = (
        live_rows[:, :, None]
        & (slot_span[None, None, :] < own_span[:, None, None])
        & (slot_doc[None, None, :] == own_doc[:, None, None])
    )
    visible = jnp.concatenate([near_mask, far_mask], axis=2)[:, None, None]
    query_heads = query.reshape(2, SPAN, KVH, GROUP, HD)
    key_heads = key.reshape(2, SPAN, KVH, HD)
    value_heads = value.reshape(2, SPAN, KVH, HD)
    grad_heads = output_cotangent.reshape(2, SPAN, KVH, GROUP, HD)
    beacon_keys = beacon_states[:, :KEY_FEATURES].reshape(-1, KVH, HD)
    beacon_values = beacon_states[:, KEY_FEATURES:].reshape(-1, KVH, HD)
    scores = (
        jnp.concatenate(
            [
                jnp.einsum(
                    "sqgmd,skgd->sgmqk", query_heads, key_heads, preferred_element_type=jnp.float32
                ),
                jnp.einsum(
                    "sqgmd,kgd->sgmqk", query_heads, beacon_keys, preferred_element_type=jnp.float32
                ),
            ],
            axis=4,
        )
        * score_scale
    )
    scores = jnp.where(visible, scores, masked_score)
    row_max = jnp.max(scores, axis=4, keepdims=True)
    log_total = row_max + jnp.log(jnp.sum(jnp.exp(scores - row_max), axis=4, keepdims=True))
    probs_exact = jnp.exp(scores - log_total)
    probs = probs_exact.astype(jnp.bfloat16)
    near_probs = probs[..., :SPAN]
    far_probs = probs[..., SPAN:]
    summed = jnp.einsum(
        "sgmqk,skgd->sqgmd", near_probs, value_heads, preferred_element_type=jnp.float32
    ) + jnp.einsum("sgmqk,kgd->sqgmd", far_probs, beacon_values, preferred_element_type=jnp.float32)
    attended = summed.astype(jnp.bfloat16)
    attended_heads = lax.optimization_barrier(attended).astype(jnp.float32)
    row_delta = jnp.transpose(
        jnp.sum(grad_heads.astype(jnp.float32) * attended_heads, axis=4), (0, 2, 3, 1)
    )[..., None]
    grad_probs = jnp.concatenate(
        [
            jnp.einsum(
                "sqgmd,skgd->sgmqk", grad_heads, value_heads, preferred_element_type=jnp.float32
            ),
            jnp.einsum(
                "sqgmd,kgd->sgmqk", grad_heads, beacon_values, preferred_element_type=jnp.float32
            ),
        ],
        axis=4,
    )
    grad_scores = (probs_exact * (grad_probs - row_delta)).astype(jnp.bfloat16)
    near_grads = grad_scores[..., :SPAN]
    far_grads = grad_scores[..., SPAN:]
    grad_query = (
        jnp.einsum("sgmqk,skgd->sqgmd", near_grads, key_heads, preferred_element_type=jnp.float32)
        + jnp.einsum("sgmqk,kgd->sqgmd", far_grads, beacon_keys, preferred_element_type=jnp.float32)
    ) * score_scale
    grad_key = (
        jnp.einsum("sgmqk,sqgmd->skgd", near_grads, query_heads, preferred_element_type=jnp.float32)
        * score_scale
    )
    grad_value = jnp.einsum(
        "sgmqk,sqgmd->skgd", near_probs, grad_heads, preferred_element_type=jnp.float32
    )
    result_list = (
        attended.reshape(2, SPAN, QW),
        grad_query.astype(jnp.bfloat16).reshape(2, SPAN, QW),
        grad_key.astype(jnp.bfloat16).reshape(2, SPAN, KEY_FEATURES),
        grad_value.astype(jnp.bfloat16).reshape(2, SPAN, KEY_FEATURES),
    )
    return (result_list, far_grads, far_probs, query_heads, grad_heads)


def local(
    query,
    key,
    value,
    beacon_slot_state,
    frozen_beacon_cache,
    adapter_down_weight,
    adapter_up_weight,
    output_cotangent,
    span_beacon_count,
    span_document,
    boundary,
):
    pair_count = lax.axis_size("ctx")
    device_index = lax.axis_index("ctx")
    own_span = jnp.stack([device_index, 2 * pair_count - 1 - device_index])
    counts = span_beacon_count[0, 0]
    doc_ids = span_document[0, 0]
    live_lengths = boundary[0, 0]
    flattened_state = beacon_slot_state[0, 0].reshape(2 * MAX_BEACONS, MODEL_WIDTH)
    reduced_state = jnp.dot(
        flattened_state, adapter_down_weight, preferred_element_type=jnp.float32
    ).astype(jnp.bfloat16)
    states = (
        frozen_beacon_cache[0, 0].reshape(2 * MAX_BEACONS, 2 * KEY_FEATURES)
        + jnp.dot(reduced_state, adapter_up_weight, preferred_element_type=jnp.float32)
    ).astype(jnp.bfloat16)
    slot_ids = jnp.arange(2 * MAX_BEACONS)
    which_side = slot_ids // MAX_BEACONS
    valid_slots = slot_ids % MAX_BEACONS < counts[which_side]
    send_span = own_span[which_side]
    send_doc = jnp.where(valid_slots, doc_ids[which_side], -1)
    slot_rows = states.shape[0]
    gathered, all_spans, all_docs = (
        lax.all_gather(states[None, None], "ctx", axis=1, tiled=True),
        lax.all_gather(send_span[None, None], "ctx", axis=1, tiled=True),
        lax.all_gather(send_doc[None, None], "ctx", axis=1, tiled=True),
    )
    all_states = gathered[0].reshape(-1, 2 * KEY_FEATURES)
    result_list, far_grads, far_probs, query_heads, grad_heads = attend(
        query[0, 0],
        key[0, 0],
        value[0, 0],
        output_cotangent[0, 0],
        all_states,
        own_span,
        doc_ids,
        live_lengths,
        all_spans.reshape(-1),
        all_docs.reshape(-1),
    )
    score_scale = HD ** (-0.5)
    key_part = (
        jnp.einsum("sgmqk,sqgmd->kgd", far_grads, query_heads, preferred_element_type=jnp.float32)
        * score_scale
    )
    value_part = jnp.einsum(
        "sgmqk,sqgmd->kgd", far_probs, grad_heads, preferred_element_type=jnp.float32
    )
    returned_values = lax.psum_scatter(
        jnp.concatenate(
            [
                key_part.reshape(lax.axis_size("ctx") * slot_rows, KEY_FEATURES),
                value_part.reshape(lax.axis_size("ctx") * slot_rows, KEY_FEATURES),
            ],
            axis=1,
        ),
        "ctx",
        scatter_dimension=0,
        tiled=True,
    ).astype(jnp.bfloat16)
    reduced_gradient = jnp.dot(
        returned_values, adapter_up_weight.T, preferred_element_type=jnp.float32
    ).astype(jnp.bfloat16)
    down_factor_piece = jnp.dot(
        reduced_gradient.T, flattened_state, preferred_element_type=jnp.float32
    )
    up_factor_piece = jnp.dot(reduced_state.T, returned_values, preferred_element_type=jnp.float32)
    adapter_gradient = lax.psum(
        jnp.concatenate([down_factor_piece, up_factor_piece], axis=1), ("ctx", "dp")
    )
    attended, grad_query, grad_key, grad_value = result_list
    return (
        attended[None, None],
        grad_query[None, None],
        grad_key[None, None],
        grad_value[None, None],
        returned_values.reshape(1, 1, 2, MAX_BEACONS, 2 * KEY_FEATURES),
        adapter_gradient,
    )


def solution(mesh):
    return jax.shard_map(
        local,
        mesh=mesh,
        in_specs=(
            P("dp", "ctx", None, None, None),
            P("dp", "ctx", None, None, None),
            P("dp", "ctx", None, None, None),
            P("dp", "ctx", None, None, None),
            P("dp", "ctx", None, None, None),
            P(),
            P(),
            P("dp", "ctx", None, None, None),
            P("dp", "ctx", None),
            P("dp", "ctx", None),
            P("dp", "ctx", None),
        ),
        out_specs=(
            P("dp", "ctx", None, None, None),
            P("dp", "ctx", None, None, None),
            P("dp", "ctx", None, None, None),
            P("dp", "ctx", None, None, None),
            P("dp", "ctx", None, None, None),
            P(),
        ),
        check_vma=False,
    )
```

profile of v0, /device:TPU:1, one launch (start us, length us, event | category | flops | bytes accessed | tf_op | source)
XLA Modules:
  0.0 627.9 jit_solution(4446207362241377549)
XLA Ops:
  13.8 2.6 fusion.54
  16.4 35.8 %all_gather.10 = s32[1,32,16]{2,0,1:T(1,128)S(1)} all-gather(s32[1,1,16]{2,0,1:T(1,128)S(1)} %fusion.54), channel_id=1, replica_groups=mesh['ctx'=32,'dp'=8] {'ctx'}, dimensions={1}, use_global_device_ids=true | all-gather | bytes 2112 | tf_op jit(solution)/shard_map/all_gather | solution.py:148
  57.3 2.6 reshape_squeeze.20
  61.2 14.0 %all-reduce = s32[512]{0:T(512)S(1)} all-reduce(s32[512]{0:T(512)S(1)} %bitcast_dynamic-update-slice_fusion), channel_id=4, replica_groups=mesh['ctx'=32,'dp'=8] {'ctx'}, use_global_device_ids=true, to_apply=%add | all-reduce | flops 512 | bytes 4096
  75.9 1.8 convolution_bitcast_fusion.3
  77.8 2.1 convolution_bitcast_fusion.2
  79.8 9.6 %all-gather.5.cloned.1.call-done = bf16[512,2048]{1,0:T(8,128)(2,1)} async-done(((bf16[16,2048]{1,0:T(8,128)(2,1)}), bf16[512,2048]{1,0:T(8,128)(2,1)}) %all-gather.5.cloned.1.call-update) | async-done | bytes 2097168 | tf_op jit(solution)/shard_map/all_gather | solution.py:146
  92.8 4.3 fusion.28
  97.1 5.0 exponential_reduce_fusion
  102.2 4.0 fusion.3
  106.6 3.3 fusion.8
  111.5 2.1 fusion.15
  114.4 7.9 %fusion.2 = bf16[2,8,4,64,576]{4,3,2,0,1:T(8,128)(2,1)S(1)} fusion(f32[2,8,4,64,512]{4,3,2,0,1:T(8,128)S(1)} %convolution_bitcast_fusion, f32[2,8,4,64,64]{4,3,2,0,1:T(8,128)S(1)} %copy-done.4, f32[2,8,4,64]{3,2,0,1:T(4,128)S(1)} %bitcast.150, f32[2,8,4,64,512]{4,3,2,0,1:T(8,128)S(1)} %convolution_bitcast_fusion.1, pred[2,64,576]{2,1,0:T(8,128)(4,1)S(1)} %pad_add_fusion, ...), kind=kLoop, calls=%fused_computation.4 | loop fusion | flops 18874368 | bytes 23699456 | tf_op jit(solution)/shard_map/convert_element_type | solution.py:89
  122.4 2.5 bitcast_multiply_fusion
  125.5 2.4 pad_maximum_fusion
  127.9 5.5 copy.172
  135.3 1.9 fusion.26
  138.2 2.7 broadcast_in_dim_reshape.14
  140.8 1.9 fusion.25
  143.7 3.1 fusion.35
  146.8 203.8 %reduce-scatter.4.cloned.1.call-done = f32[16,2048]{1,0:T(8,128)} async-done(((f32[512,2048]{1,0:T(8,128)}), f32[16,2048]{1,0:T(8,128)}) %reduce-scatter.4.cloned.1.call-update) | async-done | bytes 131088 | tf_op jit(solution)/shard_map/reduce_scatter | solution.py:171
  354.7 5.1 fusion.14
  362.8 255.9 %all-reduce.3.cloned.1.call-done = f32[64,6144]{1,0:T(8,128)} async-done(((f32[64,6144]{1,0:T(8,128)}), f32[64,6144]{1,0:T(8,128)}) %all-reduce.3.cloned.1.call-update) | async-done | bytes 1572880 | tf_op jit(solution)/shard_map/psum | solution.py:190
  618.7 2.7 copy.245
  (88 shorter events, 30.7 us)
Async XLA Ops:
  7.2 1.1 copy-start
  7.2 52.7 %copy-start.19 = (u32[256]{0:T(256)S(1)}, u32[256]{0:T(256)}, u32[]{:S(2)}) copy-start(u32[256]{0:T(256)} %constant.71) | copy-start | bytes 3076
  7.2 68.2 %copy-start.17 = (s32[1,1,2]{2,1,0:T(1,128)S(1)}, s32[1,1,2]{2,1,0:T(1,128)}, u32[]{:S(2)}) copy-start(s32[1,1,2]{2,1,0:T(1,128)} %param.20) | copy-start | bytes 28
  7.2 68.1 %copy-start.18 = (s32[1,1,2]{2,1,0:T(1,128)S(1)}, s32[1,1,2]{2,1,0:T(1,128)}, u32[]{:S(2)}) copy-start(s32[1,1,2]{2,1,0:T(1,128)} %param.21) | copy-start | bytes 28
  7.2 82.2 %all-gather.5.cloned.1.call-start = ((), (), s32[]{:S(2)}) async-start(), calls=%async_computation.2 | async-start | bytes 2162688 | tf_op jit(solution)/shard_map/all_gather | solution.py:146
  11.2 339.5 %reduce-scatter.4.cloned.1.call-start = ((), (), s32[]{:S(2)}) async-start(), calls=%async_computation.3 | async-start | bytes 4325376 | tf_op jit(solution)/shard_map/reduce_scatter | solution.py:171
  75.9 1.8 copy-start.11
  89.5 2.1 copy-start.2
  91.5 1.3 copy-start.7
  102.2 4.0 copy-start.12
  106.2 7.4 %copy-start.5 = (bf16[2,8,4,64,576]{4,3,2,0,1:T(8,128)(2,1)}, bf16[2,8,4,64,576]{4,3,2,0,1:T(8,128)(2,1)S(1)}, u32[]{:S(2)}) copy-start(bf16[2,8,4,64,576]{4,3,2,0,1:T(8,128)(2,1)S(1)} %fusion.3) | copy-start | bytes 14155780
  111.5 2.9 copy-start.4
  113.6 8.7 %copy-start.9 = (bf16[2,64,8,4,128]{4,1,3,2,0:T(8,128)(2,1)}, bf16[2,64,8,4,128]{4,1,3,2,0:T(8,128)(2,1)S(1)}, u32[]{:S(2)}) copy-start(bf16[2,64,8,4,128]{4,1,3,2,0:T(8,128)(2,1)S(1)} %fusion.15) | copy-start | bytes 3145732
  122.3 2.5 copy-start.6
  122.4 3.2 copy-start.13
  127.9 5.6 copy-start.10
  133.4 7.4 %copy-start.3 = (bf16[2,64,8,4,128]{4,3,2,1,0:T(4,128)(2,1)S(1)}, bf16[2,64,8,4,128]{4,3,2,1,0:T(4,128)(2,1)}, u32[]{:S(2)}) copy-start(bf16[2,64,8,4,128]{4,3,2,1,0:T(4,128)(2,1)} %reshape_squeeze.20) | copy-start | bytes 3145732
  133.4 485.3 %all-reduce.3.cloned.1.call-start = ((), (), s32[]{:S(2)}) async-start(), calls=%async_computation.1 | async-start | bytes 3145728 | tf_op jit(solution)/shard_map/psum | solution.py:190
  138.2 213.6 %copy-start.15 = (bf16[64,2048]{1,0:T(8,128)(2,1)S(1)}, bf16[64,2048]{1,0:T(8,128)(2,1)}, u32[]{:S(2)}) copy-start(bf16[64,2048]{1,0:T(8,128)(2,1)} %param.17) | copy-start | bytes 786436
  138.2 213.6 %copy-start.16 = (bf16[1,1,2,8,4096]{4,3,2,1,0:T(8,128)(2,1)S(1)}, bf16[1,1,2,8,4096]{4,3,2,1,0:T(8,128)(2,1)}, u32[]{:S(2)}) copy-start(bf16[1,1,2,8,4096]{4,3,2,1,0:T(8,128)(2,1)} %param.14) | copy-start | bytes 393220
  143.7 210.9 %copy-start.8 = (bf16[64,8,8,128]{3,2,1,0:T(8,128)(2,1)S(1)}, bf16[64,8,8,128]{3,2,1,0:T(8,128)(2,1)}, u32[]{:S(2)}) copy-start(bf16[64,8,8,128]{3,2,1,0:T(8,128)(2,1)} %copy-done.7) | copy-start | bytes 3145732
  354.6 7.6 %copy-start.14 = (f32[16,2048]{1,0:T(8,128)S(1)}, f32[16,2048]{1,0:T(8,128)}, u32[]{:S(2)}) copy-start(f32[16,2048]{1,0:T(8,128)} %reduce-scatter.4.cloned.1.call-done) | copy-start | bytes 393220
  354.7 266.7 %copy-start.1 = (bf16[4096,64]{0,1:T(8,128)(2,1)S(1)}, bf16[4096,64]{0,1:T(8,128)(2,1)}, u32[]{:S(2)}) copy-start(bf16[4096,64]{0,1:T(8,128)(2,1)} %param.16) | copy-start | bytes 1572868
Sparse Core Ops, SparseCore 0:
  11.3 78.1 all-gather.4
  133.6 217.0 reduce-scatter.3
  357.4 261.2 all-reduce.2
where the time goes:
time: 629 us; the launch traced here: 628 us
  waiting for transfers between devices  469 us (75%)
  blocking collectives  49.7 us (8%)
  matrix products  32.3 us (5%)
  local copies, waits for them, and re-layouts  31.2 us (5%)
  other arithmetic  30.4 us (5%)
  between operations  14.8 us (2%)
    psum x1, waiting for transfers between devices, local(): lax.psum(jnp.concatenate([down_factor_piece, up_factor_piece], axis=1), (...  256 us
    reduce_scatter x1, waiting for transfers between devices, local(): lax.psum_scatter(jnp.concatenate([key_part.reshape(lax.axis_size('ctx') *...  204 us
    all_gather x1, blocking collectives, local(): lax.all_gather(send_doc[None, None], 'ctx', axis=1, tiled=True)  35.8 us
    unnamed x49, local copies, waits for them, and re-layouts  14.8 us
    unnamed x1, blocking collectives  14 us
  transfers between devices with their start and end apart: 3, of which 3 were waited for; matrix products, arithmetic and copies ran while one was open for 6% of the time, Pallas kernels for 0%

commit v1 on v0

v1 whole, which is shorter than its diff:
```python
import functools

import jax
import jax.numpy as jnp
from jax import lax
from jax.experimental import pallas as pl
from jax.experimental.pallas import tpu as pltpu
from jax.sharding import Mesh, PartitionSpec as P

MODEL_WIDTH = 4096
KVH = 8
HD = 128
SPAN = 64
MAX_BEACONS = 8
UPDATE_RANK = 64
GROUP = 4
QW = 4096
KEY_FEATURES = 1024
NCH = 64
NZ, NX, NY, NC = 8, 4, 4, 2

bf16 = jnp.bfloat16
f32 = jnp.float32
ALL_AXES = ("z", "x", "y", "core")
WIDE = ("x", "y", "core")

TILES = 26
GRAD_TILES = 24
FAR = 384
NEAR = 128
KEYS = FAR + NEAR
ROWS = GROUP * 2 * SPAN
MASKED = -1e30
SCORE_SCALE = HD ** (-0.5)
LOG2E = 1.4426950408889634


def dot(a, b, dims=((1,), (0,))):
    return lax.dot_general(a, b, (dims, ((), ())), preferred_element_type=f32)


def selection(first, second):
    row = lax.broadcasted_iota(jnp.int32, (16, 16), 0)
    slot = lax.broadcasted_iota(jnp.int32, (16, 16), 1)
    source = jnp.where(row < first, row, row - first + MAX_BEACONS)
    return jnp.where((slot == source) & (row < first + second), 1.0, 0.0)


def project_kernel(info, state, down, up, frozen, out, low_out):
    first, second = info[0], info[1]
    low = dot(state[...], down[...]).astype(bf16)
    low_out[...] = low
    states = (frozen[...].astype(f32) + dot(low, up[...])).astype(bf16)
    pick = selection(first, second).astype(bf16)
    rows = dot(pick, states)
    low_rows = dot(pick, low).astype(bf16)
    sub = lax.broadcasted_iota(jnp.int32, (8, HD), 0)
    tiles = []
    for h in range(2 * KVH):
        tiles.append(rows[:8, h * HD : (h + 1) * HD])
    for h in range(KVH):
        keys = rows[8:, h * HD : (h + 1) * HD]
        values = rows[8:, (KVH + h) * HD : (KVH + h + 1) * HD]
        tiles.append(jnp.where(sub < 4, keys, pltpu.roll(values, 4, 0)))
    put_row = lax.broadcasted_iota(jnp.int32, (UPDATE_RANK, HD), 0)
    put_col = lax.broadcasted_iota(jnp.int32, (UPDATE_RANK, HD), 1)
    left = jnp.where(put_row == put_col, 1.0, 0.0).astype(bf16)
    right = jnp.where(put_row + UPDATE_RANK == put_col, 1.0, 0.0).astype(bf16)
    tiles.append((dot(low_rows, left)[:8] + dot(low_rows, right)[8:]))
    facts = jnp.zeros((8, HD), f32)
    for i in range(4):
        facts = jnp.where(sub == i, info[i].astype(f32), facts)
    tiles.append(facts)
    for t, tile in enumerate(tiles):
        packed = tile.astype(bf16)
        for z in range(NZ):
            out[z, t] = packed


def project(info, state, down, up, frozen):
    vmem = pl.BlockSpec(memory_space=pltpu.VMEM)
    return pl.pallas_call(
        project_kernel,
        in_specs=[pl.BlockSpec(memory_space=pltpu.SMEM)] + [vmem] * 4,
        out_specs=[vmem, vmem],
        out_shape=[
            jax.ShapeDtypeStruct((NZ, TILES, 8, HD), bf16),
            jax.ShapeDtypeStruct((16, UPDATE_RANK), bf16),
        ],
        name="project",
    )(info, state, down, up, frozen)


def fill_bias(info, boxes, bias):
    z_own, x_own = info[0], info[1]
    pair = z_own * NX + x_own
    lane = lax.broadcasted_iota(jnp.int32, (8, NEAR), 1)
    sub = lax.broadcasted_iota(jnp.int32, (8, NEAR), 0)
    side = lane // SPAN
    offset = lane % SPAN
    own_span = jnp.where(side == 0, pair, NCH - 1 - pair).astype(f32)
    own_doc = jnp.where(side == 0, info[2], info[3]).astype(f32)
    live = offset < jnp.where(side == 0, info[4], info[5])
    for block in range(NEAR // 8):
        key_side = block * 8 // SPAN
        key_offset = sub + (block * 8) % SPAN
        key_live = key_offset < info[4 + key_side]
        seen = (side == key_side) & (key_offset <= offset) & (key_live == live)
        bias[block * 8 : block * 8 + 8, :] = jnp.where(seen, 0.0, MASKED)

    def facts(box, z, slot):
        tile = boxes[box][z, 25].astype(f32)
        first, second = tile[0:1], tile[1:2]
        first_doc, second_doc = tile[2:3], tile[3:4]
        source = z * NX + lax.rem(x_own - box + NX, NX)
        low = slot < first
        high = slot < first + second
        span = jnp.where(low, source, NCH - 1 - source).astype(f32)
        doc = jnp.where(low, first_doc, second_doc)
        return jnp.where(high, span, 2.0 * NCH), doc

    def write(at, span, doc):
        seen = live & (span < own_span) & (doc == own_doc)
        bias[at : at + 8, :] = jnp.where(seen, 0.0, MASKED)

    slot = sub.astype(f32)
    for box in range(NX):
        for z in range(NZ):
            write(NEAR + box * 64 + z * 8, *facts(box, z, slot))
        for z in range(0, NZ, 2):
            span_a, doc_a = facts(box, z, slot + 8.0)
            span_b, doc_b = facts(box, z + 1, slot + 4.0)
            write(
                NEAR + 256 + box * 32 + z * 4,
                jnp.where(sub < 4, span_a, span_b),
                jnp.where(sub < 4, doc_a, doc_b),
            )


def attend_kernel(
    info, query, key, value, grad, box0, box1, box2, box3,
    attended, grad_query, grad_key, grad_value, out0, out1, out2, out3, bias,
):
    boxes = (box0, box1, box2, box3)
    outs = (out0, out1, out2, out3)
    g = pl.program_id(0)

    @pl.when(g == 0)
    def _():
        fill_bias(info, boxes, bias)

    sub = lax.broadcasted_iota(jnp.int32, (NZ // 2, 8, HD), 1)

    def stack(ref):
        whole = ref[...].reshape(2 * SPAN, GROUP * HD)
        return jnp.concatenate(
            [whole[:, m * HD : (m + 1) * HD] for m in range(GROUP)], axis=0
        )

    def far_rows(tile):
        return [box[:, tile].astype(f32).reshape(8 * NZ, HD) for box in boxes]

    extra_keys, extra_values = [], []
    for box in boxes:
        both = box[:, 16 + g].astype(f32).reshape(NZ // 2, 2, 8, HD)
        even, odd = both[:, 0], both[:, 1]
        extra_keys.append(jnp.where(sub < 4, even, pltpu.roll(odd, 4, 1)).reshape(4 * NZ, HD))
        extra_values.append(jnp.where(sub < 4, pltpu.roll(even, 4, 1), odd).reshape(4 * NZ, HD))
    keys = jnp.concatenate(
        [key[...].reshape(NEAR, HD).astype(f32)] + far_rows(g) + extra_keys, axis=0
    )
    values = jnp.concatenate(
        [value[...].reshape(NEAR, HD).astype(f32)] + far_rows(KVH + g) + extra_values, axis=0
    )
    keys_t = keys.T.astype(bf16)
    values_t = values.T.astype(bf16)
    keys = keys.astype(bf16)
    values = values.astype(bf16)
    queries = stack(query)
    grads = stack(grad)
    grads_t = grads.astype(f32).T

    scores = dot(keys, queries, ((1,), (1,))) * (SCORE_SCALE * LOG2E)
    scores = scores + jnp.tile(bias[...], (1, GROUP))
    top = jnp.max(scores, axis=0, keepdims=True)
    weights = jnp.exp2(scores - top)
    total = jnp.sum(weights, axis=0, keepdims=True)
    exact = weights * (1.0 / total)
    probs = exact.astype(bf16)
    summed_t = dot(values_t, probs)
    summed = summed_t.T.astype(bf16)
    rounded_t = summed_t.astype(bf16).astype(f32)
    delta = jnp.sum(grads_t * rounded_t, axis=0, keepdims=True)
    grad_probs = dot(values, grads_t.astype(bf16))
    grad_scores = (exact * (grad_probs - delta)).astype(bf16)
    query_grad = (dot(keys_t, grad_scores) * SCORE_SCALE).T.astype(bf16)
    key_grad = dot(grad_scores, queries) * SCORE_SCALE
    value_grad = dot(probs, grads)

    for m in range(GROUP):
        at = slice(m * 2 * SPAN, (m + 1) * 2 * SPAN)
        cols = slice(m * HD, (m + 1) * HD)
        attended[:, :, cols] = summed[at].reshape(2, SPAN, HD)
        grad_query[:, :, cols] = query_grad[at].reshape(2, SPAN, HD)
    grad_key[...] = key_grad[:NEAR].astype(bf16).reshape(2, SPAN, HD)
    grad_value[...] = value_grad[:NEAR].astype(bf16).reshape(2, SPAN, HD)
    for b, out in enumerate(outs):
        at = NEAR + b * 64
        out[:, 0, 0] = key_grad[at : at + 64].reshape(NZ, 8, HD).astype(bf16)
        out[:, 1, 0] = value_grad[at : at + 64].reshape(NZ, 8, HD).astype(bf16)
        at = NEAR + 256 + b * 32
        k = key_grad[at : at + 32].reshape(NZ // 2, 8, HD)
        v = value_grad[at : at + 32].reshape(NZ // 2, 8, HD)
        even = jnp.where(sub < 4, k, pltpu.roll(v, 4, 1)).astype(bf16)
        odd = jnp.where(sub < 4, pltpu.roll(k, 4, 1), v).astype(bf16)
        for i in range(NZ // 2):
            out[2 * i, 2, 0] = even[i]
            out[2 * i + 1, 2, 0] = odd[i]


def attend(info, query, key, value, grad, boxes):
    wide = pl.BlockSpec((2, SPAN, GROUP * HD), lambda g: (0, 0, g))
    narrow = pl.BlockSpec((2, SPAN, HD), lambda g: (0, 0, g))
    whole = pl.BlockSpec((NZ, TILES, 8, HD), lambda g: (0, 0, 0, 0))
    part = pl.BlockSpec((NZ, 3, 1, 8, HD), lambda g: (0, 0, g, 0, 0))
    wide_shape = jax.ShapeDtypeStruct((2, SPAN, QW), bf16)
    narrow_shape = jax.ShapeDtypeStruct((2, SPAN, KEY_FEATURES), bf16)
    part_shape = jax.ShapeDtypeStruct((NZ, 3, KVH, 8, HD), bf16)
    return pl.pallas_call(
        attend_kernel,
        grid=(KVH,),
        in_specs=[pl.BlockSpec(memory_space=pltpu.SMEM), wide, narrow, narrow, wide] + [whole] * NX,
        out_specs=[wide, wide, narrow, narrow] + [part] * NX,
        out_shape=[wide_shape, wide_shape, narrow_shape, narrow_shape] + [part_shape] * NX,
        scratch_shapes=[pltpu.VMEM((KEYS, NEAR), f32)],
        compiler_params=pltpu.CompilerParams(vmem_limit_bytes=48 * 1024 * 1024),
        name="attend",
    )(info, query, key, value, grad, *boxes)


def finish_kernel(info, parts, up, state, low, cache_out, pieces):
    pick = selection(info[0], info[1]).astype(bf16)
    total = jnp.sum(parts[...].astype(f32), axis=0)
    sub = lax.broadcasted_iota(jnp.int32, (8, HD), 0)
    tops = [total[h] for h in range(2 * KVH)]
    rest_keys, rest_values = [], []
    for h in range(KVH):
        both = total[16 + h]
        rest_keys.append(jnp.where(sub < 4, both, 0.0))
        rest_values.append(jnp.where(sub < 4, pltpu.roll(both, 4, 0), 0.0))
    compact = jnp.concatenate(
        [jnp.concatenate(tops, axis=1), jnp.concatenate(rest_keys + rest_values, axis=1)], axis=0
    ).astype(bf16)
    cache = dot(pick, compact, ((0,), (0,))).astype(bf16)
    cache_out[...] = cache
    low_grad = dot(cache, up[...], ((1,), (1,))).astype(bf16)
    down_piece = dot(low_grad, state[...], ((0,), (0,)))
    up_piece = dot(low[...], cache, ((0,), (0,)))
    per_row = (MODEL_WIDTH + 2 * KEY_FEATURES) // HD
    for t in range(8 * per_row):
        r, c = divmod(t, per_row)
        if c < MODEL_WIDTH // HD:
            tile = down_piece[r * 8 : r * 8 + 8, c * HD : (c + 1) * HD]
        else:
            c -= MODEL_WIDTH // HD
            tile = up_piece[r * 8 : r * 8 + 8, c * HD : (c + 1) * HD]
        pieces[t // 12, t % 12] = tile.astype(bf16)


def finish(info, parts, up, state, low):
    vmem = pl.BlockSpec(memory_space=pltpu.VMEM)
    return pl.pallas_call(
        finish_kernel,
        in_specs=[pl.BlockSpec(memory_space=pltpu.SMEM)] + [vmem] * 4,
        out_specs=[vmem, vmem],
        out_shape=[
            jax.ShapeDtypeStruct((16, 2 * KEY_FEATURES), bf16),
            jax.ShapeDtypeStruct((32, 12, 8, HD), bf16),
        ],
        name="finish",
    )(info, parts, up, state, low)


def add_kernel(copies, parts, out):
    total = jnp.sum(parts[...].astype(f32), axis=0).astype(bf16)
    for i in range(copies):
        out[i] = total


def add_and_copy(parts, copies, name):
    vmem = pl.BlockSpec(memory_space=pltpu.VMEM)
    return pl.pallas_call(
        functools.partial(add_kernel, copies),
        in_specs=[vmem],
        out_specs=vmem,
        out_shape=jax.ShapeDtypeStruct((copies,) + parts.shape[1:], bf16),
        name=name,
    )(parts)


def add_four_kernel(a, b, c, d, out):
    out[...] = (
        (a[...].astype(f32) + b[...].astype(f32)) + (c[...].astype(f32) + d[...].astype(f32))
    ).astype(bf16)


def add_four(parts):
    vmem = pl.BlockSpec(memory_space=pltpu.VMEM)
    return pl.pallas_call(
        add_four_kernel,
        in_specs=[vmem] * 4,
        out_specs=vmem,
        out_shape=jax.ShapeDtypeStruct(parts[0].shape, bf16),
        name="add_four",
    )(*parts)


def unpack_kernel(tiles, out):
    per_row = (MODEL_WIDTH + 2 * KEY_FEATURES) // HD
    for t in range(8 * per_row):
        r, c = divmod(t, per_row)
        out[r * 8 : r * 8 + 8, c * HD : (c + 1) * HD] = tiles[t // 12, t % 12].astype(f32)


def unpack(tiles):
    vmem = pl.BlockSpec(memory_space=pltpu.VMEM)
    return pl.pallas_call(
        unpack_kernel,
        in_specs=[vmem],
        out_specs=vmem,
        out_shape=jax.ShapeDtypeStruct((UPDATE_RANK, MODEL_WIDTH + 2 * KEY_FEATURES), f32),
        name="unpack",
    )(tiles)


def exchange(x, axes):
    return lax.all_to_all(x, axes, 0, 0, tiled=True)


def shift(x, by):
    return lax.ppermute(x, "x", [(i, (i + by) % NX) for i in range(NX)])


def local(
    query, key, value, beacon_slot_state, frozen_beacon_cache, adapter_down_weight,
    adapter_up_weight, output_cotangent, span_beacon_count, span_document, boundary,
):
    counts = span_beacon_count[0, 0]
    docs = span_document[0, 0]
    ends = boundary[0, 0]
    z_own = lax.axis_index("z").astype(jnp.int32)
    x_own = lax.axis_index("x").astype(jnp.int32)
    state = beacon_slot_state[0, 0].reshape(2 * MAX_BEACONS, MODEL_WIDTH)
    frozen = frozen_beacon_cache[0, 0].reshape(2 * MAX_BEACONS, 2 * KEY_FEATURES)
    pair_info = jnp.concatenate([counts, docs])
    place_info = jnp.concatenate([jnp.stack([z_own, x_own]), docs, ends])

    message, low = project(pair_info, state, adapter_down_weight, adapter_up_weight, frozen)
    column = exchange(message, "z")
    boxes = [column, shift(column, 1), shift(column, 2), shift(column, 3)]
    attended, grad_query, grad_key, grad_value, *parts = attend(
        place_info, query[0, 0], key[0, 0], value[0, 0], output_cotangent[0, 0], boxes
    )
    parts = [p.reshape(NZ, GRAD_TILES, 8, HD) for p in parts]
    mine = add_four([parts[0], shift(parts[1], -1), shift(parts[2], -2), shift(parts[3], -3)])
    cache_gradient, pieces = finish(
        pair_info, exchange(mine, "z"), adapter_up_weight, state, low
    )
    wide = add_and_copy(exchange(pieces, WIDE), NZ, "add_wide")
    full = add_and_copy(exchange(wide, "z"), 32, "add_z")
    adapter_gradient = unpack(exchange(full, WIDE))
    return (
        attended[None, None],
        grad_query[None, None],
        grad_key[None, None],
        grad_value[None, None],
        cache_gradient.reshape(1, 1, 2, MAX_BEACONS, 2 * KEY_FEATURES),
        adapter_gradient,
    )


def solution(mesh):
    chips = Mesh(mesh.devices.reshape(NZ, NX, NY, NC), ALL_AXES)
    dp, ctx = ("y", "core"), ("z", "x")
    array5 = P(dp, ctx, None, None, None)
    array3 = P(dp, ctx, None)
    return jax.shard_map(
        local,
        mesh=chips,
        in_specs=(array5, array5, array5, array5, array5, P(), P(), array5, array3, array3, array3),
        out_specs=(array5, array5, array5, array5, array5, P()),
        check_vma=False,
    )
```

time: 629 us -> 177 us (0.28)
  waiting for transfers between devices: 469 us -> 40.8 us
  blocking collectives: 49.7 us -> 95.8 us
  matrix products: 32.3 us -> 0 us
  other arithmetic: 30.4 us -> 0.63 us
  Pallas kernels: 0 us -> 27.5 us
  local copies, waits for them, and re-layouts: 31.2 us -> 5.78 us
  between operations: 14.8 us -> 0.68 us
    psum x1 -> x0, waiting for transfers between devices: 256 us -> none  [local(): lax.psum(jnp.concatenate([down_factor_piece, up_factor_piece], axis=1), (...]
    reduce_scatter x1 -> x0, waiting for transfers between devices: 204 us -> none  [local(): lax.psum_scatter(jnp.concatenate([key_part.reshape(lax.axis_size('ctx') *...]
    all_to_all x0 -> x5, blocking collectives: none -> 95.8 us  [exchange(): return lax.all_to_all(x, axes, 0, 0, tiled=True)]
    ppermute x0 -> x6, waiting for transfers between devices: none -> 40.8 us  [shift(): return lax.ppermute(x, 'x', [(i, (i + by) % NX) for i in range(NX)])]
    all_gather x1 -> x0, blocking collectives: 35.8 us -> none  [local(): lax.all_gather(send_doc[None, None], 'ctx', axis=1, tiled=True)]
    dot_general x16 -> x0, matrix products: 32.3 us -> none  [the longest x1 5.11 us: attend(): jnp.einsum('sgmqk,kgd->sqgmd', far_grads, beacon_keys, preferred_element_...]
    pallas_call x0 -> x7, Pallas kernels: none -> 27.5 us  [the longest x1 13.4 us: attend(): pl.pallas_call(attend_kernel, grid=(KVH,), in_specs=[pl.BlockSpec(memory_...]
    unnamed x1 -> x0, blocking collectives: 14 us -> none
  transfers between devices with their start and end apart: 3 -> 6, of which waited for: 3 -> 6; matrix products, arithmetic and copies ran while one was open for 6% -> 0% of each run, Pallas kernels for 0% -> 0%
where the time goes in v1:
time: 177 us; the launch traced here: 176 us
  blocking collectives  95.8 us (54%)
  waiting for transfers between devices  40.8 us (23%)
  Pallas kernels  27.5 us (16%)
  local copies, waits for them, and re-layouts  5.78 us (3%)
  starting transfers between devices  5.06 us (3%)
    all_to_all x5, blocking collectives, exchange(): return lax.all_to_all(x, axes, 0, 0, tiled=True)  95.8 us
    ppermute x6, waiting for transfers between devices, shift(): return lax.ppermute(x, 'x', [(i, (i + by) % NX) for i in range(NX)])  40.8 us
    pallas_call x1, Pallas kernels, attend(): pl.pallas_call(attend_kernel, grid=(KVH,), in_specs=[pl.BlockSpec(memory_...  13.4 us
    unnamed x23, local copies, waits for them, and re-layouts  5.78 us
    ppermute x6, starting transfers between devices, shift(): return lax.ppermute(x, 'x', [(i, (i + by) % NX) for i in range(NX)])  5.06 us
    pallas_call x2, Pallas kernels, add_and_copy(): pl.pallas_call(functools.partial(add_kernel, copies), in_specs=[vmem], ou...  3.79 us
  transfers between devices with their start and end apart: 6, of which 6 were waited for; matrix products, arithmetic and copies ran while one was open for 0% of the time, Pallas kernels for 0%

profile of v1, /device:TPU:1, one launch (start us, length us, event | category | flops | bytes accessed | tf_op | source)
XLA Modules:
  0.0 176.2 jit_solution(8119540942360616463)
XLA Ops:
  0.7 2.4 %copy.17.down = bf16[4096,64]{1,0:T(8,128)(2,1)} copy(bf16[4096,64]{0,1:T(8,128)(2,1)} %param.16) | data formatting | bytes 1048576 | tf_op args[5]
  3.6 2.8 %project.1 = (bf16[8,26,8,128]{3,2,1,0:T(8,128)(2,1)}, bf16[16,64]{1,0:T(8,128)(2,1)}) custom-call(s32[4]{0:T(128)} %pad_add_fusion.1.info, bf16[16,4096]{1,0:T(8,128)(2,1)} %bitcast.28, bf16[4096,64]{1,0:T(8,128)(2,1)} %copy.17.down, bf16[64,2048]{1,0:T(8,128)(2,1)} %up.3, bf16[16,2048]{1,0:T(8,128)(2,1)} %bitcast.30), custom_call_target="tpu_custom_call" | custom-call | tf_op jit(solution)/shard_map/project/pallas_call | solution.py:82
  6.4 22.9 %all_to_all.25.box0 = bf16[8,26,8,128]{3,2,1,0:T(8,128)(2,1)S(1)} all-to-all(bf16[8,26,8,128]{3,2,1,0:T(8,128)(2,1)} %get-tuple-element.18), channel_id=1, replica_groups=mesh['z'=8,'x'=4,'y'=4,'core'=2] {'z'}, dimensions={0} | all-to-all | bytes 851968 | tf_op jit(solution)/shard_map/all_to_all | solution.py:337
  29.3 2.5 %collective-permute-start.2 = (bf16[8,26,8,128]{3,2,1,0:T(8,128)(2,1)S(1)}, bf16[8,26,8,128]{3,2,1,0:T(8,128)(2,1)S(1)}, u32[]{:S(2)}, u32[]{:S(2)}) collective-permute-start(bf16[8,26,8,128]{3,2,1,0:T(8,128)(2,1)S(1)} %all_to_all.25.box0), channel_id=1, source_target_pairs={{0,24},{8,0},{16,8},{24,16},{1,25},{9,1},{17,9},{25,17},{2,26},{10... | collective-permute-start | bytes 1277960 | tf_op jit(solution)/shard_map/ppermute | solution.py:341
  32.9 6.2 %collective-permute-done.2.box3 = bf16[8,26,8,128]{3,2,1,0:T(8,128)(2,1)S(1)} collective-permute-done((bf16[8,26,8,128]{3,2,1,0:T(8,128)(2,1)S(1)}, bf16[8,26,8,128]{3,2,1,0:T(8,128)(2,1)S(1)}, u32[]{:S(2)}, u32[]{:S(2)}) %collective-permute-start.2) | collective-permute-done | bytes 426016 | tf_op jit(solution)/shard_map/ppermute | solution.py:341
  39.1 2.7 %collective-permute-done.1.box2 = bf16[8,26,8,128]{3,2,1,0:T(8,128)(2,1)S(1)} collective-permute-done((bf16[8,26,8,128]{3,2,1,0:T(8,128)(2,1)S(1)}, bf16[8,26,8,128]{3,2,1,0:T(8,128)(2,1)S(1)}, u32[]{:S(2)}, u32[]{:S(2)}) %collective-permute-start.1) | collective-permute-done | bytes 426016 | tf_op jit(solution)/shard_map/ppermute | solution.py:341
  41.9 12.3 %collective-permute-done.box1 = bf16[8,26,8,128]{3,2,1,0:T(8,128)(2,1)} collective-permute-done((bf16[8,26,8,128]{3,2,1,0:T(8,128)(2,1)S(1)}, bf16[8,26,8,128]{3,2,1,0:T(8,128)(2,1)}, u32[]{:S(2)}, u32[]{:S(2)}) %collective-permute-start) | collective-permute-done | bytes 426016 | tf_op jit(solution)/shard_map/ppermute | solution.py:341
  54.2 0.9 copy-done.3
  55.2 0.9 copy-done.4
  56.1 13.4 %attend.1 = (bf16[2,64,4096]{2,1,0:T(8,128)(2,1)}, bf16[2,64,4096]{2,1,0:T(8,128)(2,1)}, bf16[2,64,1024]{2,1,0:T(8,128)(2,1)}, bf16[2,64,1024]{2,1,0:T(8,128)(2,...) custom-call(s32[6]{0:T(128)S(1)} %pad_add_fusion.info, ...), custom_call_target="tpu_custom_call" | custom-call | tf_op jit(solution)/shard_map/attend/pallas_call | solution.py:229
  69.5 0.7 copy-done.2
  70.8 0.9 collective-permute-start.5
  71.7 8.7 %collective-permute-done.3.b = bf16[8,24,8,128]{3,2,1,0:T(8,128)(2,1)S(1)} collective-permute-done((bf16[8,24,8,128]{3,2,1,0:T(8,128)(2,1)S(1)}, bf16[8,24,8,128]{3,2,1,0:T(8,128)(2,1)S(1)}, u32[]{:S(2)}, u32[]{:S(2)}) %collective-permute-start.3) | collective-permute-done | bytes 393248 | tf_op jit(solution)/shard_map/ppermute | solution.py:341
  80.4 0.9 collective-permute-done.4.c
  81.3 9.9 %collective-permute-done.5.d = bf16[8,24,8,128]{3,2,1,0:T(8,128)(2,1)S(1)} collective-permute-done((bf16[8,24,8,128]{3,2,1,0:T(8,128)(2,1)S(1)}, bf16[8,24,8,128]{3,2,1,0:T(8,128)(2,1)S(1)}, u32[]{:S(2)}, u32[]{:S(2)}) %collective-permute-start.5) | collective-permute-done | bytes 393248 | tf_op jit(solution)/shard_map/ppermute | solution.py:341
  91.9 2.3 %add_four.1 = bf16[8,24,8,128]{3,2,1,0:T(8,128)(2,1)} custom-call(bf16[8,24,8,128]{3,2,1,0:T(8,128)(2,1)} %bitcast.22, bf16[8,24,8,128]{3,2,1,0:T(8,128)(2,1)} %copy-done.5, bf16[8,24,8,128]{3,2,1,0:T(8,128)(2,1)} %copy-done.6, bf16[8,24,8,128]{3,2,1,0:T(8,128)(2,1)} %copy-done.7), custom_call_target="tpu_custom_call" | custom-call | tf_op jit(solution)/shard_map/add_four/pallas_call | solution.py:309
  94.2 18.4 %all_to_all.26.parts = bf16[8,24,8,128]{3,2,1,0:T(8,128)(2,1)} all-to-all(bf16[8,24,8,128]{3,2,1,0:T(8,128)(2,1)} %add_four.1), channel_id=1, replica_groups=mesh['z'=8,'x'=4,'y'=4,'core'=2] {'z'}, dimensions={0} | all-to-all | bytes 786432 | tf_op jit(solution)/shard_map/all_to_all | solution.py:337
  112.6 2.9 %finish.1 = (bf16[16,2048]{1,0:T(8,128)(2,1)}, bf16[32,12,8,128]{3,2,1,0:T(8,128)(2,1)}) custom-call(s32[4]{0:T(128)} %pad_add_fusion.1.info, bf16[8,24,8,128]{3,2,1,0:T(8,128)(2,1)} %all_to_all.26.parts, bf16[64,2048]{1,0:T(8,128)(2,1)} %up.3, bf16[16,4096]{1,0:T(8,128)(2,1)} %bitcast.29, bf16[16,64]{1,0:T(8,128)(2,1)} %get-tuple-element.27.low), custom_call_target="tpu_custom_call" | custom-call | tf_op jit(solution)/shard_map/finish/pallas_call | solution.py:272
  115.5 20.5 %all_to_all.27.parts = bf16[32,12,8,128]{3,2,1,0:T(8,128)(2,1)} all-to-all(bf16[32,12,8,128]{3,2,1,0:T(8,128)(2,1)} %get-tuple-element.29), channel_id=1, replica_groups=mesh['z'=8,'x'=4,'y'=4,'core'=2] {'x','y','core'}, dimensions={0} | all-to-all | bytes 1572864 | tf_op jit(solution)/shard_map/all_to_all | solution.py:337
  136.0 1.9 %add_wide.1 = bf16[8,12,8,128]{3,2,1,0:T(8,128)(2,1)} custom-call(bf16[32,12,8,128]{3,2,1,0:T(8,128)(2,1)} %all_to_all.27.parts), custom_call_target="tpu_custom_call" | custom-call | tf_op jit(solution)/shard_map/add_wide/pallas_call | solution.py:292
  137.9 15.0 %all_to_all.28.parts = bf16[8,12,8,128]{3,2,1,0:T(8,128)(2,1)} all-to-all(bf16[8,12,8,128]{3,2,1,0:T(8,128)(2,1)} %add_wide.1), channel_id=1, replica_groups=mesh['z'=8,'x'=4,'y'=4,'core'=2] {'z'}, dimensions={0} | all-to-all | bytes 393216 | tf_op jit(solution)/shard_map/all_to_all | solution.py:337
  152.9 1.9 %add_z.1 = bf16[32,12,8,128]{3,2,1,0:T(8,128)(2,1)} custom-call(bf16[8,12,8,128]{3,2,1,0:T(8,128)(2,1)} %all_to_all.28.parts), custom_call_target="tpu_custom_call" | custom-call | tf_op jit(solution)/shard_map/add_z/pallas_call | solution.py:292
  154.8 19.0 %all_to_all.29.tiles = bf16[32,12,8,128]{3,2,1,0:T(8,128)(2,1)} all-to-all(bf16[32,12,8,128]{3,2,1,0:T(8,128)(2,1)} %add_z.1), channel_id=1, replica_groups=mesh['z'=8,'x'=4,'y'=4,'core'=2] {'x','y','core'}, dimensions={0} | all-to-all | bytes 1572864 | tf_op jit(solution)/shard_map/all_to_all | solution.py:337
  173.8 2.4 %unpack.1 = f32[64,6144]{1,0:T(8,128)} custom-call(bf16[32,12,8,128]{3,2,1,0:T(8,128)(2,1)} %all_to_all.29.tiles), custom_call_target="tpu_custom_call" | custom-call | tf_op jit(solution)/shard_map/unpack/pallas_call | solution.py:327
  (25 shorter events, 3.1 us)
Async XLA Ops:
  0.6 2.4 %copy-start.9 = (s32[1,1,2]{2,1,0:T(1,128)S(1)}, s32[1,1,2]{2,1,0:T(1,128)}, u32[]{:S(2)}) copy-start(s32[1,1,2]{2,1,0:T(1,128)} %param.20) | copy-start | bytes 28
  0.6 2.4 %copy-start.10 = (s32[1,1,2]{2,1,0:T(1,128)S(1)}, s32[1,1,2]{2,1,0:T(1,128)}, u32[]{:S(2)}) copy-start(s32[1,1,2]{2,1,0:T(1,128)} %param.19) | copy-start | bytes 28
  3.0 29.8 %copy-start.8 = (s32[1,1,2]{2,1,0:T(1,128)S(1)}, s32[1,1,2]{2,1,0:T(1,128)}, u32[]{:S(2)}) copy-start(s32[1,1,2]{2,1,0:T(1,128)} %param.21) | copy-start | bytes 28
  3.0 51.2 %copy-start = (bf16[1,1,2,64,4096]{4,3,2,1,0:T(8,128)(2,1)S(1)}, bf16[1,1,2,64,4096]{4,3,2,1,0:T(8,128)(2,1)}, u32[]{:S(2)}) copy-start(bf16[1,1,2,64,4096]{4,3,2,1,0:T(8,128)(2,1)} %param.11) | copy-start | bytes 3145732
  3.0 51.2 %copy-start.1 = (bf16[1,1,2,64,4096]{4,3,2,1,0:T(8,128)(2,1)S(1)}, bf16[1,1,2,64,4096]{4,3,2,1,0:T(8,128)(2,1)}, u32[]{:S(2)}) copy-start(bf16[1,1,2,64,4096]{4,3,2,1,0:T(8,128)(2,1)} %param.18) | copy-start | bytes 3145732
  29.3 9.9 %collective-permute-start.2 = (bf16[8,26,8,128]{3,2,1,0:T(8,128)(2,1)S(1)}, bf16[8,26,8,128]{3,2,1,0:T(8,128)(2,1)S(1)}, u32[]{:S(2)}, u32[]{:S(2)}) collective-permute-start(bf16[8,26,8,128]{3,2,1,0:T(8,128)(2,1)S(1)} %all_to_all.25.box0), channel_id=1, source_target_pairs={{0,24},{8,0},{16,8},{24,16},{1,25},{9,1},{17,9},{25,17},{2,26},{10... | collective-permute-start | bytes 1277960 | tf_op jit(solution)/shard_map/ppermute | solution.py:341
  31.7 10.1 %collective-permute-start.1 = (bf16[8,26,8,128]{3,2,1,0:T(8,128)(2,1)S(1)}, bf16[8,26,8,128]{3,2,1,0:T(8,128)(2,1)S(1)}, u32[]{:S(2)}, u32[]{:S(2)}) collective-permute-start(bf16[8,26,8,128]{3,2,1,0:T(8,128)(2,1)S(1)} %all_to_all.25.box0), channel_id=1, source_target_pairs={{0,16},{8,24},{16,0},{24,8},{1,17},{9,25},{17,1},{25,9},{2,18},{10... | collective-permute-start | bytes 1277960 | tf_op jit(solution)/shard_map/ppermute | solution.py:341
  32.2 22.0 %collective-permute-start = (bf16[8,26,8,128]{3,2,1,0:T(8,128)(2,1)S(1)}, bf16[8,26,8,128]{3,2,1,0:T(8,128)(2,1)}, u32[]{:S(2)}, u32[]{:S(2)}) collective-permute-start(bf16[8,26,8,128]{3,2,1,0:T(8,128)(2,1)S(1)} %all_to_all.25.box0), channel_id=1, source_target_pairs={{0,8},{8,16},{16,24},{24,0},{1,9},{9,17},{17,25},{25,1},{2,10},{10... | collective-permute-start | bytes 1277960 | tf_op jit(solution)/shard_map/ppermute | solution.py:341
  54.2 1.0 copy-start.3
  55.2 0.9 copy-start.4
  69.5 0.7 copy-start.2
  70.2 10.2 %collective-permute-start.3 = (bf16[8,24,8,128]{3,2,1,0:T(8,128)(2,1)S(1)}, bf16[8,24,8,128]{3,2,1,0:T(8,128)(2,1)S(1)}, u32[]{:S(2)}, u32[]{:S(2)}) collective-permute-start(bf16[8,24,8,128]{3,2,1,0:T(8,128)(2,1)S(1)} %bitcast.27), channel_id=1, source_target_pairs={{0,24},{8,0},{16,8},{24,16},{1,25},{9,1},{17,9},{25,17},{2,26},{10... | collective-permute-start | bytes 1179656 | tf_op jit(solution)/shard_map/ppermute | solution.py:341
  70.2 11.0 %collective-permute-start.4 = (bf16[8,24,8,128]{3,2,1,0:T(8,128)(2,1)S(1)}, bf16[8,24,8,128]{3,2,1,0:T(8,128)(2,1)S(1)}, u32[]{:S(2)}, u32[]{:S(2)}) collective-permute-start(bf16[8,24,8,128]{3,2,1,0:T(8,128)(2,1)S(1)} %bitcast.26), channel_id=1, source_target_pairs={{0,16},{8,24},{16,0},{24,8},{1,17},{9,25},{17,1},{25,9},{2,18},{10... | collective-permute-start | bytes 1179656 | tf_op jit(solution)/shard_map/ppermute | solution.py:341
  70.8 20.4 %collective-permute-start.5 = (bf16[8,24,8,128]{3,2,1,0:T(8,128)(2,1)S(1)}, bf16[8,24,8,128]{3,2,1,0:T(8,128)(2,1)S(1)}, u32[]{:S(2)}, u32[]{:S(2)}) collective-permute-start(bf16[8,24,8,128]{3,2,1,0:T(8,128)(2,1)S(1)} %bitcast.25), channel_id=1, source_target_pairs={{0,8},{8,16},{16,24},{24,0},{1,9},{9,17},{17,25},{25,1},{2,10},{10... | collective-permute-start | bytes 1179656 | tf_op jit(solution)/shard_map/ppermute | solution.py:341
  80.4 10.8 %copy-start.5 = (bf16[8,24,8,128]{3,2,1,0:T(8,128)(2,1)}, bf16[8,24,8,128]{3,2,1,0:T(8,128)(2,1)S(1)}, u32[]{:S(2)}) copy-start(bf16[8,24,8,128]{3,2,1,0:T(8,128)(2,1)S(1)} %collective-permute-done.3.b) | copy-start | bytes 1179652
  81.3 9.9 %copy-start.6 = (bf16[8,24,8,128]{3,2,1,0:T(8,128)(2,1)}, bf16[8,24,8,128]{3,2,1,0:T(8,128)(2,1)S(1)}, u32[]{:S(2)}) copy-start(bf16[8,24,8,128]{3,2,1,0:T(8,128)(2,1)S(1)} %collective-permute-done.4.c) | copy-start | bytes 1179652
  91.2 0.7 copy-start.7

commit v2 on v1

--- a/solution.py
+++ b/solution.py
@@ -1,5 +1,3 @@
-import functools
-
 import jax
 import jax.numpy as jnp
 from jax import lax
@@ -46,10 +44,9 @@
     return jnp.where((slot == source) & (row < first + second), 1.0, 0.0)
 
 
-def project_kernel(info, state, down, up, frozen, out, low_out):
-    first, second = info[0], info[1]
-    low = dot(state[...], down[...]).astype(bf16)
-    low_out[...] = low
+def project_kernel(counts, docs, state, down_t, up, frozen, out):
+    first, second = counts[0, 0, 0], counts[0, 0, 1]
+    low = dot(state[...], down_t[...], ((1,), (1,))).astype(bf16)
     states = (frozen[...].astype(f32) + dot(low, up[...])).astype(bf16)
     pick = selection(first, second).astype(bf16)
     rows = dot(pick, states)
@@ -68,8 +65,8 @@
     right = jnp.where(put_row + UPDATE_RANK == put_col, 1.0, 0.0).astype(bf16)
     tiles.append((dot(low_rows, left)[:8] + dot(low_rows, right)[8:]))
     facts = jnp.zeros((8, HD), f32)
-    for i in range(4):
-        facts = jnp.where(sub == i, info[i].astype(f32), facts)
+    for i, fact in enumerate((first, second, docs[0, 0, 0], docs[0, 0, 1])):
+        facts = jnp.where(sub == i, fact.astype(f32), facts)
     tiles.append(facts)
     for t, tile in enumerate(tiles):
         packed = tile.astype(bf16)
@@ -77,34 +74,34 @@
             out[z, t] = packed
 
 
-def project(info, state, down, up, frozen):
-    vmem = pl.BlockSpec(memory_space=pltpu.VMEM)
+VMEM = pl.BlockSpec(memory_space=pltpu.VMEM)
+SMEM = pl.BlockSpec(memory_space=pltpu.SMEM)
+
+
+def project(counts, docs, state, down_t, up, frozen):
     return pl.pallas_call(
         project_kernel,
-        in_specs=[pl.BlockSpec(memory_space=pltpu.SMEM)] + [vmem] * 4,
-        out_specs=[vmem, vmem],
-        out_shape=[
-            jax.ShapeDtypeStruct((NZ, TILES, 8, HD), bf16),
-            jax.ShapeDtypeStruct((16, UPDATE_RANK), bf16),
-        ],
+        in_specs=[SMEM] * 2 + [VMEM] * 4,
+        out_specs=VMEM,
+        out_shape=jax.ShapeDtypeStruct((NZ, TILES, 8, HD), bf16),
         name="project",
-    )(info, state, down, up, frozen)
-
-
-def fill_bias(info, boxes, bias):
-    z_own, x_own = info[0], info[1]
+    )(counts, docs, state, down_t, up, frozen)
+
+
+def fill_bias(place, docs, ends, boxes, bias):
+    z_own, x_own = place[0], place[1]
     pair = z_own * NX + x_own
     lane = lax.broadcasted_iota(jnp.int32, (8, NEAR), 1)
     sub = lax.broadcasted_iota(jnp.int32, (8, NEAR), 0)
     side = lane // SPAN
     offset = lane % SPAN
     own_span = jnp.where(side == 0, pair, NCH - 1 - pair).astype(f32)
-    own_doc = jnp.where(side == 0, info[2], info[3]).astype(f32)
-    live = offset < jnp.where(side == 0, info[4], info[5])
+    own_doc = jnp.where(side == 0, docs[0, 0, 0], docs[0, 0, 1]).astype(f32)
+    live = offset < jnp.where(side == 0, ends[0, 0, 0], ends[0, 0, 1])
     for block in range(NEAR // 8):
         key_side = block * 8 // SPAN
         key_offset = sub + (block * 8) % SPAN
-        key_live = key_offset < info[4 + key_side]
+        key_live = key_offset < ends[0, 0, key_side]
         seen = (side == key_side) & (key_offset <= offset) & (key_live == live)
         bias[block * 8 : block * 8 + 8, :] = jnp.where(seen, 0.0, MASKED)
 
@@ -137,9 +134,24 @@
             )
 
 
+def gather_low(boxes, low_all):
+    lane = lax.broadcasted_iota(jnp.int32, (NZ, 8, HD), 2)
+    sub = lax.broadcasted_iota(jnp.int32, (NZ // 2, 8, HD), 1)
+    for b, box in enumerate(boxes):
+        tile = box[:, 24].astype(f32)
+        head = jnp.where(lane < UPDATE_RANK, tile, 0.0)
+        low_all[b * 64 : b * 64 + 64, :] = head.reshape(64, HD).astype(bf16)
+        tail = jnp.where(lane < UPDATE_RANK, pltpu.roll(tile, UPDATE_RANK, 2), 0.0)
+        tail = tail.reshape(NZ // 2, 2, 8, HD)
+        tail = jnp.where(sub < 4, tail[:, 0], pltpu.roll(tail[:, 1], 4, 1))
+        at = 256 + b * 32
+        low_all[at : at + 32, :] = tail.reshape(32, HD).astype(bf16)
+
+
 def attend_kernel(
-    info, query, key, value, grad, box0, box1, box2, box3,
-    attended, grad_query, grad_key, grad_value, out0, out1, out2, out3, bias,
+    place, docs, ends, query, key, value, grad, up_key, up_value, box0, box1, box2, box3,
+    attended, grad_query, grad_key, grad_value, out0, out1, out2, out3, up_key_part,
+    up_value_part, low_part, bias, low_all, low_total,
 ):
     boxes = (box0, box1, box2, box3)
     outs = (out0, out1, out2, out3)
@@ -147,7 +159,9 @@
 
     @pl.when(g == 0)
     def _():
-        fill_bias(info, boxes, bias)
+        fill_bias(place, docs, ends, boxes, bias)
+        gather_low(boxes, low_all)
+        low_total[...] = jnp.zeros_like(low_total)
 
     sub = lax.broadcasted_iota(jnp.int32, (NZ // 2, 8, HD), 1)
 
@@ -217,30 +231,124 @@
             out[2 * i, 2, 0] = even[i]
             out[2 * i + 1, 2, 0] = odd[i]
 
-
-def attend(info, query, key, value, grad, boxes):
+    far_keys = key_grad[NEAR:].astype(bf16)
+    far_values = value_grad[NEAR:].astype(bf16)
+    up_key_part[...] = dot(low_all[...], far_keys, ((0,), (0,)))[:UPDATE_RANK]
+    up_value_part[...] = dot(low_all[...], far_values, ((0,), (0,)))[:UPDATE_RANK]
+
+    def twice(ref):
+        return jnp.concatenate([ref[...], ref[...]], axis=0)
+
+    low_total[...] += dot(far_keys, twice(up_key), ((1,), (1,)))
+    low_total[...] += dot(far_values, twice(up_value), ((1,), (1,)))
+
+    @pl.when(g == KVH - 1)
+    def _():
+        lane = lax.broadcasted_iota(jnp.int32, (8, HD), 1)
+        for b in range(NX):
+            x = lax.rem(place[1] - b + NX, NX)
+            for z in range(NZ):
+                at = b * 64 + z * 8
+                head = low_total[at : at + 8, :]
+                at = 256 + b * 32 + z // 2 * 8
+                tail = low_total[at : at + 8, :]
+                if z % 2:
+                    tail = pltpu.roll(tail, 4, 0)
+                low_part[z, x] = jnp.where(lane < UPDATE_RANK, head, tail).astype(bf16)
+
+
+def attend(place, docs, ends, query, key, value, grad, up, boxes):
     wide = pl.BlockSpec((2, SPAN, GROUP * HD), lambda g: (0, 0, g))
     narrow = pl.BlockSpec((2, SPAN, HD), lambda g: (0, 0, g))
     whole = pl.BlockSpec((NZ, TILES, 8, HD), lambda g: (0, 0, 0, 0))
     part = pl.BlockSpec((NZ, 3, 1, 8, HD), lambda g: (0, 0, g, 0, 0))
+    up_key = pl.BlockSpec((UPDATE_RANK, HD), lambda g: (0, g))
+    up_value = pl.BlockSpec((UPDATE_RANK, HD), lambda g: (0, KVH + g))
+    low_part = pl.BlockSpec((NZ, NX, 8, HD), lambda g: (0, 0, 0, 0))
     wide_shape = jax.ShapeDtypeStruct((2, SPAN, QW), bf16)
     narrow_shape = jax.ShapeDtypeStruct((2, SPAN, KEY_FEATURES), bf16)
     part_shape = jax.ShapeDtypeStruct((NZ, 3, KVH, 8, HD), bf16)
+    up_shape = jax.ShapeDtypeStruct((UPDATE_RANK, KEY_FEATURES), f32)
     return pl.pallas_call(
         attend_kernel,
         grid=(KVH,),
-        in_specs=[pl.BlockSpec(memory_space=pltpu.SMEM), wide, narrow, narrow, wide] + [whole] * NX,
-        out_specs=[wide, wide, narrow, narrow] + [part] * NX,
-        out_shape=[wide_shape, wide_shape, narrow_shape, narrow_shape] + [part_shape] * NX,
-        scratch_shapes=[pltpu.VMEM((KEYS, NEAR), f32)],
+        in_specs=[SMEM] * 3 + [wide, narrow, narrow, wide, up_key, up_value] + [whole] * NX,
+        out_specs=[wide, wide, narrow, narrow] + [part] * NX + [up_key, up_key, low_part],
+        out_shape=[wide_shape, wide_shape, narrow_shape, narrow_shape]
+        + [part_shape] * NX
+        + [up_shape, up_shape, jax.ShapeDtypeStruct((NZ, NX, 8, HD), bf16)],
+        scratch_shapes=[
+            pltpu.VMEM((KEYS, NEAR), f32),
+            pltpu.VMEM((FAR, HD), bf16),
+            pltpu.VMEM((FAR, HD), f32),
+        ],
         compiler_params=pltpu.CompilerParams(vmem_limit_bytes=48 * 1024 * 1024),
         name="attend",
-    )(info, query, key, value, grad, *boxes)
-
-
-def finish_kernel(info, parts, up, state, low, cache_out, pieces):
-    pick = selection(info[0], info[1]).astype(bf16)
+    )(place, docs, ends, query, key, value, grad, up, up, *boxes)
+
+
+PER_ROW = (MODEL_WIDTH + 2 * KEY_FEATURES) // HD
+CHUNK = 12
+CHUNKS = 8 * PER_ROW // CHUNK
+
+
+def factor_kernel(counts, low_parts, state, up_key, up_value, pieces):
+    pick = selection(counts[0, 0, 0], counts[0, 0, 1])
+    total = jnp.sum(low_parts[...].astype(f32), axis=0)
+    compact = jnp.concatenate([total, pltpu.roll(total, UPDATE_RANK, 1)], axis=0).astype(bf16)
+    low_grad = dot(pick.astype(bf16), compact, ((0,), (0,))).astype(bf16)
+    down_piece = dot(low_grad, state[...], ((0,), (0,)))
+    wide = MODEL_WIDTH // HD
+    for t in range(8 * PER_ROW):
+        r, c = divmod(t, PER_ROW)
+        rows = slice(r * 8, r * 8 + 8)
+        if c < wide:
+            tile = down_piece[rows, c * HD : (c + 1) * HD]
+        elif c < wide + KVH:
+            c -= wide
+            tile = up_key[rows, c * HD : (c + 1) * HD]
+        else:
+            c -= wide + KVH
+            tile = up_value[rows, c * HD : (c + 1) * HD]
+        pieces[t // CHUNK, t % CHUNK] = tile.astype(bf16)
+
+
+def factor(counts, low_parts, state, up_key, up_value):
+    return pl.pallas_call(
+        factor_kernel,
+        in_specs=[SMEM] + [VMEM] * 4,
+        out_specs=VMEM,
+        out_shape=jax.ShapeDtypeStruct((CHUNKS, CHUNK, 8, HD), bf16),
+        name="factor",
+    )(counts, low_parts, state, up_key, up_value)
+
+
+def middle_kernel(pieces, a, b, c, d, out):
+    chunk = jnp.sum(pieces[...].astype(f32), axis=0).astype(bf16)
+    for z in range(NZ):
+        out[z, :CHUNK] = chunk
+        out[z, CHUNK:] = (
+            (a[z].astype(f32) + b[z].astype(f32)) + (c[z].astype(f32) + d[z].astype(f32))
+        ).astype(bf16)
+
+
+def middle(pieces, parts):
+    return pl.pallas_call(
+        middle_kernel,
+        in_specs=[VMEM] * 5,
+        out_specs=VMEM,
+        out_shape=jax.ShapeDtypeStruct((NZ, CHUNK + GRAD_TILES, 8, HD), bf16),
+        name="middle",
+    )(pieces, *parts)
+
+
+def close_kernel(counts, parts, cache_out, out):
+    pick = selection(counts[0, 0, 0], counts[0, 0, 1]).astype(bf16)
     total = jnp.sum(parts[...].astype(f32), axis=0)
+    chunk = total[:CHUNK].astype(bf16)
+    for i in range(CHUNKS):
+        out[i] = chunk
+    total = total[CHUNK:]
     sub = lax.broadcasted_iota(jnp.int32, (8, HD), 0)
     tops = [total[h] for h in range(2 * KVH)]
     rest_keys, rest_values = [], []
@@ -251,83 +359,33 @@
     compact = jnp.concatenate(
         [jnp.concatenate(tops, axis=1), jnp.concatenate(rest_keys + rest_values, axis=1)], axis=0
     ).astype(bf16)
-    cache = dot(pick, compact, ((0,), (0,))).astype(bf16)
-    cache_out[...] = cache
-    low_grad = dot(cache, up[...], ((1,), (1,))).astype(bf16)
-    down_piece = dot(low_grad, state[...], ((0,), (0,)))
-    up_piece = dot(low[...], cache, ((0,), (0,)))
-    per_row = (MODEL_WIDTH + 2 * KEY_FEATURES) // HD
-    for t in range(8 * per_row):
-        r, c = divmod(t, per_row)
-        if c < MODEL_WIDTH // HD:
-            tile = down_piece[r * 8 : r * 8 + 8, c * HD : (c + 1) * HD]
-        else:
-            c -= MODEL_WIDTH // HD
-            tile = up_piece[r * 8 : r * 8 + 8, c * HD : (c + 1) * HD]
-        pieces[t // 12, t % 12] = tile.astype(bf16)
-
-
-def finish(info, parts, up, state, low):
-    vmem = pl.BlockSpec(memory_space=pltpu.VMEM)
-    return pl.pallas_call(
-        finish_kernel,
-        in_specs=[pl.BlockSpec(memory_space=pltpu.SMEM)] + [vmem] * 4,
-        out_specs=[vmem, vmem],
+    cache_out[...] = dot(pick, compact, ((0,), (0,))).astype(bf16)
+
+
+def close(counts, parts):
+    return pl.pallas_call(
+        close_kernel,
+        in_specs=[SMEM, VMEM],
+        out_specs=[VMEM, VMEM],
         out_shape=[
             jax.ShapeDtypeStruct((16, 2 * KEY_FEATURES), bf16),
-            jax.ShapeDtypeStruct((32, 12, 8, HD), bf16),
+            jax.ShapeDtypeStruct((CHUNKS, CHUNK, 8, HD), bf16),
         ],
-        name="finish",
-    )(info, parts, up, state, low)
-
-
-def add_kernel(copies, parts, out):
-    total = jnp.sum(parts[...].astype(f32), axis=0).astype(bf16)
-    for i in range(copies):
-        out[i] = total
-
-
-def add_and_copy(parts, copies, name):
-    vmem = pl.BlockSpec(memory_space=pltpu.VMEM)
-    return pl.pallas_call(
-        functools.partial(add_kernel, copies),
-        in_specs=[vmem],
-        out_specs=vmem,
-        out_shape=jax.ShapeDtypeStruct((copies,) + parts.shape[1:], bf16),
-        name=name,
-    )(parts)
-
-
-def add_four_kernel(a, b, c, d, out):
-    out[...] = (
-        (a[...].astype(f32) + b[...].astype(f32)) + (c[...].astype(f32) + d[...].astype(f32))
-    ).astype(bf16)
-
-
-def add_four(parts):
-    vmem = pl.BlockSpec(memory_space=pltpu.VMEM)
-    return pl.pallas_call(
-        add_four_kernel,
-        in_specs=[vmem] * 4,
-        out_specs=vmem,
-        out_shape=jax.ShapeDtypeStruct(parts[0].shape, bf16),
-        name="add_four",
-    )(*parts)
+        name="close",
+    )(counts, parts)
 
 
 def unpack_kernel(tiles, out):
-    per_row = (MODEL_WIDTH + 2 * KEY_FEATURES) // HD
-    for t in range(8 * per_row):
-        r, c = divmod(t, per_row)
-        out[r * 8 : r * 8 + 8, c * HD : (c + 1) * HD] = tiles[t // 12, t % 12].astype(f32)
+    for t in range(8 * PER_ROW):
+        r, c = divmod(t, PER_ROW)
+        out[r * 8 : r * 8 + 8, c * HD : (c + 1) * HD] = tiles[t // CHUNK, t % CHUNK].astype(f32)
 
 
 def unpack(tiles):
-    vmem = pl.BlockSpec(memory_space=pltpu.VMEM)
     return pl.pallas_call(
         unpack_kernel,
-        in_specs=[vmem],
-        out_specs=vmem,
+        in_specs=[VMEM],
+        out_specs=VMEM,
         out_shape=jax.ShapeDtypeStruct((UPDATE_RANK, MODEL_WIDTH + 2 * KEY_FEATURES), f32),
         name="unpack",
     )(tiles)
@@ -345,30 +403,27 @@
     query, key, value, beacon_slot_state, frozen_beacon_cache, adapter_down_weight,
     adapter_up_weight, output_cotangent, span_beacon_count, span_document, boundary,
 ):
-    counts = span_beacon_count[0, 0]
-    docs = span_document[0, 0]
-    ends = boundary[0, 0]
-    z_own = lax.axis_index("z").astype(jnp.int32)
-    x_own = lax.axis_index("x").astype(jnp.int32)
+    place = jnp.stack([lax.axis_index("z"), lax.axis_index("x")]).astype(jnp.int32)
     state = beacon_slot_state[0, 0].reshape(2 * MAX_BEACONS, MODEL_WIDTH)
     frozen = frozen_beacon_cache[0, 0].reshape(2 * MAX_BEACONS, 2 * KEY_FEATURES)
-    pair_info = jnp.concatenate([counts, docs])
-    place_info = jnp.concatenate([jnp.stack([z_own, x_own]), docs, ends])
-
-    message, low = project(pair_info, state, adapter_down_weight, adapter_up_weight, frozen)
+
+    message = project(
+        span_beacon_count, span_document, state, adapter_down_weight.T, adapter_up_weight, frozen
+    )
     column = exchange(message, "z")
     boxes = [column, shift(column, 1), shift(column, 2), shift(column, 3)]
-    attended, grad_query, grad_key, grad_value, *parts = attend(
-        place_info, query[0, 0], key[0, 0], value[0, 0], output_cotangent[0, 0], boxes
-    )
-    parts = [p.reshape(NZ, GRAD_TILES, 8, HD) for p in parts]
-    mine = add_four([parts[0], shift(parts[1], -1), shift(parts[2], -2), shift(parts[3], -3)])
-    cache_gradient, pieces = finish(
-        pair_info, exchange(mine, "z"), adapter_up_weight, state, low
-    )
-    wide = add_and_copy(exchange(pieces, WIDE), NZ, "add_wide")
-    full = add_and_copy(exchange(wide, "z"), 32, "add_z")
-    adapter_gradient = unpack(exchange(full, WIDE))
+    attended, grad_query, grad_key, grad_value, *rest = attend(
+        place, span_document, boundary, query[0, 0], key[0, 0], value[0, 0],
+        output_cotangent[0, 0], adapter_up_weight, boxes,
+    )
+    parts = [p.reshape(NZ, GRAD_TILES, 8, HD) for p in rest[:NX]]
+    up_key, up_value, low_part = rest[NX:]
+    parts = [parts[0], shift(parts[1], -1), shift(parts[2], -2), shift(parts[3], -3)]
+    low_parts = exchange(low_part.reshape(NZ * NX, 8, HD), ("z", "x"))
+    pieces = factor(span_beacon_count, low_parts, state, up_key, up_value)
+    both = exchange(middle(exchange(pieces, WIDE), parts), "z")
+    cache_gradient, chunk = close(span_beacon_count, both)
+    adapter_gradient = unpack(exchange(chunk, WIDE))
     return (
         attended[None, None],
         grad_query[None, None],

time: 177 us -> 176 us (level)
  blocking collectives: 95.8 us -> 79.1 us
  starting transfers between devices: 5.06 us -> 14.7 us
  waiting for transfers between devices: 40.8 us -> 46.1 us
    all_to_all x5 -> x4, blocking collectives: 95.8 us -> 79.1 us  [exchange(): return lax.all_to_all(x, axes, 0, 0, tiled=True)]
    all_to_all x0 -> x1, starting transfers between devices: none -> 7.24 us  [exchange(): return lax.all_to_all(x, axes, 0, 0, tiled=True)]
    ppermute x6, waiting for transfers between devices: 40.8 us -> 46.1 us  [shift(): return lax.ppermute(x, 'x', [(i, (i + by) % NX) for i in range(NX)])]
    ppermute x6, starting transfers between devices: 5.06 us -> 7.44 us  [shift(): return lax.ppermute(x, 'x', [(i, (i + by) % NX) for i in range(NX)])]
    pallas_call x7 -> x6, Pallas kernels: 27.5 us -> 28.8 us  [the longest x1 16 us: attend(): pl.pallas_call(attend_kernel, grid=(KVH,), in_specs=[SMEM] * 3 + [wide, n...]
    unnamed x23 -> x38, local copies, waits for them, and re-layouts: 5.78 us -> 5.45 us
  transfers between devices with their start and end apart: 6 -> 7, of which waited for: 6 -> 6; matrix products, arithmetic and copies ran while one was open for 0% -> 0% of each run, Pallas kernels for 0% -> 0%
where the time goes in v2:
time: 176 us; the launch traced here: 175 us
  blocking collectives  79.1 us (45%)
  waiting for transfers between devices  46.1 us (26%)
  Pallas kernels  28.8 us (16%)
  starting transfers between devices  14.7 us (8%)
  local copies, waits for them, and re-layouts  5.45 us (3%)
    all_to_all x4, blocking collectives, exchange(): return lax.all_to_all(x, axes, 0, 0, tiled=True)  79.1 us
    ppermute x6, waiting for transfers between devices, shift(): return lax.ppermute(x, 'x', [(i, (i + by) % NX) for i in range(NX)])  46.1 us
    pallas_call x1, Pallas kernels, attend(): pl.pallas_call(attend_kernel, grid=(KVH,), in_specs=[SMEM] * 3 + [wide, n...  16 us
    ppermute x6, starting transfers between devices, shift(): return lax.ppermute(x, 'x', [(i, (i + by) % NX) for i in range(NX)])  7.44 us
    all_to_all x1, starting transfers between devices, exchange(): return lax.all_to_all(x, axes, 0, 0, tiled=True)  7.24 us
    unnamed x38, local copies, waits for them, and re-layouts  5.45 us
  transfers between devices with their start and end apart: 7, of which 6 were waited for; matrix products, arithmetic and copies ran while one was open for 0% of the time, Pallas kernels for 0%

profile of v2, /device:TPU:1, one launch (start us, length us, event | category | flops | bytes accessed | tf_op | source)
XLA Modules:
  0.0 174.9 jit_solution(7179515084870784760)
XLA Ops:
  0.7 2.8 %project.1 = bf16[8,26,8,128]{3,2,1,0:T(8,128)(2,1)} custom-call(s32[1,1,2]{2,1,0:T(1,128)} %counts.5, s32[1,1,2]{2,1,0:T(1,128)} %docs.3, bf16[16,4096]{1,0:T(8,128)(2,1)} %bitcast.29, bf16[64,4096]{1,0:T(8,128)(2,1)} %bitcast.28, bf16[64,2048]{1,0:T(8,128)(2,1)} %up_value.1, bf16[16,2048]{1,0:T(8,128)(2,1)} %bitcast.31), custom_call_target="tpu_custom_call" | custom-call | tf_op jit(solution)/shard_map/project/pallas_call | solution.py:82
  3.5 22.9 %all_to_all.25.box0 = bf16[8,26,8,128]{3,2,1,0:T(8,128)(2,1)S(1)} all-to-all(bf16[8,26,8,128]{3,2,1,0:T(8,128)(2,1)} %project.1), channel_id=1, replica_groups=mesh['z'=8,'x'=4,'y'=4,'core'=2] {'z'}, dimensions={0} | all-to-all | bytes 851968 | tf_op jit(solution)/shard_map/all_to_all | solution.py:395
  26.3 2.5 %collective-permute-start.2 = (bf16[8,26,8,128]{3,2,1,0:T(8,128)(2,1)S(1)}, bf16[8,26,8,128]{3,2,1,0:T(8,128)(2,1)S(1)}, u32[]{:S(2)}, u32[]{:S(2)}) collective-permute-start(bf16[8,26,8,128]{3,2,1,0:T(8,128)(2,1)S(1)} %all_to_all.25.box0), channel_id=1, source_target_pairs={{0,24},{8,0},{16,8},{24,16},{1,25},{9,1},{17,9},{25,17},{2,26},{10... | collective-permute-start | bytes 1277960 | tf_op jit(solution)/shard_map/ppermute | solution.py:399
  30.0 6.2 %collective-permute-done.2.box3 = bf16[8,26,8,128]{3,2,1,0:T(8,128)(2,1)S(1)} collective-permute-done((bf16[8,26,8,128]{3,2,1,0:T(8,128)(2,1)S(1)}, bf16[8,26,8,128]{3,2,1,0:T(8,128)(2,1)S(1)}, u32[]{:S(2)}, u32[]{:S(2)}) %collective-permute-start.2) | collective-permute-done | bytes 426016 | tf_op jit(solution)/shard_map/ppermute | solution.py:399
  36.2 2.7 %collective-permute-done.1.box2 = bf16[8,26,8,128]{3,2,1,0:T(8,128)(2,1)S(1)} collective-permute-done((bf16[8,26,8,128]{3,2,1,0:T(8,128)(2,1)S(1)}, bf16[8,26,8,128]{3,2,1,0:T(8,128)(2,1)S(1)}, u32[]{:S(2)}, u32[]{:S(2)}) %collective-permute-start.1) | collective-permute-done | bytes 426016 | tf_op jit(solution)/shard_map/ppermute | solution.py:399
  38.9 12.2 %collective-permute-done.box1 = bf16[8,26,8,128]{3,2,1,0:T(8,128)(2,1)S(1)} collective-permute-done((bf16[8,26,8,128]{3,2,1,0:T(8,128)(2,1)S(1)}, bf16[8,26,8,128]{3,2,1,0:T(8,128)(2,1)S(1)}, u32[]{:S(2)}, u32[]{:S(2)}) %collective-permute-start) | collective-permute-done | bytes 426016 | tf_op jit(solution)/shard_map/ppermute | solution.py:399
  51.2 16.0 %attend.1 = (bf16[2,64,4096]{2,1,0:T(8,128)(2,1)}, bf16[2,64,4096]{2,1,0:T(8,128)(2,1)}, bf16[2,64,1024]{2,1,0:T(8,128)(2,1)}, bf16[2,64,1024]{2,1,0:T(8,128)(2,...) custom-call(s32[2]{0:T(128)S(1)} %pad_add_fusion.place, ...), custom_call_target="tpu_custom_call" | custom-call | tf_op jit(solution)/shard_map/attend/pallas_call | solution.py:272
  67.3 0.8 copy-done.2
  69.4 0.8 copy-done.9
  70.2 0.8 copy-done.11
  70.9 0.7 copy-done.13
  71.7 12.5 %all_to_all.26.low_parts = bf16[32,8,128]{2,1,0:T(8,128)(2,1)} all-to-all(bf16[32,8,128]{2,1,0:T(8,128)(2,1)S(1)} %bitcast.23), channel_id=1, replica_groups=mesh['z'=8,'x'=4,'y'=4,'core'=2] {'z','x'}, dimensions={0} | all-to-all | bytes 131072 | tf_op jit(solution)/shard_map/all_to_all | solution.py:395
  84.2 2.8 %factor.1 = bf16[32,12,8,128]{3,2,1,0:T(8,128)(2,1)} custom-call(s32[1,1,2]{2,1,0:T(1,128)} %counts.5, bf16[32,8,128]{2,1,0:T(8,128)(2,1)} %all_to_all.26.low_parts, bf16[16,4096]{1,0:T(8,128)(2,1)} %bitcast.30, f32[64,1024]{1,0:T(8,128)} %copy-done.5, f32[64,1024]{1,0:T(8,128)} %copy-done.6), custom_call_target="tpu_custom_call" | custom-call | tf_op jit(solution)/shard_map/factor/pallas_call | solution.py:317
  87.0 7.2 %all-to-all-start.2 = ((bf16[32,12,8,128]{3,2,1,0:T(8,128)(2,1)}), bf16[32,12,8,128]{3,2,1,0:T(8,128)(2,1)S(1)}, u32[]{:S(2)}, u32[]{:S(2)}) async-start(bf16[32,12,8,128]{3,2,1,0:T(8,128)(2,1)} %factor.1), calls=%async_computation.2 | async-start | bytes 1572864 | tf_op jit(solution)/shard_map/all_to_all | solution.py:395
  94.2 2.7 %collective-permute-start.3 = (bf16[8,24,8,128]{3,2,1,0:T(8,128)(2,1)S(1)}, bf16[8,24,8,128]{3,2,1,0:T(8,128)(2,1)S(1)}, u32[]{:S(2)}, u32[]{:S(2)}) collective-permute-start(bf16[8,24,8,128]{3,2,1,0:T(8,128)(2,1)S(1)} %bitcast.26), channel_id=1, source_target_pairs={{0,24},{8,0},{16,8},{24,16},{1,25},{9,1},{17,9},{25,17},{2,26},{10... | collective-permute-start | bytes 1179656 | tf_op jit(solution)/shard_map/ppermute | solution.py:399
  98.1 15.3 %collective-permute-done.3.b = bf16[8,24,8,128]{3,2,1,0:T(8,128)(2,1)S(1)} collective-permute-done((bf16[8,24,8,128]{3,2,1,0:T(8,128)(2,1)S(1)}, bf16[8,24,8,128]{3,2,1,0:T(8,128)(2,1)S(1)}, u32[]{:S(2)}, u32[]{:S(2)}) %collective-permute-start.3) | collective-permute-done | bytes 393248 | tf_op jit(solution)/shard_map/ppermute | solution.py:399
  113.3 1.5 collective-permute-done.4.c
  114.8 8.2 %collective-permute-done.5.d = bf16[8,24,8,128]{3,2,1,0:T(8,128)(2,1)S(1)} collective-permute-done((bf16[8,24,8,128]{3,2,1,0:T(8,128)(2,1)S(1)}, bf16[8,24,8,128]{3,2,1,0:T(8,128)(2,1)S(1)}, u32[]{:S(2)}, u32[]{:S(2)}) %collective-permute-start.5) | collective-permute-done | bytes 393248 | tf_op jit(solution)/shard_map/ppermute | solution.py:399
  123.0 0.7 copy-done.18
  124.0 2.7 %middle.1 = bf16[8,36,8,128]{3,2,1,0:T(8,128)(2,1)} custom-call(bf16[32,12,8,128]{3,2,1,0:T(8,128)(2,1)} %copy-done.15, bf16[8,24,8,128]{3,2,1,0:T(8,128)(2,1)} %bitcast.20, bf16[8,24,8,128]{3,2,1,0:T(8,128)(2,1)} %copy-done.16, bf16[8,24,8,128]{3,2,1,0:T(8,128)(2,1)} %copy-done.17, bf16[8,24,8,128]{3,2,1,0:T(8,128)(2,1)} %copy-done.18), custom_call_target="tpu_custom_call" | custom-call | tf_op jit(solution)/shard_map/middle/pallas_call | solution.py:336
  126.7 22.3 %all_to_all.27.parts = bf16[8,36,8,128]{3,2,1,0:T(8,128)(2,1)} all-to-all(bf16[8,36,8,128]{3,2,1,0:T(8,128)(2,1)} %middle.1), channel_id=1, replica_groups=mesh['z'=8,'x'=4,'y'=4,'core'=2] {'z'}, dimensions={0} | all-to-all | bytes 1179648 | tf_op jit(solution)/shard_map/all_to_all | solution.py:395
  149.0 2.1 %close.1 = (bf16[16,2048]{1,0:T(8,128)(2,1)}, bf16[32,12,8,128]{3,2,1,0:T(8,128)(2,1)}) custom-call(s32[1,1,2]{2,1,0:T(1,128)} %counts.5, bf16[8,36,8,128]{3,2,1,0:T(8,128)(2,1)} %all_to_all.27.parts), custom_call_target="tpu_custom_call" | custom-call | tf_op jit(solution)/shard_map/close/pallas_call | solution.py:366
  151.1 21.5 %all_to_all.28.tiles = bf16[32,12,8,128]{3,2,1,0:T(8,128)(2,1)} all-to-all(bf16[32,12,8,128]{3,2,1,0:T(8,128)(2,1)} %get-tuple-element.31), channel_id=1, replica_groups=mesh['z'=8,'x'=4,'y'=4,'core'=2] {'x','y','core'}, dimensions={0} | all-to-all | bytes 1572864 | tf_op jit(solution)/shard_map/all_to_all | solution.py:395
  172.6 2.4 %unpack.1 = f32[64,6144]{1,0:T(8,128)} custom-call(bf16[32,12,8,128]{3,2,1,0:T(8,128)(2,1)} %all_to_all.28.tiles), custom_call_target="tpu_custom_call" | custom-call | tf_op jit(solution)/shard_map/unpack/pallas_call | solution.py:385
  (39 shorter events, 4.0 us)
Async XLA Ops:
  0.6 50.6 %copy-start.7 = (s32[1,1,2]{2,1,0:T(1,128)S(1)}, s32[1,1,2]{2,1,0:T(1,128)}, u32[]{:S(2)}) copy-start(s32[1,1,2]{2,1,0:T(1,128)} %docs.3) | copy-start | bytes 28
  0.6 50.6 %copy-start = (bf16[64,2048]{1,0:T(8,128)(2,1)S(1)}, bf16[64,2048]{1,0:T(8,128)(2,1)}, u32[]{:S(2)}) copy-start(bf16[64,2048]{1,0:T(8,128)(2,1)} %up_value.1) | copy-start | bytes 786436
  0.7 50.5 %copy-start.8 = (s32[1,1,2]{2,1,0:T(1,128)S(1)}, s32[1,1,2]{2,1,0:T(1,128)}, u32[]{:S(2)}) copy-start(s32[1,1,2]{2,1,0:T(1,128)} %ends.1) | copy-start | bytes 28
  0.7 50.5 %copy-start.4 = (bf16[1,1,2,64,1024]{4,3,2,1,0:T(8,128)(2,1)S(1)}, bf16[1,1,2,64,1024]{4,3,2,1,0:T(8,128)(2,1)}, u32[]{:S(2)}) copy-start(bf16[1,1,2,64,1024]{4,3,2,1,0:T(8,128)(2,1)} %param.13) | copy-start | bytes 786436
  0.7 50.5 %copy-start.3 = (bf16[1,1,2,64,1024]{4,3,2,1,0:T(8,128)(2,1)S(1)}, bf16[1,1,2,64,1024]{4,3,2,1,0:T(8,128)(2,1)}, u32[]{:S(2)}) copy-start(bf16[1,1,2,64,1024]{4,3,2,1,0:T(8,128)(2,1)} %param.12) | copy-start | bytes 786436
  0.7 50.5 %copy-start.1 = (bf16[1,1,2,64,4096]{4,3,2,1,0:T(8,128)(2,1)S(1)}, bf16[1,1,2,64,4096]{4,3,2,1,0:T(8,128)(2,1)}, u32[]{:S(2)}) copy-start(bf16[1,1,2,64,4096]{4,3,2,1,0:T(8,128)(2,1)} %param.11) | copy-start | bytes 3145732
  26.3 9.9 %collective-permute-start.2 = (bf16[8,26,8,128]{3,2,1,0:T(8,128)(2,1)S(1)}, bf16[8,26,8,128]{3,2,1,0:T(8,128)(2,1)S(1)}, u32[]{:S(2)}, u32[]{:S(2)}) collective-permute-start(bf16[8,26,8,128]{3,2,1,0:T(8,128)(2,1)S(1)} %all_to_all.25.box0), channel_id=1, source_target_pairs={{0,24},{8,0},{16,8},{24,16},{1,25},{9,1},{17,9},{25,17},{2,26},{10... | collective-permute-start | bytes 1277960 | tf_op jit(solution)/shard_map/ppermute | solution.py:399
  28.8 10.1 %collective-permute-start.1 = (bf16[8,26,8,128]{3,2,1,0:T(8,128)(2,1)S(1)}, bf16[8,26,8,128]{3,2,1,0:T(8,128)(2,1)S(1)}, u32[]{:S(2)}, u32[]{:S(2)}) collective-permute-start(bf16[8,26,8,128]{3,2,1,0:T(8,128)(2,1)S(1)} %all_to_all.25.box0), channel_id=1, source_target_pairs={{0,16},{8,24},{16,0},{24,8},{1,17},{9,25},{17,1},{25,9},{2,18},{10... | collective-permute-start | bytes 1277960 | tf_op jit(solution)/shard_map/ppermute | solution.py:399
  29.3 21.9 %collective-permute-start = (bf16[8,26,8,128]{3,2,1,0:T(8,128)(2,1)S(1)}, bf16[8,26,8,128]{3,2,1,0:T(8,128)(2,1)S(1)}, u32[]{:S(2)}, u32[]{:S(2)}) collective-permute-start(bf16[8,26,8,128]{3,2,1,0:T(8,128)(2,1)S(1)} %all_to_all.25.box0), channel_id=1, source_target_pairs={{0,8},{8,16},{16,24},{24,0},{1,9},{9,17},{17,25},{25,1},{2,10},{10... | collective-permute-start | bytes 1277960 | tf_op jit(solution)/shard_map/ppermute | solution.py:399
  67.3 0.8 copy-start.2
  69.4 0.8 copy-start.9
  70.2 0.8 copy-start.11
  70.9 0.7 copy-start.13
  84.2 10.0 %copy-start.14 = (bf16[8,3,8,8,128]{4,3,2,1,0:T(8,128)(2,1)S(1)}, bf16[8,3,8,8,128]{4,3,2,1,0:T(8,128)(2,1)}, u32[]{:S(2)}) copy-start(bf16[8,3,8,8,128]{4,3,2,1,0:T(8,128)(2,1)} %copy-done.13) | copy-start | bytes 1179652
  84.2 12.7 %copy-start.12 = (bf16[8,3,8,8,128]{4,3,2,1,0:T(8,128)(2,1)S(1)}, bf16[8,3,8,8,128]{4,3,2,1,0:T(8,128)(2,1)}, u32[]{:S(2)}) copy-start(bf16[8,3,8,8,128]{4,3,2,1,0:T(8,128)(2,1)} %copy-done.11) | copy-start | bytes 1179652
  84.2 13.3 %copy-start.10 = (bf16[8,3,8,8,128]{4,3,2,1,0:T(8,128)(2,1)S(1)}, bf16[8,3,8,8,128]{4,3,2,1,0:T(8,128)(2,1)}, u32[]{:S(2)}) copy-start(bf16[8,3,8,8,128]{4,3,2,1,0:T(8,128)(2,1)} %copy-done.9) | copy-start | bytes 1179652
  87.0 36.1 %all-to-all-start.2 = ((bf16[32,12,8,128]{3,2,1,0:T(8,128)(2,1)}), bf16[32,12,8,128]{3,2,1,0:T(8,128)(2,1)S(1)}, u32[]{:S(2)}, u32[]{:S(2)}) async-start(bf16[32,12,8,128]{3,2,1,0:T(8,128)(2,1)} %factor.1), calls=%async_computation.2 | async-start | bytes 1572864 | tf_op jit(solution)/shard_map/all_to_all | solution.py:395
  94.2 19.1 %collective-permute-start.3 = (bf16[8,24,8,128]{3,2,1,0:T(8,128)(2,1)S(1)}, bf16[8,24,8,128]{3,2,1,0:T(8,128)(2,1)S(1)}, u32[]{:S(2)}, u32[]{:S(2)}) collective-permute-start(bf16[8,24,8,128]{3,2,1,0:T(8,128)(2,1)S(1)} %bitcast.26), channel_id=1, source_target_pairs={{0,24},{8,0},{16,8},{24,16},{1,25},{9,1},{17,9},{25,17},{2,26},{10... | collective-permute-start | bytes 1179656 | tf_op jit(solution)/shard_map/ppermute | solution.py:399
  96.9 17.9 %collective-permute-start.4 = (bf16[8,24,8,128]{3,2,1,0:T(8,128)(2,1)S(1)}, bf16[8,24,8,128]{3,2,1,0:T(8,128)(2,1)S(1)}, u32[]{:S(2)}, u32[]{:S(2)}) collective-permute-start(bf16[8,24,8,128]{3,2,1,0:T(8,128)(2,1)S(1)} %bitcast.25), channel_id=1, source_target_pairs={{0,16},{8,24},{16,0},{24,8},{1,17},{9,25},{17,1},{25,9},{2,18},{10... | collective-permute-start | bytes 1179656 | tf_op jit(solution)/shard_map/ppermute | solution.py:399
  97.5 25.5 %collective-permute-start.5 = (bf16[8,24,8,128]{3,2,1,0:T(8,128)(2,1)S(1)}, bf16[8,24,8,128]{3,2,1,0:T(8,128)(2,1)S(1)}, u32[]{:S(2)}, u32[]{:S(2)}) collective-permute-start(bf16[8,24,8,128]{3,2,1,0:T(8,128)(2,1)S(1)} %bitcast.24), channel_id=1, source_target_pairs={{0,8},{8,16},{16,24},{24,0},{1,9},{9,17},{17,25},{25,1},{2,10},{10... | collective-permute-start | bytes 1179656 | tf_op jit(solution)/shard_map/ppermute | solution.py:399
  113.3 9.7 %copy-start.16 = (bf16[8,24,8,128]{3,2,1,0:T(8,128)(2,1)}, bf16[8,24,8,128]{3,2,1,0:T(8,128)(2,1)S(1)}, u32[]{:S(2)}) copy-start(bf16[8,24,8,128]{3,2,1,0:T(8,128)(2,1)S(1)} %collective-permute-done.3.b) | copy-start | bytes 1179652
  114.8 8.2 %copy-start.17 = (bf16[8,24,8,128]{3,2,1,0:T(8,128)(2,1)}, bf16[8,24,8,128]{3,2,1,0:T(8,128)(2,1)S(1)}, u32[]{:S(2)}) copy-start(bf16[8,24,8,128]{3,2,1,0:T(8,128)(2,1)S(1)} %collective-permute-done.4.c) | copy-start | bytes 1179652
  123.0 0.8 copy-start.18
  123.0 1.0 copy-start.15
  (2 other events, 1.4 us)

commit v3 on v2

--- a/solution.py
+++ b/solution.py
@@ -22,8 +22,10 @@
 ALL_AXES = ("z", "x", "y", "core")
 WIDE = ("x", "y", "core")
 
-TILES = 26
-GRAD_TILES = 24
+HEADS = 4
+HALF_TILES = 3 * HEADS
+LOW_TILE = HALF_TILES
+FACT_TILE = HALF_TILES + 1
 FAR = 384
 NEAR = 128
 KEYS = FAR + NEAR
@@ -44,7 +46,7 @@
     return jnp.where((slot == source) & (row < first + second), 1.0, 0.0)
 
 
-def project_kernel(counts, docs, state, down_t, up, frozen, out):
+def project_kernel(counts, docs, state, down_t, up, frozen, out_a, out_b):
     first, second = counts[0, 0, 0], counts[0, 0, 1]
     low = dot(state[...], down_t[...], ((1,), (1,))).astype(bf16)
     states = (frozen[...].astype(f32) + dot(low, up[...])).astype(bf16)
@@ -52,26 +54,29 @@
     rows = dot(pick, states)
     low_rows = dot(pick, low).astype(bf16)
     sub = lax.broadcasted_iota(jnp.int32, (8, HD), 0)
-    tiles = []
-    for h in range(2 * KVH):
-        tiles.append(rows[:8, h * HD : (h + 1) * HD])
-    for h in range(KVH):
-        keys = rows[8:, h * HD : (h + 1) * HD]
-        values = rows[8:, (KVH + h) * HD : (KVH + h + 1) * HD]
-        tiles.append(jnp.where(sub < 4, keys, pltpu.roll(values, 4, 0)))
+    halves = []
+    for heads in (range(HEADS), range(HEADS, KVH)):
+        tiles = [rows[:8, h * HD : (h + 1) * HD] for h in heads]
+        tiles += [rows[:8, (KVH + h) * HD : (KVH + h + 1) * HD] for h in heads]
+        for h in heads:
+            keys = rows[8:, h * HD : (h + 1) * HD]
+            values = rows[8:, (KVH + h) * HD : (KVH + h + 1) * HD]
+            tiles.append(jnp.where(sub < 4, keys, pltpu.roll(values, 4, 0)))
+        halves.append(tiles)
     put_row = lax.broadcasted_iota(jnp.int32, (UPDATE_RANK, HD), 0)
     put_col = lax.broadcasted_iota(jnp.int32, (UPDATE_RANK, HD), 1)
     left = jnp.where(put_row == put_col, 1.0, 0.0).astype(bf16)
     right = jnp.where(put_row + UPDATE_RANK == put_col, 1.0, 0.0).astype(bf16)
-    tiles.append((dot(low_rows, left)[:8] + dot(low_rows, right)[8:]))
+    halves[0].append(dot(low_rows, left)[:8] + dot(low_rows, right)[8:])
     facts = jnp.zeros((8, HD), f32)
     for i, fact in enumerate((first, second, docs[0, 0, 0], docs[0, 0, 1])):
         facts = jnp.where(sub == i, fact.astype(f32), facts)
-    tiles.append(facts)
-    for t, tile in enumerate(tiles):
-        packed = tile.astype(bf16)
-        for z in range(NZ):
-            out[z, t] = packed
+    halves[0].append(facts)
+    for out, tiles in zip((out_a, out_b), halves):
+        for t, tile in enumerate(tiles):
+            packed = tile.astype(bf16)
+            for z in range(NZ):
+                out[z, t] = packed
 
 
 VMEM = pl.BlockSpec(memory_space=pltpu.VMEM)
@@ -82,8 +87,11 @@
     return pl.pallas_call(
         project_kernel,
         in_specs=[SMEM] * 2 + [VMEM] * 4,
-        out_specs=VMEM,
-        out_shape=jax.ShapeDtypeStruct((NZ, TILES, 8, HD), bf16),
+        out_specs=[VMEM] * 2,
+        out_shape=[
+            jax.ShapeDtypeStruct((NZ, FACT_TILE + 1, 8, HD), bf16),
+            jax.ShapeDtypeStruct((NZ, HALF_TILES, 8, HD), bf16),
+        ],
         name="project",
     )(counts, docs, state, down_t, up, frozen)
 
@@ -106,7 +114,7 @@
         bias[block * 8 : block * 8 + 8, :] = jnp.where(seen, 0.0, MASKED)
 
     def facts(box, z, slot):
-        tile = boxes[box][z, 25].astype(f32)
+        tile = boxes[box][z, FACT_TILE].astype(f32)
         first, second = tile[0:1], tile[1:2]
         first_doc, second_doc = tile[2:3], tile[3:4]
         source = z * NX + lax.rem(x_own - box + NX, NX)
@@ -138,7 +146,7 @@
     lane = lax.broadcasted_iota(jnp.int32, (NZ, 8, HD), 2)
     sub = lax.broadcasted_iota(jnp.int32, (NZ // 2, 8, HD), 1)
     for b, box in enumerate(boxes):
-        tile = box[:, 24].astype(f32)
+        tile = box[:, LOW_TILE].astype(f32)
         head = jnp.where(lane < UPDATE_RANK, tile, 0.0)
         low_all[b * 64 : b * 64 + 64, :] = head.reshape(64, HD).astype(bf16)
         tail = jnp.where(lane < UPDATE_RANK, pltpu.roll(tile, UPDATE_RANK, 2), 0.0)
@@ -150,8 +158,9 @@
 
 def attend_kernel(
     place, docs, ends, query, key, value, grad, up_key, up_value, box0, box1, box2, box3,
+    bias, low_all, low_before,
     attended, grad_query, grad_key, grad_value, out0, out1, out2, out3, up_key_part,
-    up_value_part, low_part, bias, low_all, low_total,
+    up_value_part, low_part, low_total, last,
 ):
     boxes = (box0, box1, box2, box3)
     outs = (out0, out1, out2, out3)
@@ -159,9 +168,12 @@
 
     @pl.when(g == 0)
     def _():
-        fill_bias(place, docs, ends, boxes, bias)
-        gather_low(boxes, low_all)
-        low_total[...] = jnp.zeros_like(low_total)
+        if low_before is None:
+            fill_bias(place, docs, ends, boxes, bias)
+            gather_low(boxes, low_all)
+            low_total[...] = jnp.zeros_like(low_total)
+        else:
+            low_total[...] = low_before[...]
 
     sub = lax.broadcasted_iota(jnp.int32, (NZ // 2, 8, HD), 1)
 
@@ -176,7 +188,7 @@
 
     extra_keys, extra_values = [], []
     for box in boxes:
-        both = box[:, 16 + g].astype(f32).reshape(NZ // 2, 2, 8, HD)
+        both = box[:, 2 * HEADS + g].astype(f32).reshape(NZ // 2, 2, 8, HD)
         even, odd = both[:, 0], both[:, 1]
         extra_keys.append(jnp.where(sub < 4, even, pltpu.roll(odd, 4, 1)).reshape(4 * NZ, HD))
         extra_values.append(jnp.where(sub < 4, pltpu.roll(even, 4, 1), odd).reshape(4 * NZ, HD))
@@ -184,7 +196,7 @@
         [key[...].reshape(NEAR, HD).astype(f32)] + far_rows(g) + extra_keys, axis=0
     )
     values = jnp.concatenate(
-        [value[...].reshape(NEAR, HD).astype(f32)] + far_rows(KVH + g) + extra_values, axis=0
+        [value[...].reshape(NEAR, HD).astype(f32)] + far_rows(HEADS + g) + extra_values, axis=0
     )
     keys_t = keys.T.astype(bf16)
     values_t = values.T.astype(bf16)
@@ -242,7 +254,10 @@
     low_total[...] += dot(far_keys, twice(up_key), ((1,), (1,)))
     low_total[...] += dot(far_values, twice(up_value), ((1,), (1,)))
 
-    @pl.when(g == KVH - 1)
+    if not last:
+        return
+
+    @pl.when(g == HEADS - 1)
     def _():
         lane = lax.broadcasted_iota(jnp.int32, (8, HD), 1)
         for b in range(NX):
@@ -257,34 +272,76 @@
                 low_part[z, x] = jnp.where(lane < UPDATE_RANK, head, tail).astype(bf16)
 
 
-def attend(place, docs, ends, query, key, value, grad, up, boxes):
-    wide = pl.BlockSpec((2, SPAN, GROUP * HD), lambda g: (0, 0, g))
-    narrow = pl.BlockSpec((2, SPAN, HD), lambda g: (0, 0, g))
-    whole = pl.BlockSpec((NZ, TILES, 8, HD), lambda g: (0, 0, 0, 0))
+def first_kernel(*refs):
+    (place, docs, ends, query, key, value, grad, up_key, up_value, *boxes) = refs[:13]
+    (attended, grad_query, grad_key, grad_value, *rest) = refs[13:]
+    outs, (up_k, up_v, low_total, bias, low_all) = rest[:4], rest[4:]
+    attend_kernel(
+        place, docs, ends, query, key, value, grad, up_key, up_value, *boxes,
+        bias, low_all, None,
+        attended, grad_query, grad_key, grad_value, *outs, up_k, up_v, None, low_total, False,
+    )
+
+
+def second_kernel(*refs):
+    (place, query, key, value, grad, up_key, up_value, *boxes) = refs[:11]
+    bias, low_all, low_before = refs[11:14]
+    (attended, grad_query, grad_key, grad_value, *rest) = refs[18:]
+    outs, (up_k, up_v, low_part, low_total) = rest[:4], rest[4:]
+    attend_kernel(
+        place, None, None, query, key, value, grad, up_key, up_value, *boxes,
+        bias, low_all, low_before,
+        attended, grad_query, grad_key, grad_value, *outs, up_k, up_v, low_part, low_total, True,
+    )
+
+
+def attend(half, small, query, key, value, grad, up, boxes, carried=(), filled=()):
+    at = half * HEADS
+    wide = pl.BlockSpec((2, SPAN, GROUP * HD), lambda g: (0, 0, g + at))
+    narrow = pl.BlockSpec((2, SPAN, HD), lambda g: (0, 0, g + at))
+    whole = pl.BlockSpec(boxes[0].shape, lambda g: (0, 0, 0, 0))
     part = pl.BlockSpec((NZ, 3, 1, 8, HD), lambda g: (0, 0, g, 0, 0))
-    up_key = pl.BlockSpec((UPDATE_RANK, HD), lambda g: (0, g))
-    up_value = pl.BlockSpec((UPDATE_RANK, HD), lambda g: (0, KVH + g))
+    up_key = pl.BlockSpec((UPDATE_RANK, HD), lambda g: (0, g + at))
+    up_value = pl.BlockSpec((UPDATE_RANK, HD), lambda g: (0, KVH + g + at))
+    up_part = pl.BlockSpec((UPDATE_RANK, HD), lambda g: (0, g))
     low_part = pl.BlockSpec((NZ, NX, 8, HD), lambda g: (0, 0, 0, 0))
     wide_shape = jax.ShapeDtypeStruct((2, SPAN, QW), bf16)
     narrow_shape = jax.ShapeDtypeStruct((2, SPAN, KEY_FEATURES), bf16)
-    part_shape = jax.ShapeDtypeStruct((NZ, 3, KVH, 8, HD), bf16)
-    up_shape = jax.ShapeDtypeStruct((UPDATE_RANK, KEY_FEATURES), f32)
+    part_shape = jax.ShapeDtypeStruct((NZ, 3, HEADS, 8, HD), bf16)
+    up_shape = jax.ShapeDtypeStruct((UPDATE_RANK, HEADS * HD), f32)
+    kept = [
+        jax.ShapeDtypeStruct((FAR, HD), f32),
+        jax.ShapeDtypeStruct((KEYS, NEAR), f32),
+        jax.ShapeDtypeStruct((FAR, HD), bf16),
+    ]
+    kept_specs = [pl.BlockSpec(k.shape, lambda g: (0, 0)) for k in kept]
+    in_specs = [SMEM] * len(small) + [wide, narrow, narrow, wide, up_key, up_value] + [whole] * NX
+    out_specs = [wide, wide, narrow, narrow] + [part] * NX + [up_part] * 2
+    out_shape = [wide_shape] * 2 + [narrow_shape] * 2 + [part_shape] * NX + [up_shape] * 2
+    scratch, aliases = [], {}
+    if half == 0:
+        out_specs += kept_specs
+        out_shape += kept
+    else:
+        in_specs += kept_specs[1:] + kept_specs[:1] + [pl.BlockSpec(memory_space=pl.ANY)] * 4
+        out_specs.append(low_part)
+        out_shape.append(jax.ShapeDtypeStruct((NZ, NX, 8, HD), bf16))
+        scratch = [pltpu.VMEM((FAR, HD), f32)]
+        aliases = {len(in_specs) - 4 + i: i for i in range(4)}
     return pl.pallas_call(
-        attend_kernel,
-        grid=(KVH,),
-        in_specs=[SMEM] * 3 + [wide, narrow, narrow, wide, up_key, up_value] + [whole] * NX,
-        out_specs=[wide, wide, narrow, narrow] + [part] * NX + [up_key, up_key, low_part],
-        out_shape=[wide_shape, wide_shape, narrow_shape, narrow_shape]
-        + [part_shape] * NX
-        + [up_shape, up_shape, jax.ShapeDtypeStruct((NZ, NX, 8, HD), bf16)],
-        scratch_shapes=[
-            pltpu.VMEM((KEYS, NEAR), f32),
-            pltpu.VMEM((FAR, HD), bf16),
-            pltpu.VMEM((FAR, HD), f32),
-        ],
-        compiler_params=pltpu.CompilerParams(vmem_limit_bytes=48 * 1024 * 1024),
-        name="attend",
-    )(place, docs, ends, query, key, value, grad, up, up, *boxes)
+        (first_kernel, second_kernel)[half],
+        grid=(HEADS,),
+        in_specs=in_specs,
+        out_specs=out_specs,
+        out_shape=out_shape,
+        scratch_shapes=scratch,
+        input_output_aliases=aliases,
+        compiler_params=pltpu.CompilerParams(vmem_limit_bytes=20 * 1024 * 1024),
+        cost_estimate=pl.CostEstimate(
+            flops=6 * 10**9, bytes_accessed=4 * 2**20, transcendentals=HEADS * KEYS * ROWS
+        ),
+        name=("attend_first", "attend_second")[half],
+    )(*small, query, key, value, grad, up, up, *boxes, *carried, *filled)
 
 
 PER_ROW = (MODEL_WIDTH + 2 * KEY_FEATURES) // HD
@@ -292,52 +349,54 @@
 CHUNKS = 8 * PER_ROW // CHUNK
 
 
-def factor_kernel(counts, low_parts, state, up_key, up_value, pieces):
+def factor_kernel(counts, low_parts, state, key_a, value_a, key_b, value_b, pieces):
     pick = selection(counts[0, 0, 0], counts[0, 0, 1])
     total = jnp.sum(low_parts[...].astype(f32), axis=0)
     compact = jnp.concatenate([total, pltpu.roll(total, UPDATE_RANK, 1)], axis=0).astype(bf16)
     low_grad = dot(pick.astype(bf16), compact, ((0,), (0,))).astype(bf16)
     down_piece = dot(low_grad, state[...], ((0,), (0,)))
     wide = MODEL_WIDTH // HD
+    ups = (key_a, key_b, value_a, value_b)
     for t in range(8 * PER_ROW):
         r, c = divmod(t, PER_ROW)
         rows = slice(r * 8, r * 8 + 8)
         if c < wide:
             tile = down_piece[rows, c * HD : (c + 1) * HD]
-        elif c < wide + KVH:
-            c -= wide
-            tile = up_key[rows, c * HD : (c + 1) * HD]
         else:
-            c -= wide + KVH
-            tile = up_value[rows, c * HD : (c + 1) * HD]
+            which, c = divmod(c - wide, HEADS)
+            tile = ups[which][rows, c * HD : (c + 1) * HD]
         pieces[t // CHUNK, t % CHUNK] = tile.astype(bf16)
 
 
-def factor(counts, low_parts, state, up_key, up_value):
+def factor(counts, low_parts, state, ups):
     return pl.pallas_call(
         factor_kernel,
-        in_specs=[SMEM] + [VMEM] * 4,
+        in_specs=[SMEM] + [VMEM] * 6,
         out_specs=VMEM,
         out_shape=jax.ShapeDtypeStruct((CHUNKS, CHUNK, 8, HD), bf16),
         name="factor",
-    )(counts, low_parts, state, up_key, up_value)
-
-
-def middle_kernel(pieces, a, b, c, d, out):
+    )(counts, low_parts, state, *ups)
+
+
+def middle_kernel(pieces, *refs):
+    out = refs[-1]
     chunk = jnp.sum(pieces[...].astype(f32), axis=0).astype(bf16)
     for z in range(NZ):
         out[z, :CHUNK] = chunk
-        out[z, CHUNK:] = (
-            (a[z].astype(f32) + b[z].astype(f32)) + (c[z].astype(f32) + d[z].astype(f32))
-        ).astype(bf16)
+        for half in range(2):
+            a, b, c, d = refs[half * NX : half * NX + NX]
+            at = CHUNK + half * HALF_TILES
+            out[z, at : at + HALF_TILES] = (
+                (a[z].astype(f32) + b[z].astype(f32)) + (c[z].astype(f32) + d[z].astype(f32))
+            ).astype(bf16)
 
 
 def middle(pieces, parts):
     return pl.pallas_call(
         middle_kernel,
-        in_specs=[VMEM] * 5,
+        in_specs=[VMEM] * (1 + len(parts)),
         out_specs=VMEM,
-        out_shape=jax.ShapeDtypeStruct((NZ, CHUNK + GRAD_TILES, 8, HD), bf16),
+        out_shape=jax.ShapeDtypeStruct((NZ, CHUNK + 2 * HALF_TILES, 8, HD), bf16),
         name="middle",
     )(pieces, *parts)
 
@@ -348,16 +407,21 @@
     chunk = total[:CHUNK].astype(bf16)
     for i in range(CHUNKS):
         out[i] = chunk
-    total = total[CHUNK:]
     sub = lax.broadcasted_iota(jnp.int32, (8, HD), 0)
-    tops = [total[h] for h in range(2 * KVH)]
-    rest_keys, rest_values = [], []
+    top_keys, top_values, rest_keys, rest_values = [], [], [], []
     for h in range(KVH):
-        both = total[16 + h]
+        at = CHUNK + h // HEADS * HALF_TILES + h % HEADS
+        top_keys.append(total[at])
+        top_values.append(total[at + HEADS])
+        both = total[at + 2 * HEADS]
         rest_keys.append(jnp.where(sub < 4, both, 0.0))
         rest_values.append(jnp.where(sub < 4, pltpu.roll(both, 4, 0), 0.0))
     compact = jnp.concatenate(
-        [jnp.concatenate(tops, axis=1), jnp.concatenate(rest_keys + rest_values, axis=1)], axis=0
+        [
+            jnp.concatenate(top_keys + top_values, axis=1),
+            jnp.concatenate(rest_keys + rest_values, axis=1),
+        ],
+        axis=0,
     ).astype(bf16)
     cache_out[...] = dot(pick, compact, ((0,), (0,))).astype(bf16)
 
@@ -399,6 +463,15 @@
     return lax.ppermute(x, "x", [(i, (i + by) % NX) for i in range(NX)])
 
 
+def spread(column):
+    return [column, shift(column, 1), shift(column, 2), shift(column, 3)]
+
+
+def collect(parts):
+    parts = [p.reshape(NZ, HALF_TILES, 8, HD) for p in parts]
+    return [parts[0], shift(parts[1], -1), shift(parts[2], -2), shift(parts[3], -3)]
+
+
 def local(
     query, key, value, beacon_slot_state, frozen_beacon_cache, adapter_down_weight,
     adapter_up_weight, output_cotangent, span_beacon_count, span_document, boundary,
@@ -407,21 +480,23 @@
     state = beacon_slot_state[0, 0].reshape(2 * MAX_BEACONS, MODEL_WIDTH)
     frozen = frozen_beacon_cache[0, 0].reshape(2 * MAX_BEACONS, 2 * KEY_FEATURES)
 
-    message = project(
+    message_a, message_b = project(
         span_beacon_count, span_document, state, adapter_down_weight.T, adapter_up_weight, frozen
     )
-    column = exchange(message, "z")
-    boxes = [column, shift(column, 1), shift(column, 2), shift(column, 3)]
-    attended, grad_query, grad_key, grad_value, *rest = attend(
-        place, span_document, boundary, query[0, 0], key[0, 0], value[0, 0],
-        output_cotangent[0, 0], adapter_up_weight, boxes,
-    )
-    parts = [p.reshape(NZ, GRAD_TILES, 8, HD) for p in rest[:NX]]
-    up_key, up_value, low_part = rest[NX:]
-    parts = [parts[0], shift(parts[1], -1), shift(parts[2], -2), shift(parts[3], -3)]
+    arrays = (query[0, 0], key[0, 0], value[0, 0], output_cotangent[0, 0], adapter_up_weight)
+    boxes_a = spread(exchange(message_a, "z"))
+    boxes_b = spread(exchange(message_b, "z"))
+    first = attend(0, (place, span_document, boundary), *arrays, boxes_a)
+    low_total, bias, low_all = first[10:]
+    parts_a = collect(first[4:8])
+    second = attend(1, (place,), *arrays, boxes_b, (bias, low_all, low_total), first[:4])
+    parts_b = collect(second[4:8])
+    attended, grad_query, grad_key, grad_value = second[:4]
+    low_part, parts_a = lax.optimization_barrier((second[10], parts_a))
     low_parts = exchange(low_part.reshape(NZ * NX, 8, HD), ("z", "x"))
-    pieces = factor(span_beacon_count, low_parts, state, up_key, up_value)
-    both = exchange(middle(exchange(pieces, WIDE), parts), "z")
+    low_parts, parts_b = lax.optimization_barrier((low_parts, parts_b))
+    pieces = factor(span_beacon_count, low_parts, state, first[8:10] + second[8:10])
+    both = exchange(middle(exchange(pieces, WIDE), parts_a + parts_b), "z")
     cache_gradient, chunk = close(span_beacon_count, both)
     adapter_gradient = unpack(exchange(chunk, WIDE))
     return (

time: 176 us -> 168 us (0.955)
  waiting for transfers between devices: 46.1 us -> 17.3 us
  starting transfers between devices: 14.7 us -> 26.5 us
  blocking collectives: 79.1 us -> 87.2 us
    ppermute x6 -> x12, waiting for transfers between devices: 46.1 us -> 3.7 us  [shift(): return lax.ppermute(x, 'x', [(i, (i + by) % NX) for i in range(NX)])]
    all_to_all x1 -> x2, waiting for transfers between devices: 0.01 us -> 13.6 us  [exchange(): return lax.all_to_all(x, axes, 0, 0, tiled=True)]
    all_to_all x4, blocking collectives: 79.1 us -> 87.2 us  [exchange(): return lax.all_to_all(x, axes, 0, 0, tiled=True)]
    all_to_all x1 -> x2, starting transfers between devices: 7.24 us -> 13.4 us  [exchange(): return lax.all_to_all(x, axes, 0, 0, tiled=True)]
    ppermute x6 -> x12, starting transfers between devices: 7.44 us -> 13.2 us  [shift(): return lax.ppermute(x, 'x', [(i, (i + by) % NX) for i in range(NX)])]
    pallas_call x3 -> x4, Pallas kernels: 21.5 us -> 22.3 us  [the longest x2 16.8 us: attend(): pl.pallas_call((first_kernel, second_kernel)[half], grid=(HEADS,), in_spe...]
    unnamed x38 -> x42, local copies, waits for them, and re-layouts: 5.45 us -> 5.89 us
  transfers between devices with their start and end apart: 7 -> 14, of which waited for: 6 -> 3; matrix products, arithmetic and copies ran while one was open for 0% -> 0% of each run, Pallas kernels for 0% -> 10%
where the time goes in v3:
time: 168 us; the launch traced here: 167 us
  blocking collectives  87.2 us (52%)
  Pallas kernels  29.5 us (18%)
  starting transfers between devices  26.5 us (16%)
  waiting for transfers between devices  17.3 us (10%)
  local copies, waits for them, and re-layouts  5.89 us (4%)
    all_to_all x4, blocking collectives, exchange(): return lax.all_to_all(x, axes, 0, 0, tiled=True)  87.2 us
    pallas_call x2, Pallas kernels, attend(): pl.pallas_call((first_kernel, second_kernel)[half], grid=(HEADS,), in_spe...  16.8 us
    all_to_all x2, waiting for transfers between devices, exchange(): return lax.all_to_all(x, axes, 0, 0, tiled=True)  13.6 us
    all_to_all x2, starting transfers between devices, exchange(): return lax.all_to_all(x, axes, 0, 0, tiled=True)  13.4 us
    ppermute x12, starting transfers between devices, shift(): return lax.ppermute(x, 'x', [(i, (i + by) % NX) for i in range(NX)])  13.2 us
    unnamed x42, local copies, waits for them, and re-layouts  5.89 us
    ppermute x12, waiting for transfers between devices, shift(): return lax.ppermute(x, 'x', [(i, (i + by) % NX) for i in range(NX)])  3.7 us
  transfers between devices with their start and end apart: 14, of which 3 were waited for; matrix products, arithmetic and copies ran while one was open for 0% of the time, Pallas kernels for 10%

profile of v3, /device:TPU:1, one launch (start us, length us, event | category | flops | bytes accessed | tf_op | source)
XLA Modules:
  0.0 167.3 jit_solution(13817859566063047133)
XLA Ops:
  0.7 2.7 %project.1 = (bf16[8,14,8,128]{3,2,1,0:T(8,128)(2,1)}, bf16[8,12,8,128]{3,2,1,0:T(8,128)(2,1)}) custom-call(s32[1,1,2]{2,1,0:T(1,128)} %counts.5, s32[1,1,2]{2,1,0:T(1,128)} %refs_1_.1, bf16[16,4096]{1,0:T(8,128)(2,1)} %bitcast.40, bf16[64,4096]{1,0:T(8,128)(2,1)} %bitcast.39, bf16[64,2048]{1,0:T(8,128)(2,1)} %refs_6_.1, bf16[16,2048]{1,0:T(8,128)(2,1)} %bitcast.42), custom_call_target="tpu_custom_call" | custom-call | tf_op jit(solution)/shard_map/project/pallas_call | solution.py:87
  3.4 18.8 %all_to_all.30.refs_9_ = bf16[8,14,8,128]{3,2,1,0:T(8,128)(2,1)S(1)} all-to-all(bf16[8,14,8,128]{3,2,1,0:T(8,128)(2,1)} %get-tuple-element.45), channel_id=1, replica_groups=mesh['z'=8,'x'=4,'y'=4,'core'=2] {'z'}, dimensions={0} | all-to-all | bytes 458752 | tf_op jit(solution)/shard_map/all_to_all | solution.py:459
  22.2 3.4 %all-to-all-start = ((bf16[8,12,8,128]{3,2,1,0:T(8,128)(2,1)}), bf16[8,12,8,128]{3,2,1,0:T(8,128)(2,1)S(1)}, u32[]{:S(2)}, u32[]{:S(2)}) async-start(bf16[8,12,8,128]{3,2,1,0:T(8,128)(2,1)} %get-tuple-element.44), calls=%async_computation | async-start | bytes 393216 | tf_op jit(solution)/shard_map/all_to_all | solution.py:459
  25.6 2.6 %collective-permute-start.5 = (bf16[8,14,8,128]{3,2,1,0:T(8,128)(2,1)S(1)}, bf16[8,14,8,128]{3,2,1,0:T(8,128)(2,1)S(1)}, u32[]{:S(2)}, u32[]{:S(2)}) collective-permute-start(bf16[8,14,8,128]{3,2,1,0:T(8,128)(2,1)S(1)} %all_to_all.30.refs_9_), channel_id=1, source_target_pairs={{0,24},{8,0},{16,8},{24,16},{1,25},{9,1},{17,9},{25,17},{2,26},{10... | collective-permute-start | bytes 688136 | tf_op jit(solution)/shard_map/ppermute | solution.py:463
  29.3 4.8 %all-to-all-done.refs_7_ = bf16[8,12,8,128]{3,2,1,0:T(8,128)(2,1)S(1)} async-done(((bf16[8,12,8,128]{3,2,1,0:T(8,128)(2,1)}), bf16[8,12,8,128]{3,2,1,0:T(8,128)(2,1)S(1)}, u32[]{:S(2)}, u32[]{:S(2)}) %all-to-all-start) | async-done | bytes 196640 | tf_op jit(solution)/shard_map/all_to_all | solution.py:459
  34.1 2.5 %collective-permute-start.2 = (bf16[8,12,8,128]{3,2,1,0:T(8,128)(2,1)S(1)}, bf16[8,12,8,128]{3,2,1,0:T(8,128)(2,1)S(1)}, u32[]{:S(2)}, u32[]{:S(2)}) collective-permute-start(bf16[8,12,8,128]{3,2,1,0:T(8,128)(2,1)S(1)} %all-to-all-done.refs_7_), channel_id=1, source_target_pairs={{0,24},{8,0},{16,8},{24,16},{1,25},{9,1},{17,9},{25,17},{2,26},{10... | collective-permute-start | bytes 589832 | tf_op jit(solution)/shard_map/ppermute | solution.py:463
  37.8 3.7 %collective-permute-done.3.refs_10_ = bf16[8,14,8,128]{3,2,1,0:T(8,128)(2,1)S(1)} collective-permute-done((bf16[8,14,8,128]{3,2,1,0:T(8,128)(2,1)S(1)}, bf16[8,14,8,128]{3,2,1,0:T(8,128)(2,1)S(1)}, u32[]{:S(2)}, u32[]{:S(2)}) %collective-permute-start.3) | collective-permute-done | bytes 229408 | tf_op jit(solution)/shard_map/ppermute | solution.py:463
  41.5 1.2 copy-done.9
  42.7 8.4 %attend_first.1 = (bf16[2,64,4096]{2,1,0:T(8,128)(2,1)}, bf16[2,64,4096]{2,1,0:T(8,128)(2,1)}, bf16[2,64,1024]{2,1,0:T(8,128)(2,1)}, bf16[2,64,1024]{2,1,0:T(8,1...) custom-call(s32[2]{0:T(128)S(1)} %pad_add_fusion.refs_0_, ...), custom_call_target="tpu_custom_call" | custom-call | flops 6000000000 | bytes 4194304 | tf_op jit(solution)/shard_map/attend_first/pallas_call | solution.py:331
  51.0 0.7 copy-done.1
  53.1 1.5 collective-permute-start.8
  54.5 8.4 %attend_second.1 = (bf16[2,64,4096]{2,1,0:T(8,128)(2,1)}, bf16[2,64,4096]{2,1,0:T(8,128)(2,1)}, bf16[2,64,1024]{2,1,0:T(8,128)(2,1)}, bf16[2,64,1024]{2,1,0:T(8,...) custom-call(s32[2]{0:T(128)S(1)} %pad_add_fusion.refs_0_, ...), custom_call_target="tpu_custom_call", output_to_operand_aliasing={{0}: (14, {}), {1}: (15, {}), {2}: (16, {}), {3}: (17, {})} | custom-call | flops 6000000000 | bytes 4194304 | tf_op jit(solution)/shard_map/attend_second/pallas_call | solution.py:331
  64.9 2.4 %collective-permute-start.9 = (bf16[8,12,8,128]{3,2,1,0:T(8,128)(2,1)S(1)}, bf16[8,12,8,128]{3,2,1,0:T(8,128)(2,1)S(1)}, u32[]{:S(2)}, u32[]{:S(2)}) collective-permute-start(bf16[8,12,8,128]{3,2,1,0:T(8,128)(2,1)S(1)} %bitcast.38), channel_id=1, source_target_pairs={{0,24},{8,0},{16,8},{24,16},{1,25},{9,1},{17,9},{25,17},{2,26},{10... | collective-permute-start | bytes 589832 | tf_op jit(solution)/shard_map/ppermute | solution.py:463
  67.3 1.2 collective-permute-start.10
  68.5 0.9 collective-permute-start.11
  69.4 10.0 %all-to-all-start.2 = ((bf16[32,8,128]{2,1,0:T(8,128)(2,1)}), bf16[32,8,128]{2,1,0:T(8,128)(2,1)S(1)}, u32[]{:S(2)}, u32[]{:S(2)}) async-start(bf16[32,8,128]{2,1,0:T(8,128)(2,1)} %bitcast.17), calls=%async_computation.2 | async-start | bytes 131072 | tf_op jit(solution)/shard_map/all_to_all | solution.py:459
  79.4 8.8 %all-to-all-done.2.low_parts = bf16[32,8,128]{2,1,0:T(8,128)(2,1)S(1)} async-done(((bf16[32,8,128]{2,1,0:T(8,128)(2,1)}), bf16[32,8,128]{2,1,0:T(8,128)(2,1)S(1)}, u32[]{:S(2)}, u32[]{:S(2)}) %all-to-all-start.2) | async-done | bytes 65568 | tf_op jit(solution)/shard_map/all_to_all | solution.py:459
  88.8 2.7 %factor.1 = bf16[32,12,8,128]{3,2,1,0:T(8,128)(2,1)} custom-call(s32[1,1,2]{2,1,0:T(1,128)} %counts.5, bf16[32,8,128]{2,1,0:T(8,128)(2,1)} %copy-done.14, bf16[16,4096]{1,0:T(8,128)(2,1)} %bitcast.41, f32[64,512]{1,0:T(8,128)} %copy-done.3, f32[64,512]{1,0:T(8,128)} %copy-done.4, f32[64,512]{1,0:T(8,128)} %copy-done.5, f32[64,512]{1,0:T(8,128)} %copy-done.6), custom_call_target="tpu_custom_call" | custom-call | tf_op jit(solution)/shard_map/factor/pallas_call | solution.py:372
  91.6 25.8 %all_to_all.31.pieces = bf16[32,12,8,128]{3,2,1,0:T(8,128)(2,1)} all-to-all(bf16[32,12,8,128]{3,2,1,0:T(8,128)(2,1)} %factor.1), channel_id=1, replica_groups=mesh['z'=8,'x'=4,'y'=4,'core'=2] {'x','y','core'}, dimensions={0} | all-to-all | bytes 1572864 | tf_op jit(solution)/shard_map/all_to_all | solution.py:459
  117.4 2.8 %middle.1 = bf16[8,36,8,128]{3,2,1,0:T(8,128)(2,1)} custom-call(bf16[32,12,8,128]{3,2,1,0:T(8,128)(2,1)} %all_to_all.31.pieces, bf16[8,12,8,128]{3,2,1,0:T(8,128)(2,1)} %bitcast.23, bf16[8,12,8,128]{3,2,1,0:T(8,128)(2,1)} %copy-done.15, bf16[8,12,8,128]{3,2,1,0:T(8,128)(2,1)} %copy-done.16, bf16[8,12,8,128]{3,2,1,0:T(8,128)(2,1)} %copy-done.17, ...), custom_call_target="tpu_custom_call" | custom-call | tf_op jit(solution)/shard_map/middle/pallas_call | solution.py:395
  120.2 23.6 %all_to_all.32.parts = bf16[8,36,8,128]{3,2,1,0:T(8,128)(2,1)} all-to-all(bf16[8,36,8,128]{3,2,1,0:T(8,128)(2,1)} %middle.1), channel_id=1, replica_groups=mesh['z'=8,'x'=4,'y'=4,'core'=2] {'z'}, dimensions={0} | all-to-all | bytes 1179648 | tf_op jit(solution)/shard_map/all_to_all | solution.py:459
  143.8 2.1 %close.1 = (bf16[16,2048]{1,0:T(8,128)(2,1)}, bf16[32,12,8,128]{3,2,1,0:T(8,128)(2,1)}) custom-call(s32[1,1,2]{2,1,0:T(1,128)} %counts.5, bf16[8,36,8,128]{3,2,1,0:T(8,128)(2,1)} %all_to_all.32.parts), custom_call_target="tpu_custom_call" | custom-call | tf_op jit(solution)/shard_map/close/pallas_call | solution.py:430
  145.9 19.0 %all_to_all.33.tiles = bf16[32,12,8,128]{3,2,1,0:T(8,128)(2,1)} all-to-all(bf16[32,12,8,128]{3,2,1,0:T(8,128)(2,1)} %get-tuple-element.81), channel_id=1, replica_groups=mesh['z'=8,'x'=4,'y'=4,'core'=2] {'x','y','core'}, dimensions={0} | all-to-all | bytes 1572864 | tf_op jit(solution)/shard_map/all_to_all | solution.py:459
  164.9 2.4 %unpack.1 = f32[64,6144]{1,0:T(8,128)} custom-call(bf16[32,12,8,128]{3,2,1,0:T(8,128)(2,1)} %all_to_all.33.tiles), custom_call_target="tpu_custom_call" | custom-call | tf_op jit(solution)/shard_map/unpack/pallas_call | solution.py:449
  (58 shorter events, 6.4 us)
Async XLA Ops:
  0.6 40.8 %copy-start = (bf16[64,2048]{1,0:T(8,128)(2,1)S(1)}, bf16[64,2048]{1,0:T(8,128)(2,1)}, u32[]{:S(2)}) copy-start(bf16[64,2048]{1,0:T(8,128)(2,1)} %refs_6_.1) | copy-start | bytes 786436
  0.6 40.8 %copy-start.7 = (s32[1,1,2]{2,1,0:T(1,128)S(1)}, s32[1,1,2]{2,1,0:T(1,128)}, u32[]{:S(2)}) copy-start(s32[1,1,2]{2,1,0:T(1,128)} %refs_1_.1) | copy-start | bytes 28
  0.7 40.8 %copy-start.13 = (s32[1,1,2]{2,1,0:T(1,128)S(1)}, s32[1,1,2]{2,1,0:T(1,128)}, u32[]{:S(2)}) copy-start(s32[1,1,2]{2,1,0:T(1,128)} %refs_2_.1) | copy-start | bytes 28
  0.7 40.8 %copy-start.12 = (bf16[1,1,2,64,1024]{4,3,2,1,0:T(8,128)(2,1)S(1)}, bf16[1,1,2,64,1024]{4,3,2,1,0:T(8,128)(2,1)}, u32[]{:S(2)}) copy-start(bf16[1,1,2,64,1024]{4,3,2,1,0:T(8,128)(2,1)} %param.13) | copy-start | bytes 786436
  0.7 40.8 %copy-start.11 = (bf16[1,1,2,64,1024]{4,3,2,1,0:T(8,128)(2,1)S(1)}, bf16[1,1,2,64,1024]{4,3,2,1,0:T(8,128)(2,1)}, u32[]{:S(2)}) copy-start(bf16[1,1,2,64,1024]{4,3,2,1,0:T(8,128)(2,1)} %param.12) | copy-start | bytes 786436
  0.7 40.8 %copy-start.8 = (bf16[1,1,2,64,4096]{4,3,2,1,0:T(8,128)(2,1)S(1)}, bf16[1,1,2,64,4096]{4,3,2,1,0:T(8,128)(2,1)}, u32[]{:S(2)}) copy-start(bf16[1,1,2,64,4096]{4,3,2,1,0:T(8,128)(2,1)} %param.11) | copy-start | bytes 3145732
  22.2 12.0 %all-to-all-start = ((bf16[8,12,8,128]{3,2,1,0:T(8,128)(2,1)}), bf16[8,12,8,128]{3,2,1,0:T(8,128)(2,1)S(1)}, u32[]{:S(2)}, u32[]{:S(2)}) async-start(bf16[8,12,8,128]{3,2,1,0:T(8,128)(2,1)} %get-tuple-element.44), calls=%async_computation | async-start | bytes 393216 | tf_op jit(solution)/shard_map/all_to_all | solution.py:459
  25.6 11.6 %collective-permute-start.5 = (bf16[8,14,8,128]{3,2,1,0:T(8,128)(2,1)S(1)}, bf16[8,14,8,128]{3,2,1,0:T(8,128)(2,1)S(1)}, u32[]{:S(2)}, u32[]{:S(2)}) collective-permute-start(bf16[8,14,8,128]{3,2,1,0:T(8,128)(2,1)S(1)} %all_to_all.30.refs_9_), channel_id=1, source_target_pairs={{0,24},{8,0},{16,8},{24,16},{1,25},{9,1},{17,9},{25,17},{2,26},{10... | collective-permute-start | bytes 688136 | tf_op jit(solution)/shard_map/ppermute | solution.py:463
  28.1 9.6 %collective-permute-start.4 = (bf16[8,14,8,128]{3,2,1,0:T(8,128)(2,1)S(1)}, bf16[8,14,8,128]{3,2,1,0:T(8,128)(2,1)S(1)}, u32[]{:S(2)}, u32[]{:S(2)}) collective-permute-start(bf16[8,14,8,128]{3,2,1,0:T(8,128)(2,1)S(1)} %all_to_all.30.refs_9_), channel_id=1, source_target_pairs={{0,16},{8,24},{16,0},{24,8},{1,17},{9,25},{17,1},{25,9},{2,18},{10... | collective-permute-start | bytes 688136 | tf_op jit(solution)/shard_map/ppermute | solution.py:463
  28.7 12.8 %collective-permute-start.3 = (bf16[8,14,8,128]{3,2,1,0:T(8,128)(2,1)S(1)}, bf16[8,14,8,128]{3,2,1,0:T(8,128)(2,1)S(1)}, u32[]{:S(2)}, u32[]{:S(2)}) collective-permute-start(bf16[8,14,8,128]{3,2,1,0:T(8,128)(2,1)S(1)} %all_to_all.30.refs_9_), channel_id=1, source_target_pairs={{0,8},{8,16},{16,24},{24,0},{1,9},{9,17},{17,25},{25,1},{2,10},{10... | collective-permute-start | bytes 688136 | tf_op jit(solution)/shard_map/ppermute | solution.py:463
  34.1 18.9 %collective-permute-start.2 = (bf16[8,12,8,128]{3,2,1,0:T(8,128)(2,1)S(1)}, bf16[8,12,8,128]{3,2,1,0:T(8,128)(2,1)S(1)}, u32[]{:S(2)}, u32[]{:S(2)}) collective-permute-start(bf16[8,12,8,128]{3,2,1,0:T(8,128)(2,1)S(1)} %all-to-all-done.refs_7_), channel_id=1, source_target_pairs={{0,24},{8,0},{16,8},{24,16},{1,25},{9,1},{17,9},{25,17},{2,26},{10... | collective-permute-start | bytes 589832 | tf_op jit(solution)/shard_map/ppermute | solution.py:463
  36.6 17.9 %collective-permute-start.1 = (bf16[8,12,8,128]{3,2,1,0:T(8,128)(2,1)S(1)}, bf16[8,12,8,128]{3,2,1,0:T(8,128)(2,1)S(1)}, u32[]{:S(2)}, u32[]{:S(2)}) collective-permute-start(bf16[8,12,8,128]{3,2,1,0:T(8,128)(2,1)S(1)} %all-to-all-done.refs_7_), channel_id=1, source_target_pairs={{0,16},{8,24},{16,0},{24,8},{1,17},{9,25},{17,1},{25,9},{2,18},{10... | collective-permute-start | bytes 589832 | tf_op jit(solution)/shard_map/ppermute | solution.py:463
  37.1 17.4 %collective-permute-start = (bf16[8,12,8,128]{3,2,1,0:T(8,128)(2,1)S(1)}, bf16[8,12,8,128]{3,2,1,0:T(8,128)(2,1)S(1)}, u32[]{:S(2)}, u32[]{:S(2)}) collective-permute-start(bf16[8,12,8,128]{3,2,1,0:T(8,128)(2,1)S(1)} %all-to-all-done.refs_7_), channel_id=1, source_target_pairs={{0,8},{8,16},{16,24},{24,0},{1,9},{9,17},{17,25},{25,1},{2,10},{10... | collective-permute-start | bytes 589832 | tf_op jit(solution)/shard_map/ppermute | solution.py:463
  53.0 15.5 %collective-permute-start.6 = (bf16[8,12,8,128]{3,2,1,0:T(8,128)(2,1)S(1)}, bf16[8,12,8,128]{3,2,1,0:T(8,128)(2,1)S(1)}, u32[]{:S(2)}, u32[]{:S(2)}) collective-permute-start(bf16[8,12,8,128]{3,2,1,0:T(8,128)(2,1)S(1)} %bitcast.35), channel_id=1, source_target_pairs={{0,24},{8,0},{16,8},{24,16},{1,25},{9,1},{17,9},{25,17},{2,26},{10... | collective-permute-start | bytes 589832 | tf_op jit(solution)/shard_map/ppermute | solution.py:463
  53.1 16.3 %collective-permute-start.7 = (bf16[8,12,8,128]{3,2,1,0:T(8,128)(2,1)S(1)}, bf16[8,12,8,128]{3,2,1,0:T(8,128)(2,1)S(1)}, u32[]{:S(2)}, u32[]{:S(2)}) collective-permute-start(bf16[8,12,8,128]{3,2,1,0:T(8,128)(2,1)S(1)} %bitcast.34), channel_id=1, source_target_pairs={{0,16},{8,24},{16,0},{24,8},{1,17},{9,25},{17,1},{25,9},{2,18},{10... | collective-permute-start | bytes 589832 | tf_op jit(solution)/shard_map/ppermute | solution.py:463
  53.1 16.3 %collective-permute-start.8 = (bf16[8,12,8,128]{3,2,1,0:T(8,128)(2,1)S(1)}, bf16[8,12,8,128]{3,2,1,0:T(8,128)(2,1)S(1)}, u32[]{:S(2)}, u32[]{:S(2)}) collective-permute-start(bf16[8,12,8,128]{3,2,1,0:T(8,128)(2,1)S(1)} %bitcast.33), channel_id=1, source_target_pairs={{0,8},{8,16},{16,24},{24,0},{1,9},{9,17},{17,25},{25,1},{2,10},{10... | collective-permute-start | bytes 589832 | tf_op jit(solution)/shard_map/ppermute | solution.py:463
  64.9 14.4 %collective-permute-start.9 = (bf16[8,12,8,128]{3,2,1,0:T(8,128)(2,1)S(1)}, bf16[8,12,8,128]{3,2,1,0:T(8,128)(2,1)S(1)}, u32[]{:S(2)}, u32[]{:S(2)}) collective-permute-start(bf16[8,12,8,128]{3,2,1,0:T(8,128)(2,1)S(1)} %bitcast.38), channel_id=1, source_target_pairs={{0,24},{8,0},{16,8},{24,16},{1,25},{9,1},{17,9},{25,17},{2,26},{10... | collective-permute-start | bytes 589832 | tf_op jit(solution)/shard_map/ppermute | solution.py:463
  67.3 12.0 %collective-permute-start.10 = (bf16[8,12,8,128]{3,2,1,0:T(8,128)(2,1)S(1)}, bf16[8,12,8,128]{3,2,1,0:T(8,128)(2,1)S(1)}, u32[]{:S(2)}, u32[]{:S(2)}) collective-permute-start(bf16[8,12,8,128]{3,2,1,0:T(8,128)(2,1)S(1)} %bitcast.37), channel_id=1, source_target_pairs={{0,16},{8,24},{16,0},{24,8},{1,17},{9,25},{17,1},{25,9},{2,18},{10... | collective-permute-start | bytes 589832 | tf_op jit(solution)/shard_map/ppermute | solution.py:463
  68.5 48.8 %copy-start.15 = (bf16[8,12,8,128]{3,2,1,0:T(8,128)(2,1)}, bf16[8,12,8,128]{3,2,1,0:T(8,128)(2,1)S(1)}, u32[]{:S(2)}) copy-start(bf16[8,12,8,128]{3,2,1,0:T(8,128)(2,1)S(1)} %collective-permute-done.6.refs_1_) | copy-start | bytes 589828
  68.5 10.9 %collective-permute-start.11 = (bf16[8,12,8,128]{3,2,1,0:T(8,128)(2,1)S(1)}, bf16[8,12,8,128]{3,2,1,0:T(8,128)(2,1)S(1)}, u32[]{:S(2)}, u32[]{:S(2)}) collective-permute-start(bf16[8,12,8,128]{3,2,1,0:T(8,128)(2,1)S(1)} %bitcast.36), channel_id=1, source_target_pairs={{0,8},{8,16},{16,24},{24,0},{1,9},{9,17},{17,25},{25,1},{2,10},{10... | collective-permute-start | bytes 589832 | tf_op jit(solution)/shard_map/ppermute | solution.py:463
  69.4 48.0 %copy-start.16 = (bf16[8,12,8,128]{3,2,1,0:T(8,128)(2,1)}, bf16[8,12,8,128]{3,2,1,0:T(8,128)(2,1)S(1)}, u32[]{:S(2)}) copy-start(bf16[8,12,8,128]{3,2,1,0:T(8,128)(2,1)S(1)} %collective-permute-done.7.refs_2_) | copy-start | bytes 589828
  69.4 48.0 %copy-start.17 = (bf16[8,12,8,128]{3,2,1,0:T(8,128)(2,1)}, bf16[8,12,8,128]{3,2,1,0:T(8,128)(2,1)S(1)}, u32[]{:S(2)}) copy-start(bf16[8,12,8,128]{3,2,1,0:T(8,128)(2,1)S(1)} %collective-permute-done.8.refs_3_) | copy-start | bytes 589828
  69.4 18.8 %all-to-all-start.2 = ((bf16[32,8,128]{2,1,0:T(8,128)(2,1)}), bf16[32,8,128]{2,1,0:T(8,128)(2,1)S(1)}, u32[]{:S(2)}, u32[]{:S(2)}) async-start(bf16[32,8,128]{2,1,0:T(8,128)(2,1)} %bitcast.17), calls=%async_computation.2 | async-start | bytes 131072 | tf_op jit(solution)/shard_map/all_to_all | solution.py:459
  79.4 38.0 %copy-start.18 = (bf16[8,12,8,128]{3,2,1,0:T(8,128)(2,1)}, bf16[8,12,8,128]{3,2,1,0:T(8,128)(2,1)S(1)}, u32[]{:S(2)}) copy-start(bf16[8,12,8,128]{3,2,1,0:T(8,128)(2,1)S(1)} %collective-permute-done.9.refs_5_) | copy-start | bytes 589828
  (11 other events, 93.7 us)

commit v4 on v3

--- a/solution.py
+++ b/solution.py
@@ -20,7 +20,7 @@
 bf16 = jnp.bfloat16
 f32 = jnp.float32
 ALL_AXES = ("z", "x", "y", "core")
-WIDE = ("x", "y", "core")
+PLANE = ("x", "y")
 
 HEADS = 4
 HALF_TILES = 3 * HEADS
@@ -46,7 +46,7 @@
     return jnp.where((slot == source) & (row < first + second), 1.0, 0.0)
 
 
-def project_kernel(counts, docs, state, down_t, up, frozen, out_a, out_b):
+def project_kernel(counts, docs, state, down_t, up, frozen, out):
     first, second = counts[0, 0, 0], counts[0, 0, 1]
     low = dot(state[...], down_t[...], ((1,), (1,))).astype(bf16)
     states = (frozen[...].astype(f32) + dot(low, up[...])).astype(bf16)
@@ -72,26 +72,24 @@
     for i, fact in enumerate((first, second, docs[0, 0, 0], docs[0, 0, 1])):
         facts = jnp.where(sub == i, fact.astype(f32), facts)
     halves[0].append(facts)
-    for out, tiles in zip((out_a, out_b), halves):
-        for t, tile in enumerate(tiles):
-            packed = tile.astype(bf16)
-            for z in range(NZ):
-                out[z, t] = packed
+    for t, tile in enumerate(halves[0] + halves[1]):
+        packed = tile.astype(bf16)
+        for z in range(NZ):
+            out[z, t] = packed
 
 
 VMEM = pl.BlockSpec(memory_space=pltpu.VMEM)
 SMEM = pl.BlockSpec(memory_space=pltpu.SMEM)
+SMALL = pltpu.CompilerParams(vmem_limit_bytes=8 * 1024 * 1024)
 
 
 def project(counts, docs, state, down_t, up, frozen):
     return pl.pallas_call(
         project_kernel,
         in_specs=[SMEM] * 2 + [VMEM] * 4,
-        out_specs=[VMEM] * 2,
-        out_shape=[
-            jax.ShapeDtypeStruct((NZ, FACT_TILE + 1, 8, HD), bf16),
-            jax.ShapeDtypeStruct((NZ, HALF_TILES, 8, HD), bf16),
-        ],
+        out_specs=VMEM,
+        out_shape=jax.ShapeDtypeStruct((NZ, FACT_TILE + 1 + HALF_TILES, 8, HD), bf16),
+        compiler_params=SMALL,
         name="project",
     )(counts, docs, state, down_t, up, frozen)
 
@@ -317,7 +315,9 @@
     kept_specs = [pl.BlockSpec(k.shape, lambda g: (0, 0)) for k in kept]
     in_specs = [SMEM] * len(small) + [wide, narrow, narrow, wide, up_key, up_value] + [whole] * NX
     out_specs = [wide, wide, narrow, narrow] + [part] * NX + [up_part] * 2
-    out_shape = [wide_shape] * 2 + [narrow_shape] * 2 + [part_shape] * NX + [up_shape] * 2
+    out_shape = [wide_shape] * 2 + [narrow_shape] * 2
+    out_shape += [pltpu.HBM(part_shape.shape, bf16)] + [part_shape] * (NX - 1)
+    out_shape += [pltpu.HBM(up_shape.shape, f32)] * 2
     scratch, aliases = [], {}
     if half == 0:
         out_specs += kept_specs
@@ -346,10 +346,11 @@
 
 PER_ROW = (MODEL_WIDTH + 2 * KEY_FEATURES) // HD
 CHUNK = 12
-CHUNKS = 8 * PER_ROW // CHUNK
-
-
-def factor_kernel(counts, low_parts, state, key_a, value_a, key_b, value_b, pieces):
+CHUNKS = NX * NY
+HALF = CHUNKS * CHUNK
+
+
+def factor_kernel(place, counts, low_parts, state, key_a, value_a, key_b, value_b, keep, send):
     pick = selection(counts[0, 0, 0], counts[0, 0, 1])
     total = jnp.sum(low_parts[...].astype(f32), axis=0)
     compact = jnp.concatenate([total, pltpu.roll(total, UPDATE_RANK, 1)], axis=0).astype(bf16)
@@ -357,25 +358,31 @@
     down_piece = dot(low_grad, state[...], ((0,), (0,)))
     wide = MODEL_WIDTH // HD
     ups = (key_a, key_b, value_a, value_b)
-    for t in range(8 * PER_ROW):
+
+    def tile(t):
         r, c = divmod(t, PER_ROW)
         rows = slice(r * 8, r * 8 + 8)
         if c < wide:
-            tile = down_piece[rows, c * HD : (c + 1) * HD]
-        else:
-            which, c = divmod(c - wide, HEADS)
-            tile = ups[which][rows, c * HD : (c + 1) * HD]
-        pieces[t // CHUNK, t % CHUNK] = tile.astype(bf16)
-
-
-def factor(counts, low_parts, state, ups):
+            return down_piece[rows, c * HD : (c + 1) * HD]
+        which, c = divmod(c - wide, HEADS)
+        return ups[which][rows, c * HD : (c + 1) * HD]
+
+    lower = place[2] == 0
+    for t in range(HALF):
+        a, b = tile(t), tile(HALF + t)
+        keep[t // CHUNK, t % CHUNK] = jnp.where(lower, a, b).astype(bf16)
+        send[t // CHUNK, t % CHUNK] = jnp.where(lower, b, a).astype(bf16)
+
+
+def factor(place, counts, low_parts, state, ups):
     return pl.pallas_call(
         factor_kernel,
-        in_specs=[SMEM] + [VMEM] * 6,
-        out_specs=VMEM,
-        out_shape=jax.ShapeDtypeStruct((CHUNKS, CHUNK, 8, HD), bf16),
+        in_specs=[SMEM] * 2 + [VMEM] * 6,
+        out_specs=[VMEM] * 2,
+        out_shape=[jax.ShapeDtypeStruct((CHUNKS, CHUNK, 8, HD), bf16)] * 2,
+        compiler_params=SMALL,
         name="factor",
-    )(counts, low_parts, state, *ups)
+    )(place, counts, low_parts, state, *ups)
 
 
 def middle_kernel(pieces, *refs):
@@ -397,6 +404,7 @@
         in_specs=[VMEM] * (1 + len(parts)),
         out_specs=VMEM,
         out_shape=jax.ShapeDtypeStruct((NZ, CHUNK + 2 * HALF_TILES, 8, HD), bf16),
+        compiler_params=SMALL,
         name="middle",
     )(pieces, *parts)
 
@@ -435,24 +443,30 @@
             jax.ShapeDtypeStruct((16, 2 * KEY_FEATURES), bf16),
             jax.ShapeDtypeStruct((CHUNKS, CHUNK, 8, HD), bf16),
         ],
+        compiler_params=SMALL,
         name="close",
     )(counts, parts)
 
 
-def unpack_kernel(tiles, out):
-    for t in range(8 * PER_ROW):
-        r, c = divmod(t, PER_ROW)
-        out[r * 8 : r * 8 + 8, c * HD : (c + 1) * HD] = tiles[t // CHUNK, t % CHUNK].astype(f32)
-
-
-def unpack(tiles):
+def unpack_kernel(place, mine, other, out):
+    lower = place[2] == 0
+    for t in range(HALF):
+        a = mine[t // CHUNK, t % CHUNK].astype(f32)
+        b = other[t // CHUNK, t % CHUNK].astype(f32)
+        for at, tile in ((t, jnp.where(lower, a, b)), (t + HALF, jnp.where(lower, b, a))):
+            r, c = divmod(at, PER_ROW)
+            out[r * 8 : r * 8 + 8, c * HD : (c + 1) * HD] = tile
+
+
+def unpack(place, mine, other):
     return pl.pallas_call(
         unpack_kernel,
-        in_specs=[VMEM],
+        in_specs=[SMEM] + [VMEM] * 2,
         out_specs=VMEM,
         out_shape=jax.ShapeDtypeStruct((UPDATE_RANK, MODEL_WIDTH + 2 * KEY_FEATURES), f32),
+        compiler_params=SMALL,
         name="unpack",
-    )(tiles)
+    )(place, mine, other)
 
 
 def exchange(x, axes):
@@ -461,6 +475,10 @@
 
 def shift(x, by):
     return lax.ppermute(x, "x", [(i, (i + by) % NX) for i in range(NX)])
+
+
+def swap(x):
+    return lax.ppermute(x, "core", [(0, 1), (1, 0)])
 
 
 def spread(column):
@@ -476,16 +494,17 @@
     query, key, value, beacon_slot_state, frozen_beacon_cache, adapter_down_weight,
     adapter_up_weight, output_cotangent, span_beacon_count, span_document, boundary,
 ):
-    place = jnp.stack([lax.axis_index("z"), lax.axis_index("x")]).astype(jnp.int32)
+    place = jnp.stack([lax.axis_index(axis) for axis in ("z", "x", "core")]).astype(jnp.int32)
     state = beacon_slot_state[0, 0].reshape(2 * MAX_BEACONS, MODEL_WIDTH)
     frozen = frozen_beacon_cache[0, 0].reshape(2 * MAX_BEACONS, 2 * KEY_FEATURES)
 
-    message_a, message_b = project(
+    message = project(
         span_beacon_count, span_document, state, adapter_down_weight.T, adapter_up_weight, frozen
     )
     arrays = (query[0, 0], key[0, 0], value[0, 0], output_cotangent[0, 0], adapter_up_weight)
-    boxes_a = spread(exchange(message_a, "z"))
-    boxes_b = spread(exchange(message_b, "z"))
+    column = exchange(message, "z")
+    boxes_a = spread(column[:, : FACT_TILE + 1])
+    boxes_b = spread(column[:, FACT_TILE + 1 :])
     first = attend(0, (place, span_document, boundary), *arrays, boxes_a)
     low_total, bias, low_all = first[10:]
     parts_a = collect(first[4:8])
@@ -495,10 +514,12 @@
     low_part, parts_a = lax.optimization_barrier((second[10], parts_a))
     low_parts = exchange(low_part.reshape(NZ * NX, 8, HD), ("z", "x"))
     low_parts, parts_b = lax.optimization_barrier((low_parts, parts_b))
-    pieces = factor(span_beacon_count, low_parts, state, first[8:10] + second[8:10])
-    both = exchange(middle(exchange(pieces, WIDE), parts_a + parts_b), "z")
+    keep, send = factor(place, span_beacon_count, low_parts, state, first[8:10] + second[8:10])
+    pieces = (keep.astype(f32) + swap(send).astype(f32)).astype(bf16)
+    both = exchange(middle(exchange(pieces, PLANE), parts_a + parts_b), "z")
     cache_gradient, chunk = close(span_beacon_count, both)
-    adapter_gradient = unpack(exchange(chunk, WIDE))
+    mine = exchange(chunk, PLANE)
+    adapter_gradient = unpack(place, mine, swap(mine))
     return (
         attended[None, None],
         grad_query[None, None],

time: 168 us -> 148 us (0.88)
  blocking collectives: 87.2 us -> 67.4 us
  Pallas kernels: 29.5 us -> 23.5 us
  waiting for transfers between devices: 17.3 us -> 21.1 us
  local copies, waits for them, and re-layouts: 5.89 us -> 7.87 us
    all_to_all x4, blocking collectives: 87.2 us -> 67.4 us  [exchange(): return lax.all_to_all(x, axes, 0, 0, tiled=True)]
    ppermute x0 -> x2, starting transfers between devices: none -> 8.07 us  [swap(): return lax.ppermute(x, 'core', [(0, 1), (1, 0)])]
    all_to_all x2 -> x1, starting transfers between devices: 13.4 us -> 5.8 us  [exchange(): return lax.all_to_all(x, axes, 0, 0, tiled=True)]
    ppermute x12, waiting for transfers between devices: 3.7 us -> 9.94 us  [shift(): return lax.ppermute(x, 'x', [(i, (i + by) % NX) for i in range(NX)])]
    all_to_all x2 -> x1, waiting for transfers between devices: 13.6 us -> 8.43 us  [exchange(): return lax.all_to_all(x, axes, 0, 0, tiled=True)]
    ppermute x0 -> x2, waiting for transfers between devices: none -> 2.7 us  [swap(): return lax.ppermute(x, 'core', [(0, 1), (1, 0)])]
    pallas_call x1, Pallas kernels: 2.82 us -> 0.25 us  [middle(): pl.pallas_call(middle_kernel, in_specs=[VMEM] * (1 + len(parts)), out_spe...]
    pallas_call x2, Pallas kernels: 5.11 us -> 3 us  [the longest x1 1.79 us: unpack(): pl.pallas_call(unpack_kernel, in_specs=[SMEM] + [VMEM] * 2, out_specs=VME...]
  transfers between devices with their start and end apart: 14 -> 15, of which waited for: 3 -> 6; matrix products, arithmetic and copies ran while one was open for 0% -> 1% of each run, Pallas kernels for 10% -> 12%
where the time goes in v4:
time: 148 us
  blocking collectives  67.4 us (46%)
  starting transfers between devices  27 us (18%)
  Pallas kernels  23.5 us (16%)
  waiting for transfers between devices  21.1 us (14%)
  local copies, waits for them, and re-layouts  7.87 us (5%)
    all_to_all x4, blocking collectives, exchange(): return lax.all_to_all(x, axes, 0, 0, tiled=True)  67.4 us
    pallas_call x2, Pallas kernels, attend(): pl.pallas_call((first_kernel, second_kernel)[half], grid=(HEADS,), in_spe...  17.6 us
    ppermute x12, starting transfers between devices, shift(): return lax.ppermute(x, 'x', [(i, (i + by) % NX) for i in range(NX)])  13.1 us
    ppermute x12, waiting for transfers between devices, shift(): return lax.ppermute(x, 'x', [(i, (i + by) % NX) for i in range(NX)])  9.94 us
    all_to_all x1, waiting for transfers between devices, exchange(): return lax.all_to_all(x, axes, 0, 0, tiled=True)  8.43 us
    ppermute x2, starting transfers between devices, swap(): return lax.ppermute(x, 'core', [(0, 1), (1, 0)])  8.07 us
    unnamed x48, local copies, waits for them, and re-layouts  6.91 us
    all_to_all x1, starting transfers between devices, exchange(): return lax.all_to_all(x, axes, 0, 0, tiled=True)  5.8 us
  transfers between devices with their start and end apart: 15, of which 6 were waited for; matrix products, arithmetic and copies ran while one was open for 1% of the time, Pallas kernels for 12%

profile of v4, /device:TPU:1, one launch (start us, length us, event | category | flops | bytes accessed | tf_op | source)
XLA Modules:
  0.0 147.8 jit_solution(6501242506301354717)
XLA Ops:
  0.6 1.0 copy-done
  2.6 0.9 copy-done.3
  5.7 1.3 project.1
  7.0 22.7 %all_to_all.25 = bf16[8,26,8,128]{3,2,1,0:T(8,128)(2,1)S(1)} all-to-all(bf16[8,26,8,128]{3,2,1,0:T(8,128)(2,1)S(1)} %project.1), channel_id=1, replica_groups=mesh['z'=8,'x'=4,'y'=4,'core'=2] {'z'}, dimensions={0} | all-to-all | bytes 851968 | tf_op jit(solution)/shard_map/all_to_all | solution.py:473
  29.7 2.6 %collective-permute-start.5 = (bf16[8,14,8,128]{3,2,1,0:T(8,128)(2,1)S(1)}, bf16[8,14,8,128]{3,2,1,0:T(8,128)(2,1)}, u32[]{:S(2)}, u32[]{:S(2)}) collective-permute-start(bf16[8,14,8,128]{3,2,1,0:T(8,128)(2,1)S(1)} %slice.9.refs_9_), channel_id=1, source_target_pairs={{0,24},{8,0},{16,8},{24,16},{1,25},{9,1},{17,9},{25,17},{2,26},{10... | collective-permute-start | bytes 688136 | tf_op jit(solution)/shard_map/ppermute | solution.py:477
  34.5 2.4 %collective-permute-start.2 = (bf16[8,12,8,128]{3,2,1,0:T(8,128)(2,1)S(1)}, bf16[8,12,8,128]{3,2,1,0:T(8,128)(2,1)S(1)}, u32[]{:S(2)}, u32[]{:S(2)}) collective-permute-start(bf16[8,12,8,128]{3,2,1,0:T(8,128)(2,1)S(1)} %slice.8.refs_7_), channel_id=1, source_target_pairs={{0,24},{8,0},{16,8},{24,16},{1,25},{9,1},{17,9},{25,17},{2,26},{10... | collective-permute-start | bytes 589832 | tf_op jit(solution)/shard_map/ppermute | solution.py:477
  37.8 1.0 collective-permute-done.4.refs_11_
  38.8 8.4 %collective-permute-done.3.refs_10_ = bf16[8,14,8,128]{3,2,1,0:T(8,128)(2,1)} collective-permute-done((bf16[8,14,8,128]{3,2,1,0:T(8,128)(2,1)S(1)}, bf16[8,14,8,128]{3,2,1,0:T(8,128)(2,1)}, u32[]{:S(2)}, u32[]{:S(2)}) %collective-permute-start.3) | collective-permute-done | bytes 229408 | tf_op jit(solution)/shard_map/ppermute | solution.py:477
  47.3 9.1 %attend_first.1 = (bf16[2,64,4096]{2,1,0:T(8,128)(2,1)}, bf16[2,64,4096]{2,1,0:T(8,128)(2,1)}, bf16[2,64,1024]{2,1,0:T(8,128)(2,1)}, bf16[2,64,1024]{2,1,0:T(8,1...) custom-call(s32[3]{0:T(128)S(1)} %pad_add_fusion.refs_0_.place, ...), custom_call_target="tpu_custom_call" | custom-call | flops 6000000000 | bytes 4194304 | tf_op jit(solution)/shard_map/attend_first/pallas_call | solution.py:331
  58.1 8.4 %attend_second.1 = (bf16[2,64,4096]{2,1,0:T(8,128)(2,1)}, bf16[2,64,4096]{2,1,0:T(8,128)(2,1)}, bf16[2,64,1024]{2,1,0:T(8,128)(2,1)}, bf16[2,64,1024]{2,1,0:T(8,...) custom-call(s32[3]{0:T(128)S(1)} %pad_add_fusion.refs_0_.place, ...), custom_call_target="tpu_custom_call", output_to_operand_aliasing={{0}: (14, {}), {1}: (15, {}), {2}: (16, {}), {3}: (17, {})} | custom-call | flops 6000000000 | bytes 4194304 | tf_op jit(solution)/shard_map/attend_second/pallas_call | solution.py:331
  66.6 2.4 %collective-permute-start.9 = (bf16[8,12,8,128]{3,2,1,0:T(8,128)(2,1)}, bf16[8,12,8,128]{3,2,1,0:T(8,128)(2,1)S(1)}, u32[]{:S(2)}, u32[]{:S(2)}) collective-permute-start(bf16[8,12,8,128]{3,2,1,0:T(8,128)(2,1)} %bitcast.20), channel_id=1, source_target_pairs={{0,24},{8,0},{16,8},{24,16},{1,25},{9,1},{17,9},{25,17},{2,26},{10... | collective-permute-start | bytes 589832 | tf_op jit(solution)/shard_map/ppermute | solution.py:477
  69.0 1.3 collective-permute-start.10
  71.0 5.8 %all-to-all-start.1 = ((bf16[32,8,128]{2,1,0:T(8,128)(2,1)}), bf16[32,8,128]{2,1,0:T(8,128)(2,1)S(1)}, u32[]{:S(2)}, u32[]{:S(2)}) async-start(bf16[32,8,128]{2,1,0:T(8,128)(2,1)} %bitcast.18), calls=%async_computation.1 | async-start | bytes 131072 | tf_op jit(solution)/shard_map/all_to_all | solution.py:473
  77.3 8.4 %all-to-all-done.1.low_parts = bf16[32,8,128]{2,1,0:T(8,128)(2,1)S(1)} async-done(((bf16[32,8,128]{2,1,0:T(8,128)(2,1)}), bf16[32,8,128]{2,1,0:T(8,128)(2,1)S(1)}, u32[]{:S(2)}, u32[]{:S(2)}) %all-to-all-start.1) | async-done | bytes 65568 | tf_op jit(solution)/shard_map/all_to_all | solution.py:473
  87.6 1.2 factor.1
  88.8 3.8 %collective-permute-start.12 = (bf16[16,12,8,128]{3,2,1,0:T(8,128)(2,1)S(1)}, bf16[16,12,8,128]{3,2,1,0:T(8,128)(2,1)S(1)}, u32[]{:S(2)}, u32[]{:S(2)}) collective-permute-start(bf16[16,12,8,128]{3,2,1,0:T(8,128)(2,1)S(1)} %get-tuple-element.71), channel_id=1, source_target_pairs={{0,1},{1,0},{2,3},{3,2},{4,5},{5,4},{6,7},{7,6},{8,9},{9,8},{10,11... | collective-permute-start | bytes 1179656 | tf_op jit(solution)/shard_map/ppermute | solution.py:481
  92.6 1.3 collective-permute-done.12
  94.0 14.1 %all_to_all.26.pieces = bf16[16,12,8,128]{3,2,1,0:T(8,128)(2,1)S(1)} all-to-all(bf16[16,12,8,128]{3,2,1,0:T(8,128)(2,1)S(1)} %add_convert_fusion), channel_id=1, replica_groups=mesh['z'=8,'x'=4,'y'=4,'core'=2] {'x','y'}, dimensions={0} | all-to-all | bytes 786432 | tf_op jit(solution)/shard_map/all_to_all | solution.py:473
  108.4 19.3 %all_to_all.27.parts = bf16[8,36,8,128]{3,2,1,0:T(8,128)(2,1)S(1)} all-to-all(bf16[8,36,8,128]{3,2,1,0:T(8,128)(2,1)S(1)} %middle.1), channel_id=1, replica_groups=mesh['z'=8,'x'=4,'y'=4,'core'=2] {'z'}, dimensions={0} | all-to-all | bytes 1179648 | tf_op jit(solution)/shard_map/all_to_all | solution.py:473
  127.7 1.4 close.1
  129.0 11.3 %all_to_all.28.mine = bf16[16,12,8,128]{3,2,1,0:T(8,128)(2,1)S(1)} all-to-all(bf16[16,12,8,128]{3,2,1,0:T(8,128)(2,1)S(1)} %get-tuple-element.81), channel_id=1, replica_groups=mesh['z'=8,'x'=4,'y'=4,'core'=2] {'x','y'}, dimensions={0} | all-to-all | bytes 786432 | tf_op jit(solution)/shard_map/all_to_all | solution.py:473
  140.4 4.3 %collective-permute-start.13 = (bf16[16,12,8,128]{3,2,1,0:T(8,128)(2,1)S(1)}, bf16[16,12,8,128]{3,2,1,0:T(8,128)(2,1)S(1)}, u32[]{:S(2)}, u32[]{:S(2)}) collective-permute-start(bf16[16,12,8,128]{3,2,1,0:T(8,128)(2,1)S(1)} %all_to_all.28.mine), channel_id=1, source_target_pairs={{0,1},{1,0},{2,3},{3,2},{4,5},{5,4},{6,7},{7,6},{8,9},{9,8},{10,11... | collective-permute-start | bytes 1179656 | tf_op jit(solution)/shard_map/ppermute | solution.py:481
  144.7 1.3 collective-permute-done.13.other
  146.0 1.8 %unpack.1 = f32[64,6144]{1,0:T(8,128)} custom-call(s32[3]{0:T(128)S(1)} %pad_add_fusion.refs_0_.place, bf16[16,12,8,128]{3,2,1,0:T(8,128)(2,1)S(1)} %all_to_all.28.mine, bf16[16,12,8,128]{3,2,1,0:T(8,128)(2,1)S(1)} %collective-permute-done.13.other), custom_call_target="tpu_custom_call" | custom-call | tf_op jit(solution)/shard_map/unpack/pallas_call | solution.py:462
  (69 shorter events, 11.2 us)
Async XLA Ops:
  5.7 41.6 %copy-start.4 = (bf16[64,2048]{1,0:T(8,128)(2,1)S(1)}, bf16[64,2048]{1,0:T(8,128)(2,1)}, u32[]{:S(2)}) copy-start(bf16[64,2048]{1,0:T(8,128)(2,1)} %refs_6_.1) | copy-start | bytes 786436
  5.7 41.6 %copy-start.15 = (s32[1,1,2]{2,1,0:T(1,128)S(1)}, s32[1,1,2]{2,1,0:T(1,128)}, u32[]{:S(2)}) copy-start(s32[1,1,2]{2,1,0:T(1,128)} %refs_1_.1) | copy-start | bytes 28
  5.7 41.6 %copy-start.16 = (bf16[1,1,2,64,4096]{4,3,2,1,0:T(8,128)(2,1)S(1)}, bf16[1,1,2,64,4096]{4,3,2,1,0:T(8,128)(2,1)}, u32[]{:S(2)}) copy-start(bf16[1,1,2,64,4096]{4,3,2,1,0:T(8,128)(2,1)} %param.11) | copy-start | bytes 3145732
  5.7 41.6 %copy-start.17 = (bf16[1,1,2,64,4096]{4,3,2,1,0:T(8,128)(2,1)S(1)}, bf16[1,1,2,64,4096]{4,3,2,1,0:T(8,128)(2,1)}, u32[]{:S(2)}) copy-start(bf16[1,1,2,64,4096]{4,3,2,1,0:T(8,128)(2,1)} %param.18) | copy-start | bytes 3145732
  5.7 41.6 %copy-start.19 = (bf16[1,1,2,64,1024]{4,3,2,1,0:T(8,128)(2,1)S(1)}, bf16[1,1,2,64,1024]{4,3,2,1,0:T(8,128)(2,1)}, u32[]{:S(2)}) copy-start(bf16[1,1,2,64,1024]{4,3,2,1,0:T(8,128)(2,1)} %param.12) | copy-start | bytes 786436
  5.7 41.6 %copy-start.20 = (bf16[1,1,2,64,1024]{4,3,2,1,0:T(8,128)(2,1)S(1)}, bf16[1,1,2,64,1024]{4,3,2,1,0:T(8,128)(2,1)}, u32[]{:S(2)}) copy-start(bf16[1,1,2,64,1024]{4,3,2,1,0:T(8,128)(2,1)} %param.13) | copy-start | bytes 786436
  5.7 41.6 %copy-start.22 = (s32[1,1,2]{2,1,0:T(1,128)S(1)}, s32[1,1,2]{2,1,0:T(1,128)}, u32[]{:S(2)}) copy-start(s32[1,1,2]{2,1,0:T(1,128)} %refs_2_.1) | copy-start | bytes 28
  29.7 8.1 %collective-permute-start.5 = (bf16[8,14,8,128]{3,2,1,0:T(8,128)(2,1)S(1)}, bf16[8,14,8,128]{3,2,1,0:T(8,128)(2,1)}, u32[]{:S(2)}, u32[]{:S(2)}) collective-permute-start(bf16[8,14,8,128]{3,2,1,0:T(8,128)(2,1)S(1)} %slice.9.refs_9_), channel_id=1, source_target_pairs={{0,24},{8,0},{16,8},{24,16},{1,25},{9,1},{17,9},{25,17},{2,26},{10... | collective-permute-start | bytes 688136 | tf_op jit(solution)/shard_map/ppermute | solution.py:477
  32.2 6.6 %collective-permute-start.4 = (bf16[8,14,8,128]{3,2,1,0:T(8,128)(2,1)S(1)}, bf16[8,14,8,128]{3,2,1,0:T(8,128)(2,1)}, u32[]{:S(2)}, u32[]{:S(2)}) collective-permute-start(bf16[8,14,8,128]{3,2,1,0:T(8,128)(2,1)S(1)} %slice.9.refs_9_), channel_id=1, source_target_pairs={{0,16},{8,24},{16,0},{24,8},{1,17},{9,25},{17,1},{25,9},{2,18},{10... | collective-permute-start | bytes 688136 | tf_op jit(solution)/shard_map/ppermute | solution.py:477
  33.2 14.1 %collective-permute-start.3 = (bf16[8,14,8,128]{3,2,1,0:T(8,128)(2,1)S(1)}, bf16[8,14,8,128]{3,2,1,0:T(8,128)(2,1)}, u32[]{:S(2)}, u32[]{:S(2)}) collective-permute-start(bf16[8,14,8,128]{3,2,1,0:T(8,128)(2,1)S(1)} %slice.9.refs_9_), channel_id=1, source_target_pairs={{0,8},{8,16},{16,24},{24,0},{1,9},{9,17},{17,25},{25,1},{2,10},{10... | collective-permute-start | bytes 688136 | tf_op jit(solution)/shard_map/ppermute | solution.py:477
  34.5 22.8 %collective-permute-start.2 = (bf16[8,12,8,128]{3,2,1,0:T(8,128)(2,1)S(1)}, bf16[8,12,8,128]{3,2,1,0:T(8,128)(2,1)S(1)}, u32[]{:S(2)}, u32[]{:S(2)}) collective-permute-start(bf16[8,12,8,128]{3,2,1,0:T(8,128)(2,1)S(1)} %slice.8.refs_7_), channel_id=1, source_target_pairs={{0,24},{8,0},{16,8},{24,16},{1,25},{9,1},{17,9},{25,17},{2,26},{10... | collective-permute-start | bytes 589832 | tf_op jit(solution)/shard_map/ppermute | solution.py:477
  36.9 21.1 %collective-permute-start.1 = (bf16[8,12,8,128]{3,2,1,0:T(8,128)(2,1)S(1)}, bf16[8,12,8,128]{3,2,1,0:T(8,128)(2,1)S(1)}, u32[]{:S(2)}, u32[]{:S(2)}) collective-permute-start(bf16[8,12,8,128]{3,2,1,0:T(8,128)(2,1)S(1)} %slice.8.refs_7_), channel_id=1, source_target_pairs={{0,16},{8,24},{16,0},{24,8},{1,17},{9,25},{17,1},{25,9},{2,18},{10... | collective-permute-start | bytes 589832 | tf_op jit(solution)/shard_map/ppermute | solution.py:477
  37.8 20.2 %collective-permute-start = (bf16[8,12,8,128]{3,2,1,0:T(8,128)(2,1)S(1)}, bf16[8,12,8,128]{3,2,1,0:T(8,128)(2,1)S(1)}, u32[]{:S(2)}, u32[]{:S(2)}) collective-permute-start(bf16[8,12,8,128]{3,2,1,0:T(8,128)(2,1)S(1)} %slice.8.refs_7_), channel_id=1, source_target_pairs={{0,8},{8,16},{16,24},{24,0},{1,9},{9,17},{17,25},{25,1},{2,10},{10... | collective-permute-start | bytes 589832 | tf_op jit(solution)/shard_map/ppermute | solution.py:477
  56.4 13.8 %collective-permute-start.6 = (bf16[8,12,8,128]{3,2,1,0:T(8,128)(2,1)S(1)}, bf16[8,12,8,128]{3,2,1,0:T(8,128)(2,1)S(1)}, u32[]{:S(2)}, u32[]{:S(2)}) collective-permute-start(bf16[8,12,8,128]{3,2,1,0:T(8,128)(2,1)S(1)} %bitcast.40), channel_id=1, source_target_pairs={{0,24},{8,0},{16,8},{24,16},{1,25},{9,1},{17,9},{25,17},{2,26},{10... | collective-permute-start | bytes 589832 | tf_op jit(solution)/shard_map/ppermute | solution.py:477
  56.5 14.5 %collective-permute-start.7 = (bf16[8,12,8,128]{3,2,1,0:T(8,128)(2,1)S(1)}, bf16[8,12,8,128]{3,2,1,0:T(8,128)(2,1)S(1)}, u32[]{:S(2)}, u32[]{:S(2)}) collective-permute-start(bf16[8,12,8,128]{3,2,1,0:T(8,128)(2,1)S(1)} %bitcast.39), channel_id=1, source_target_pairs={{0,16},{8,24},{16,0},{24,8},{1,17},{9,25},{17,1},{25,9},{2,18},{10... | collective-permute-start | bytes 589832 | tf_op jit(solution)/shard_map/ppermute | solution.py:477
  57.3 13.8 %collective-permute-start.8 = (bf16[8,12,8,128]{3,2,1,0:T(8,128)(2,1)S(1)}, bf16[8,12,8,128]{3,2,1,0:T(8,128)(2,1)S(1)}, u32[]{:S(2)}, u32[]{:S(2)}) collective-permute-start(bf16[8,12,8,128]{3,2,1,0:T(8,128)(2,1)S(1)} %bitcast.38), channel_id=1, source_target_pairs={{0,8},{8,16},{16,24},{24,0},{1,9},{9,17},{17,25},{25,1},{2,10},{10... | collective-permute-start | bytes 589832 | tf_op jit(solution)/shard_map/ppermute | solution.py:477
  66.5 41.6 %copy-start.5 = (bf16[8,3,4,8,128]{4,3,2,1,0:T(8,128)(2,1)S(1)}, bf16[8,3,4,8,128]{4,3,2,1,0:T(8,128)(2,1)}, u32[]{:S(2)}) copy-start(bf16[8,3,4,8,128]{4,3,2,1,0:T(8,128)(2,1)} %get-tuple-element.56) | copy-start | bytes 589828
  66.5 41.6 %copy-start.6 = (bf16[8,3,4,8,128]{4,3,2,1,0:T(8,128)(2,1)S(1)}, bf16[8,3,4,8,128]{4,3,2,1,0:T(8,128)(2,1)}, u32[]{:S(2)}) copy-start(bf16[8,3,4,8,128]{4,3,2,1,0:T(8,128)(2,1)} %get-tuple-element.61) | copy-start | bytes 589828
  66.6 10.3 %collective-permute-start.9 = (bf16[8,12,8,128]{3,2,1,0:T(8,128)(2,1)}, bf16[8,12,8,128]{3,2,1,0:T(8,128)(2,1)S(1)}, u32[]{:S(2)}, u32[]{:S(2)}) collective-permute-start(bf16[8,12,8,128]{3,2,1,0:T(8,128)(2,1)} %bitcast.20), channel_id=1, source_target_pairs={{0,24},{8,0},{16,8},{24,16},{1,25},{9,1},{17,9},{25,17},{2,26},{10... | collective-permute-start | bytes 589832 | tf_op jit(solution)/shard_map/ppermute | solution.py:477
  69.0 7.9 %collective-permute-start.10 = (bf16[8,12,8,128]{3,2,1,0:T(8,128)(2,1)}, bf16[8,12,8,128]{3,2,1,0:T(8,128)(2,1)S(1)}, u32[]{:S(2)}, u32[]{:S(2)}) collective-permute-start(bf16[8,12,8,128]{3,2,1,0:T(8,128)(2,1)} %bitcast.21), channel_id=1, source_target_pairs={{0,16},{8,24},{16,0},{24,8},{1,17},{9,25},{17,1},{25,9},{2,18},{10... | collective-permute-start | bytes 589832 | tf_op jit(solution)/shard_map/ppermute | solution.py:477
  70.3 7.1 %collective-permute-start.11 = (bf16[8,12,8,128]{3,2,1,0:T(8,128)(2,1)S(1)}, bf16[8,12,8,128]{3,2,1,0:T(8,128)(2,1)S(1)}, u32[]{:S(2)}, u32[]{:S(2)}) collective-permute-start(bf16[8,12,8,128]{3,2,1,0:T(8,128)(2,1)S(1)} %bitcast.41), channel_id=1, source_target_pairs={{0,8},{8,16},{16,24},{24,0},{1,9},{9,17},{17,25},{25,1},{2,10},{10... | collective-permute-start | bytes 589832 | tf_op jit(solution)/shard_map/ppermute | solution.py:477
  71.0 14.7 %all-to-all-start.1 = ((bf16[32,8,128]{2,1,0:T(8,128)(2,1)}), bf16[32,8,128]{2,1,0:T(8,128)(2,1)S(1)}, u32[]{:S(2)}, u32[]{:S(2)}) async-start(bf16[32,8,128]{2,1,0:T(8,128)(2,1)} %bitcast.18), calls=%async_computation.1 | async-start | bytes 131072 | tf_op jit(solution)/shard_map/all_to_all | solution.py:473
  88.8 5.1 %collective-permute-start.12 = (bf16[16,12,8,128]{3,2,1,0:T(8,128)(2,1)S(1)}, bf16[16,12,8,128]{3,2,1,0:T(8,128)(2,1)S(1)}, u32[]{:S(2)}, u32[]{:S(2)}) collective-permute-start(bf16[16,12,8,128]{3,2,1,0:T(8,128)(2,1)S(1)} %get-tuple-element.71), channel_id=1, source_target_pairs={{0,1},{1,0},{2,3},{3,2},{4,5},{5,4},{6,7},{7,6},{8,9},{9,8},{10,11... | collective-permute-start | bytes 1179656 | tf_op jit(solution)/shard_map/ppermute | solution.py:481
  140.4 5.6 %collective-permute-start.13 = (bf16[16,12,8,128]{3,2,1,0:T(8,128)(2,1)S(1)}, bf16[16,12,8,128]{3,2,1,0:T(8,128)(2,1)S(1)}, u32[]{:S(2)}, u32[]{:S(2)}) collective-permute-start(bf16[16,12,8,128]{3,2,1,0:T(8,128)(2,1)S(1)} %all_to_all.28.mine), channel_id=1, source_target_pairs={{0,1},{1,0},{2,3},{3,2},{4,5},{5,4},{6,7},{7,6},{8,9},{9,8},{10,11... | collective-permute-start | bytes 1179656 | tf_op jit(solution)/shard_map/ppermute | solution.py:481
  (15 other events, 141.7 us)

commit v5 on v4

--- a/solution.py
+++ b/solution.py
@@ -25,7 +25,6 @@
 HEADS = 4
 HALF_TILES = 3 * HEADS
 LOW_TILE = HALF_TILES
-FACT_TILE = HALF_TILES + 1
 FAR = 384
 NEAR = 128
 KEYS = FAR + NEAR
@@ -67,11 +66,11 @@
     put_col = lax.broadcasted_iota(jnp.int32, (UPDATE_RANK, HD), 1)
     left = jnp.where(put_row == put_col, 1.0, 0.0).astype(bf16)
     right = jnp.where(put_row + UPDATE_RANK == put_col, 1.0, 0.0).astype(bf16)
-    halves[0].append(dot(low_rows, left)[:8] + dot(low_rows, right)[8:])
-    facts = jnp.zeros((8, HD), f32)
+    extra = dot(low_rows, left)[:8] + dot(low_rows, right)[8:]
+    side = lax.broadcasted_iota(jnp.int32, (8, HD), 1) >= UPDATE_RANK
     for i, fact in enumerate((first, second, docs[0, 0, 0], docs[0, 0, 1])):
-        facts = jnp.where(sub == i, fact.astype(f32), facts)
-    halves[0].append(facts)
+        extra = jnp.where(side & (sub == 4 + i), fact.astype(f32), extra)
+    halves[0].append(extra)
     for t, tile in enumerate(halves[0] + halves[1]):
         packed = tile.astype(bf16)
         for z in range(NZ):
@@ -88,8 +87,7 @@
         project_kernel,
         in_specs=[SMEM] * 2 + [VMEM] * 4,
         out_specs=VMEM,
-        out_shape=jax.ShapeDtypeStruct((NZ, FACT_TILE + 1 + HALF_TILES, 8, HD), bf16),
-        compiler_params=SMALL,
+        out_shape=jax.ShapeDtypeStruct((NZ, LOW_TILE + 1 + HALF_TILES, 8, HD), bf16),
         name="project",
     )(counts, docs, state, down_t, up, frozen)
 
@@ -112,9 +110,10 @@
         bias[block * 8 : block * 8 + 8, :] = jnp.where(seen, 0.0, MASKED)
 
     def facts(box, z, slot):
-        tile = boxes[box][z, FACT_TILE].astype(f32)
-        first, second = tile[0:1], tile[1:2]
-        first_doc, second_doc = tile[2:3], tile[3:4]
+        tile = boxes[box][z, LOW_TILE].astype(f32)
+        tile = jnp.where(lane < UPDATE_RANK, pltpu.roll(tile, UPDATE_RANK, 1), tile)
+        first, second = tile[4:5], tile[5:6]
+        first_doc, second_doc = tile[6:7], tile[7:8]
         source = z * NX + lax.rem(x_own - box + NX, NX)
         low = slot < first
         high = slot < first + second
@@ -141,17 +140,18 @@
 
 
 def gather_low(boxes, low_all):
+    rows = [None] * (2 * NX)
     lane = lax.broadcasted_iota(jnp.int32, (NZ, 8, HD), 2)
     sub = lax.broadcasted_iota(jnp.int32, (NZ // 2, 8, HD), 1)
     for b, box in enumerate(boxes):
         tile = box[:, LOW_TILE].astype(f32)
         head = jnp.where(lane < UPDATE_RANK, tile, 0.0)
-        low_all[b * 64 : b * 64 + 64, :] = head.reshape(64, HD).astype(bf16)
+        rows[b] = head.reshape(64, HD)
         tail = jnp.where(lane < UPDATE_RANK, pltpu.roll(tile, UPDATE_RANK, 2), 0.0)
         tail = tail.reshape(NZ // 2, 2, 8, HD)
         tail = jnp.where(sub < 4, tail[:, 0], pltpu.roll(tail[:, 1], 4, 1))
-        at = 256 + b * 32
-        low_all[at : at + 32, :] = tail.reshape(32, HD).astype(bf16)
+        rows[NX + b] = tail.reshape(32, HD)
+    low_all[...] = jnp.concatenate(rows, axis=0).T[:UPDATE_RANK].astype(bf16)
 
 
 def attend_kernel(
@@ -196,13 +196,13 @@
     values = jnp.concatenate(
         [value[...].reshape(NEAR, HD).astype(f32)] + far_rows(HEADS + g) + extra_values, axis=0
     )
-    keys_t = keys.T.astype(bf16)
-    values_t = values.T.astype(bf16)
     keys = keys.astype(bf16)
     values = values.astype(bf16)
+    keys_t = keys.T
+    values_t = values.T
     queries = stack(query)
     grads = stack(grad)
-    grads_t = grads.astype(f32).T
+    grads_t = grads.T
 
     scores = dot(keys, queries, ((1,), (1,))) * (SCORE_SCALE * LOG2E)
     scores = scores + jnp.tile(bias[...], (1, GROUP))
@@ -212,12 +212,12 @@
     exact = weights * (1.0 / total)
     probs = exact.astype(bf16)
     summed_t = dot(values_t, probs)
-    summed = summed_t.T.astype(bf16)
-    rounded_t = summed_t.astype(bf16).astype(f32)
-    delta = jnp.sum(grads_t * rounded_t, axis=0, keepdims=True)
-    grad_probs = dot(values, grads_t.astype(bf16))
+    rounded_t = summed_t.astype(bf16)
+    summed = rounded_t.T
+    delta = jnp.sum(grads_t.astype(f32) * rounded_t.astype(f32), axis=0, keepdims=True)
+    grad_probs = dot(values, grads_t)
     grad_scores = (exact * (grad_probs - delta)).astype(bf16)
-    query_grad = (dot(keys_t, grad_scores) * SCORE_SCALE).T.astype(bf16)
+    query_grad = (dot(keys_t, grad_scores) * SCORE_SCALE).astype(bf16).T
     key_grad = dot(grad_scores, queries) * SCORE_SCALE
     value_grad = dot(probs, grads)
 
@@ -243,14 +243,12 @@
 
     far_keys = key_grad[NEAR:].astype(bf16)
     far_values = value_grad[NEAR:].astype(bf16)
-    up_key_part[...] = dot(low_all[...], far_keys, ((0,), (0,)))[:UPDATE_RANK]
-    up_value_part[...] = dot(low_all[...], far_values, ((0,), (0,)))[:UPDATE_RANK]
-
-    def twice(ref):
-        return jnp.concatenate([ref[...], ref[...]], axis=0)
-
-    low_total[...] += dot(far_keys, twice(up_key), ((1,), (1,)))
-    low_total[...] += dot(far_values, twice(up_value), ((1,), (1,)))
+    far = jnp.concatenate([far_keys, far_values], axis=1)
+    up_part = dot(low_all[...], far)
+    up_key_part[...] = up_part[:, :HD]
+    up_value_part[...] = up_part[:, HD:]
+    up_both = jnp.concatenate([up_key[...], up_value[...]], axis=1)
+    low_total[...] += dot(far, jnp.concatenate([up_both, up_both], axis=0), ((1,), (1,)))
 
     if not last:
         return
@@ -310,14 +308,13 @@
     kept = [
         jax.ShapeDtypeStruct((FAR, HD), f32),
         jax.ShapeDtypeStruct((KEYS, NEAR), f32),
-        jax.ShapeDtypeStruct((FAR, HD), bf16),
+        jax.ShapeDtypeStruct((UPDATE_RANK, FAR), bf16),
     ]
     kept_specs = [pl.BlockSpec(k.shape, lambda g: (0, 0)) for k in kept]
     in_specs = [SMEM] * len(small) + [wide, narrow, narrow, wide, up_key, up_value] + [whole] * NX
     out_specs = [wide, wide, narrow, narrow] + [part] * NX + [up_part] * 2
     out_shape = [wide_shape] * 2 + [narrow_shape] * 2
-    out_shape += [pltpu.HBM(part_shape.shape, bf16)] + [part_shape] * (NX - 1)
-    out_shape += [pltpu.HBM(up_shape.shape, f32)] * 2
+    out_shape += [part_shape] * NX + [up_shape] * 2
     scratch, aliases = [], {}
     if half == 0:
         out_specs += kept_specs
@@ -503,8 +500,8 @@
     )
     arrays = (query[0, 0], key[0, 0], value[0, 0], output_cotangent[0, 0], adapter_up_weight)
     column = exchange(message, "z")
-    boxes_a = spread(column[:, : FACT_TILE + 1])
-    boxes_b = spread(column[:, FACT_TILE + 1 :])
+    boxes_a = spread(column[:, : LOW_TILE + 1])
+    boxes_b = spread(column[:, LOW_TILE + 1 :])
     first = attend(0, (place, span_document, boundary), *arrays, boxes_a)
     low_total, bias, low_all = first[10:]
     parts_a = collect(first[4:8])

time: 148 us -> 143 us (0.966)
  local copies, waits for them, and re-layouts: 7.87 us -> 3.84 us
    unnamed x48 -> x28, local copies, waits for them, and re-layouts: 6.91 us -> 2.89 us
    pallas_call x2, Pallas kernels: 17.6 us -> 15.7 us  [attend(): pl.pallas_call((first_kernel, second_kernel)[half], grid=(HEADS,), in_spe...]
    pallas_call x1, Pallas kernels: 1.27 us -> 2.78 us  [project(): pl.pallas_call(project_kernel, in_specs=[SMEM] * 2 + [VMEM] * 4, out_spec...]
  transfers between devices with their start and end apart: 15 -> 15, of which waited for: 6 -> 6; matrix products, arithmetic and copies ran while one was open for 1% -> 1% of each run, Pallas kernels for 12% -> 11%
where the time goes in v5:
time: 143 us
  blocking collectives  67.5 us (47%)
  starting transfers between devices  27.1 us (19%)
  Pallas kernels  23.2 us (16%)
  waiting for transfers between devices  20.1 us (14%)
  local copies, waits for them, and re-layouts  3.84 us (3%)
    all_to_all x4, blocking collectives, exchange(): return lax.all_to_all(x, axes, 0, 0, tiled=True)  67.5 us
    pallas_call x2, Pallas kernels, attend(): pl.pallas_call((first_kernel, second_kernel)[half], grid=(HEADS,), in_spe...  15.7 us
    ppermute x12, starting transfers between devices, shift(): return lax.ppermute(x, 'x', [(i, (i + by) % NX) for i in range(NX)])  13.1 us
    ppermute x12, waiting for transfers between devices, shift(): return lax.ppermute(x, 'x', [(i, (i + by) % NX) for i in range(NX)])  9.32 us
    ppermute x2, starting transfers between devices, swap(): return lax.ppermute(x, 'core', [(0, 1), (1, 0)])  8.51 us
    all_to_all x1, waiting for transfers between devices, exchange(): return lax.all_to_all(x, axes, 0, 0, tiled=True)  8.1 us
    all_to_all x1, starting transfers between devices, exchange(): return lax.all_to_all(x, axes, 0, 0, tiled=True)  5.57 us
    unnamed x28, local copies, waits for them, and re-layouts  2.89 us
  transfers between devices with their start and end apart: 15, of which 6 were waited for; matrix products, arithmetic and copies ran while one was open for 1% of the time, Pallas kernels for 11%

profile of v5, /device:TPU:1, one launch (start us, length us, event | category | flops | bytes accessed | tf_op | source)
XLA Modules:
  0.0 142.7 jit_solution(3351340531119583387)
XLA Ops:
  0.7 2.8 %project.1 = bf16[8,25,8,128]{3,2,1,0:T(8,128)(2,1)} custom-call(s32[1,1,2]{2,1,0:T(1,128)} %counts.5, s32[1,1,2]{2,1,0:T(1,128)} %refs_1_.1, bf16[16,4096]{1,0:T(8,128)(2,1)} %bitcast.24, bf16[64,4096]{1,0:T(8,128)(2,1)} %bitcast.39, bf16[64,2048]{1,0:T(8,128)(2,1)} %refs_6_.1, bf16[16,2048]{1,0:T(8,128)(2,1)} %bitcast.40), custom_call_target="tpu_custom_call" | custom-call | tf_op jit(solution)/shard_map/project/pallas_call | solution.py:86
  3.5 22.8 %all_to_all.25 = bf16[8,25,8,128]{3,2,1,0:T(8,128)(2,1)S(1)} all-to-all(bf16[8,25,8,128]{3,2,1,0:T(8,128)(2,1)} %project.1), channel_id=1, replica_groups=mesh['z'=8,'x'=4,'y'=4,'core'=2] {'z'}, dimensions={0} | all-to-all | bytes 819200 | tf_op jit(solution)/shard_map/all_to_all | solution.py:470
  26.3 2.6 %collective-permute-start.5 = (bf16[8,13,8,128]{3,2,1,0:T(8,128)(2,1)S(1)}, bf16[8,13,8,128]{3,2,1,0:T(8,128)(2,1)S(1)}, u32[]{:S(2)}, u32[]{:S(2)}) collective-permute-start(bf16[8,13,8,128]{3,2,1,0:T(8,128)(2,1)S(1)} %slice.9.refs_9_), channel_id=1, source_target_pairs={{0,24},{8,0},{16,8},{24,16},{1,25},{9,1},{17,9},{25,17},{2,26},{10... | collective-permute-start | bytes 638984 | tf_op jit(solution)/shard_map/ppermute | solution.py:474
  30.1 0.9 slice.8.refs_7_
  31.1 2.4 %collective-permute-start.2 = (bf16[8,12,8,128]{3,2,1,0:T(8,128)(2,1)S(1)}, bf16[8,12,8,128]{3,2,1,0:T(8,128)(2,1)S(1)}, u32[]{:S(2)}, u32[]{:S(2)}) collective-permute-start(bf16[8,12,8,128]{3,2,1,0:T(8,128)(2,1)S(1)} %slice.8.refs_7_), channel_id=1, source_target_pairs={{0,24},{8,0},{16,8},{24,16},{1,25},{9,1},{17,9},{25,17},{2,26},{10... | collective-permute-start | bytes 589832 | tf_op jit(solution)/shard_map/ppermute | solution.py:474
  35.1 7.8 %collective-permute-done.3.refs_10_ = bf16[8,13,8,128]{3,2,1,0:T(8,128)(2,1)S(1)} collective-permute-done((bf16[8,13,8,128]{3,2,1,0:T(8,128)(2,1)S(1)}, bf16[8,13,8,128]{3,2,1,0:T(8,128)(2,1)S(1)}, u32[]{:S(2)}, u32[]{:S(2)}) %collective-permute-start.3) | collective-permute-done | bytes 213024 | tf_op jit(solution)/shard_map/ppermute | solution.py:474
  43.7 1.2 copy-done.5
  44.9 0.9 copy-done.11
  45.9 7.9 %attend_first.1 = (bf16[2,64,4096]{2,1,0:T(8,128)(2,1)}, bf16[2,64,4096]{2,1,0:T(8,128)(2,1)}, bf16[2,64,1024]{2,1,0:T(8,128)(2,1)}, bf16[2,64,1024]{2,1,0:T(8,1...) custom-call(s32[3]{0:T(128)S(1)} %pad_add_fusion.refs_0_.place, ...), custom_call_target="tpu_custom_call" | custom-call | flops 6000000000 | bytes 4194304 | tf_op jit(solution)/shard_map/attend_first/pallas_call | solution.py:328
  55.4 7.8 %attend_second.1 = (bf16[2,64,4096]{2,1,0:T(8,128)(2,1)}, bf16[2,64,4096]{2,1,0:T(8,128)(2,1)}, bf16[2,64,1024]{2,1,0:T(8,128)(2,1)}, bf16[2,64,1024]{2,1,0:T(8,...) custom-call(s32[3]{0:T(128)S(1)} %pad_add_fusion.refs_0_.place, ...), custom_call_target="tpu_custom_call", output_to_operand_aliasing={{0}: (14, {}), {1}: (15, {}), {2}: (16, {}), {3}: (17, {})} | custom-call | flops 6000000000 | bytes 4194304 | tf_op jit(solution)/shard_map/attend_second/pallas_call | solution.py:328
  63.2 2.4 %collective-permute-start.9 = (bf16[8,12,8,128]{3,2,1,0:T(8,128)(2,1)}, bf16[8,12,8,128]{3,2,1,0:T(8,128)(2,1)S(1)}, u32[]{:S(2)}, u32[]{:S(2)}) collective-permute-start(bf16[8,12,8,128]{3,2,1,0:T(8,128)(2,1)} %bitcast.20), channel_id=1, source_target_pairs={{0,24},{8,0},{16,8},{24,16},{1,25},{9,1},{17,9},{25,17},{2,26},{10... | collective-permute-start | bytes 589832 | tf_op jit(solution)/shard_map/ppermute | solution.py:474
  65.6 1.3 collective-permute-start.10
  67.7 5.6 %all-to-all-start.1 = ((bf16[32,8,128]{2,1,0:T(8,128)(2,1)}), bf16[32,8,128]{2,1,0:T(8,128)(2,1)S(1)}, u32[]{:S(2)}, u32[]{:S(2)}) async-start(bf16[32,8,128]{2,1,0:T(8,128)(2,1)} %bitcast.18), calls=%async_computation.1 | async-start | bytes 131072 | tf_op jit(solution)/shard_map/all_to_all | solution.py:470
  74.0 8.1 %all-to-all-done.1.low_parts = bf16[32,8,128]{2,1,0:T(8,128)(2,1)S(1)} async-done(((bf16[32,8,128]{2,1,0:T(8,128)(2,1)}), bf16[32,8,128]{2,1,0:T(8,128)(2,1)S(1)}, u32[]{:S(2)}, u32[]{:S(2)}) %all-to-all-start.1) | async-done | bytes 65568 | tf_op jit(solution)/shard_map/all_to_all | solution.py:470
  82.1 1.2 factor.1
  83.3 4.2 %collective-permute-start.12 = (bf16[16,12,8,128]{3,2,1,0:T(8,128)(2,1)S(1)}, bf16[16,12,8,128]{3,2,1,0:T(8,128)(2,1)S(1)}, u32[]{:S(2)}, u32[]{:S(2)}) collective-permute-start(bf16[16,12,8,128]{3,2,1,0:T(8,128)(2,1)S(1)} %get-tuple-element.71), channel_id=1, source_target_pairs={{0,1},{1,0},{2,3},{3,2},{4,5},{5,4},{6,7},{7,6},{8,9},{9,8},{10,11... | collective-permute-start | bytes 1179656 | tf_op jit(solution)/shard_map/ppermute | solution.py:478
  87.5 1.3 collective-permute-done.12
  88.9 14.1 %all_to_all.26.pieces = bf16[16,12,8,128]{3,2,1,0:T(8,128)(2,1)S(1)} all-to-all(bf16[16,12,8,128]{3,2,1,0:T(8,128)(2,1)S(1)} %add_convert_fusion), channel_id=1, replica_groups=mesh['z'=8,'x'=4,'y'=4,'core'=2] {'x','y'}, dimensions={0} | all-to-all | bytes 786432 | tf_op jit(solution)/shard_map/all_to_all | solution.py:470
  103.3 19.3 %all_to_all.27.parts = bf16[8,36,8,128]{3,2,1,0:T(8,128)(2,1)S(1)} all-to-all(bf16[8,36,8,128]{3,2,1,0:T(8,128)(2,1)S(1)} %middle.1), channel_id=1, replica_groups=mesh['z'=8,'x'=4,'y'=4,'core'=2] {'z'}, dimensions={0} | all-to-all | bytes 1179648 | tf_op jit(solution)/shard_map/all_to_all | solution.py:470
  122.6 1.4 close.1
  124.0 11.3 %all_to_all.28.mine = bf16[16,12,8,128]{3,2,1,0:T(8,128)(2,1)S(1)} all-to-all(bf16[16,12,8,128]{3,2,1,0:T(8,128)(2,1)S(1)} %get-tuple-element.81), channel_id=1, replica_groups=mesh['z'=8,'x'=4,'y'=4,'core'=2] {'x','y'}, dimensions={0} | all-to-all | bytes 786432 | tf_op jit(solution)/shard_map/all_to_all | solution.py:470
  135.3 4.3 %collective-permute-start.13 = (bf16[16,12,8,128]{3,2,1,0:T(8,128)(2,1)S(1)}, bf16[16,12,8,128]{3,2,1,0:T(8,128)(2,1)S(1)}, u32[]{:S(2)}, u32[]{:S(2)}) collective-permute-start(bf16[16,12,8,128]{3,2,1,0:T(8,128)(2,1)S(1)} %all_to_all.28.mine), channel_id=1, source_target_pairs={{0,1},{1,0},{2,3},{3,2},{4,5},{5,4},{6,7},{7,6},{8,9},{9,8},{10,11... | collective-permute-start | bytes 1179656 | tf_op jit(solution)/shard_map/ppermute | solution.py:478
  139.6 1.3 collective-permute-done.13.other
  140.9 1.8 %unpack.1 = f32[64,6144]{1,0:T(8,128)} custom-call(s32[3]{0:T(128)S(1)} %pad_add_fusion.refs_0_.place, bf16[16,12,8,128]{3,2,1,0:T(8,128)(2,1)S(1)} %all_to_all.28.mine, bf16[16,12,8,128]{3,2,1,0:T(8,128)(2,1)S(1)} %collective-permute-done.13.other), custom_call_target="tpu_custom_call" | custom-call | tf_op jit(solution)/shard_map/unpack/pallas_call | solution.py:459
  (49 shorter events, 7.1 us)
Async XLA Ops:
  0.6 43.0 %copy-start.1 = (bf16[64,2048]{1,0:T(8,128)(2,1)S(1)}, bf16[64,2048]{1,0:T(8,128)(2,1)}, u32[]{:S(2)}) copy-start(bf16[64,2048]{1,0:T(8,128)(2,1)} %refs_6_.1) | copy-start | bytes 786436
  0.6 43.0 %copy-start.3 = (s32[1,1,2]{2,1,0:T(1,128)S(1)}, s32[1,1,2]{2,1,0:T(1,128)}, u32[]{:S(2)}) copy-start(s32[1,1,2]{2,1,0:T(1,128)} %refs_1_.1) | copy-start | bytes 28
  0.7 43.0 %copy-start.12 = (s32[1,1,2]{2,1,0:T(1,128)S(1)}, s32[1,1,2]{2,1,0:T(1,128)}, u32[]{:S(2)}) copy-start(s32[1,1,2]{2,1,0:T(1,128)} %refs_2_.1) | copy-start | bytes 28
  0.7 43.0 %copy-start.8 = (bf16[1,1,2,64,1024]{4,3,2,1,0:T(8,128)(2,1)S(1)}, bf16[1,1,2,64,1024]{4,3,2,1,0:T(8,128)(2,1)}, u32[]{:S(2)}) copy-start(bf16[1,1,2,64,1024]{4,3,2,1,0:T(8,128)(2,1)} %param.13) | copy-start | bytes 786436
  0.7 43.0 %copy-start.7 = (bf16[1,1,2,64,1024]{4,3,2,1,0:T(8,128)(2,1)S(1)}, bf16[1,1,2,64,1024]{4,3,2,1,0:T(8,128)(2,1)}, u32[]{:S(2)}) copy-start(bf16[1,1,2,64,1024]{4,3,2,1,0:T(8,128)(2,1)} %param.12) | copy-start | bytes 786436
  0.7 43.0 %copy-start.4 = (bf16[1,1,2,64,4096]{4,3,2,1,0:T(8,128)(2,1)S(1)}, bf16[1,1,2,64,4096]{4,3,2,1,0:T(8,128)(2,1)}, u32[]{:S(2)}) copy-start(bf16[1,1,2,64,4096]{4,3,2,1,0:T(8,128)(2,1)} %param.11) | copy-start | bytes 3145732
  26.3 8.1 %collective-permute-start.5 = (bf16[8,13,8,128]{3,2,1,0:T(8,128)(2,1)S(1)}, bf16[8,13,8,128]{3,2,1,0:T(8,128)(2,1)S(1)}, u32[]{:S(2)}, u32[]{:S(2)}) collective-permute-start(bf16[8,13,8,128]{3,2,1,0:T(8,128)(2,1)S(1)} %slice.9.refs_9_), channel_id=1, source_target_pairs={{0,24},{8,0},{16,8},{24,16},{1,25},{9,1},{17,9},{25,17},{2,26},{10... | collective-permute-start | bytes 638984 | tf_op jit(solution)/shard_map/ppermute | solution.py:474
  28.8 6.3 %collective-permute-start.4 = (bf16[8,13,8,128]{3,2,1,0:T(8,128)(2,1)S(1)}, bf16[8,13,8,128]{3,2,1,0:T(8,128)(2,1)S(1)}, u32[]{:S(2)}, u32[]{:S(2)}) collective-permute-start(bf16[8,13,8,128]{3,2,1,0:T(8,128)(2,1)S(1)} %slice.9.refs_9_), channel_id=1, source_target_pairs={{0,16},{8,24},{16,0},{24,8},{1,17},{9,25},{17,1},{25,9},{2,18},{10... | collective-permute-start | bytes 638984 | tf_op jit(solution)/shard_map/ppermute | solution.py:474
  29.8 13.2 %collective-permute-start.3 = (bf16[8,13,8,128]{3,2,1,0:T(8,128)(2,1)S(1)}, bf16[8,13,8,128]{3,2,1,0:T(8,128)(2,1)S(1)}, u32[]{:S(2)}, u32[]{:S(2)}) collective-permute-start(bf16[8,13,8,128]{3,2,1,0:T(8,128)(2,1)S(1)} %slice.9.refs_9_), channel_id=1, source_target_pairs={{0,8},{8,16},{16,24},{24,0},{1,9},{9,17},{17,25},{25,1},{2,10},{10... | collective-permute-start | bytes 638984 | tf_op jit(solution)/shard_map/ppermute | solution.py:474
  31.1 23.5 %collective-permute-start.2 = (bf16[8,12,8,128]{3,2,1,0:T(8,128)(2,1)S(1)}, bf16[8,12,8,128]{3,2,1,0:T(8,128)(2,1)S(1)}, u32[]{:S(2)}, u32[]{:S(2)}) collective-permute-start(bf16[8,12,8,128]{3,2,1,0:T(8,128)(2,1)S(1)} %slice.8.refs_7_), channel_id=1, source_target_pairs={{0,24},{8,0},{16,8},{24,16},{1,25},{9,1},{17,9},{25,17},{2,26},{10... | collective-permute-start | bytes 589832 | tf_op jit(solution)/shard_map/ppermute | solution.py:474
  33.5 21.8 %collective-permute-start.1 = (bf16[8,12,8,128]{3,2,1,0:T(8,128)(2,1)S(1)}, bf16[8,12,8,128]{3,2,1,0:T(8,128)(2,1)S(1)}, u32[]{:S(2)}, u32[]{:S(2)}) collective-permute-start(bf16[8,12,8,128]{3,2,1,0:T(8,128)(2,1)S(1)} %slice.8.refs_7_), channel_id=1, source_target_pairs={{0,16},{8,24},{16,0},{24,8},{1,17},{9,25},{17,1},{25,9},{2,18},{10... | collective-permute-start | bytes 589832 | tf_op jit(solution)/shard_map/ppermute | solution.py:474
  34.4 21.0 %collective-permute-start = (bf16[8,12,8,128]{3,2,1,0:T(8,128)(2,1)S(1)}, bf16[8,12,8,128]{3,2,1,0:T(8,128)(2,1)S(1)}, u32[]{:S(2)}, u32[]{:S(2)}) collective-permute-start(bf16[8,12,8,128]{3,2,1,0:T(8,128)(2,1)S(1)} %slice.8.refs_7_), channel_id=1, source_target_pairs={{0,8},{8,16},{16,24},{24,0},{1,9},{9,17},{17,25},{25,1},{2,10},{10... | collective-permute-start | bytes 589832 | tf_op jit(solution)/shard_map/ppermute | solution.py:474
  45.9 9.5 %copy-start.9 = (bf16[1,1,2,64,1024]{4,3,2,1,0:T(8,128)(2,1)S(1)}, bf16[1,1,2,64,1024]{4,3,2,1,0:T(8,128)(2,1)}, u32[]{:S(2)}) copy-start(bf16[1,1,2,64,1024]{4,3,2,1,0:T(8,128)(2,1)} %param.13) | copy-start | bytes 786436
  53.8 13.1 %collective-permute-start.6 = (bf16[8,12,8,128]{3,2,1,0:T(8,128)(2,1)S(1)}, bf16[8,12,8,128]{3,2,1,0:T(8,128)(2,1)S(1)}, u32[]{:S(2)}, u32[]{:S(2)}) collective-permute-start(bf16[8,12,8,128]{3,2,1,0:T(8,128)(2,1)S(1)} %bitcast.38), channel_id=1, source_target_pairs={{0,24},{8,0},{16,8},{24,16},{1,25},{9,1},{17,9},{25,17},{2,26},{10... | collective-permute-start | bytes 589832 | tf_op jit(solution)/shard_map/ppermute | solution.py:474
  53.8 13.8 %collective-permute-start.7 = (bf16[8,12,8,128]{3,2,1,0:T(8,128)(2,1)S(1)}, bf16[8,12,8,128]{3,2,1,0:T(8,128)(2,1)S(1)}, u32[]{:S(2)}, u32[]{:S(2)}) collective-permute-start(bf16[8,12,8,128]{3,2,1,0:T(8,128)(2,1)S(1)} %bitcast.37), channel_id=1, source_target_pairs={{0,16},{8,24},{16,0},{24,8},{1,17},{9,25},{17,1},{25,9},{2,18},{10... | collective-permute-start | bytes 589832 | tf_op jit(solution)/shard_map/ppermute | solution.py:474
  54.6 13.1 %collective-permute-start.8 = (bf16[8,12,8,128]{3,2,1,0:T(8,128)(2,1)S(1)}, bf16[8,12,8,128]{3,2,1,0:T(8,128)(2,1)S(1)}, u32[]{:S(2)}, u32[]{:S(2)}) collective-permute-start(bf16[8,12,8,128]{3,2,1,0:T(8,128)(2,1)S(1)} %bitcast.36), channel_id=1, source_target_pairs={{0,8},{8,16},{16,24},{24,0},{1,9},{9,17},{17,25},{25,1},{2,10},{10... | collective-permute-start | bytes 589832 | tf_op jit(solution)/shard_map/ppermute | solution.py:474
  55.4 26.7 %copy-start = (bf16[1,1,2,8,4096]{4,3,2,1,0:T(8,128)(2,1)S(1)}, bf16[1,1,2,8,4096]{4,3,2,1,0:T(8,128)(2,1)}, u32[]{:S(2)}) copy-start(bf16[1,1,2,8,4096]{4,3,2,1,0:T(8,128)(2,1)} %param.14) | copy-start | bytes 393220
  55.4 26.7 %copy-start.2 = (s32[1,1,2]{2,1,0:T(1,128)S(1)}, s32[1,1,2]{2,1,0:T(1,128)}, u32[]{:S(2)}) copy-start(s32[1,1,2]{2,1,0:T(1,128)} %counts.5) | copy-start | bytes 28
  63.2 10.0 %collective-permute-start.9 = (bf16[8,12,8,128]{3,2,1,0:T(8,128)(2,1)}, bf16[8,12,8,128]{3,2,1,0:T(8,128)(2,1)S(1)}, u32[]{:S(2)}, u32[]{:S(2)}) collective-permute-start(bf16[8,12,8,128]{3,2,1,0:T(8,128)(2,1)} %bitcast.20), channel_id=1, source_target_pairs={{0,24},{8,0},{16,8},{24,16},{1,25},{9,1},{17,9},{25,17},{2,26},{10... | collective-permute-start | bytes 589832 | tf_op jit(solution)/shard_map/ppermute | solution.py:474
  65.6 7.6 %collective-permute-start.10 = (bf16[8,12,8,128]{3,2,1,0:T(8,128)(2,1)}, bf16[8,12,8,128]{3,2,1,0:T(8,128)(2,1)S(1)}, u32[]{:S(2)}, u32[]{:S(2)}) collective-permute-start(bf16[8,12,8,128]{3,2,1,0:T(8,128)(2,1)} %bitcast.21), channel_id=1, source_target_pairs={{0,16},{8,24},{16,0},{24,8},{1,17},{9,25},{17,1},{25,9},{2,18},{10... | collective-permute-start | bytes 589832 | tf_op jit(solution)/shard_map/ppermute | solution.py:474
  66.9 7.1 %collective-permute-start.11 = (bf16[8,12,8,128]{3,2,1,0:T(8,128)(2,1)}, bf16[8,12,8,128]{3,2,1,0:T(8,128)(2,1)S(1)}, u32[]{:S(2)}, u32[]{:S(2)}) collective-permute-start(bf16[8,12,8,128]{3,2,1,0:T(8,128)(2,1)} %bitcast.22), channel_id=1, source_target_pairs={{0,8},{8,16},{16,24},{24,0},{1,9},{9,17},{17,25},{25,1},{2,10},{10... | collective-permute-start | bytes 589832 | tf_op jit(solution)/shard_map/ppermute | solution.py:474
  67.7 14.4 %all-to-all-start.1 = ((bf16[32,8,128]{2,1,0:T(8,128)(2,1)}), bf16[32,8,128]{2,1,0:T(8,128)(2,1)S(1)}, u32[]{:S(2)}, u32[]{:S(2)}) async-start(bf16[32,8,128]{2,1,0:T(8,128)(2,1)} %bitcast.18), calls=%async_computation.1 | async-start | bytes 131072 | tf_op jit(solution)/shard_map/all_to_all | solution.py:470
  83.3 5.6 %collective-permute-start.12 = (bf16[16,12,8,128]{3,2,1,0:T(8,128)(2,1)S(1)}, bf16[16,12,8,128]{3,2,1,0:T(8,128)(2,1)S(1)}, u32[]{:S(2)}, u32[]{:S(2)}) collective-permute-start(bf16[16,12,8,128]{3,2,1,0:T(8,128)(2,1)S(1)} %get-tuple-element.71), channel_id=1, source_target_pairs={{0,1},{1,0},{2,3},{3,2},{4,5},{5,4},{6,7},{7,6},{8,9},{9,8},{10,11... | collective-permute-start | bytes 1179656 | tf_op jit(solution)/shard_map/ppermute | solution.py:478
  135.3 5.6 %collective-permute-start.13 = (bf16[16,12,8,128]{3,2,1,0:T(8,128)(2,1)S(1)}, bf16[16,12,8,128]{3,2,1,0:T(8,128)(2,1)S(1)}, u32[]{:S(2)}, u32[]{:S(2)}) collective-permute-start(bf16[16,12,8,128]{3,2,1,0:T(8,128)(2,1)S(1)} %all_to_all.28.mine), channel_id=1, source_target_pairs={{0,1},{1,0},{2,3},{3,2},{4,5},{5,4},{6,7},{7,6},{8,9},{9,8},{10,11... | collective-permute-start | bytes 1179656 | tf_op jit(solution)/shard_map/ppermute | solution.py:478
  (5 other events, 14.9 us)

commit v6 on v5

--- a/solution.py
+++ b/solution.py
@@ -25,6 +25,7 @@
 HEADS = 4
 HALF_TILES = 3 * HEADS
 LOW_TILE = HALF_TILES
+STATE_TILES = 6
 FAR = 384
 NEAR = 128
 KEYS = FAR + NEAR
@@ -45,7 +46,7 @@
     return jnp.where((slot == source) & (row < first + second), 1.0, 0.0)
 
 
-def project_kernel(counts, docs, state, down_t, up, frozen, out):
+def project_kernel(counts, docs, state, down_t, up, frozen, out, state_out):
     first, second = counts[0, 0, 0], counts[0, 0, 1]
     low = dot(state[...], down_t[...], ((1,), (1,))).astype(bf16)
     states = (frozen[...].astype(f32) + dot(low, up[...])).astype(bf16)
@@ -71,6 +72,15 @@
     for i, fact in enumerate((first, second, docs[0, 0, 0], docs[0, 0, 1])):
         extra = jnp.where(side & (sub == 4 + i), fact.astype(f32), extra)
     halves[0].append(extra)
+    state_rows = dot(pick, state[...])
+    half = MODEL_WIDTH // HD // 2
+    blocks = [state_rows[:, c * HD : (c + 1) * HD] for c in range(2 * half)]
+    tiles = [block[:8] for block in blocks]
+    for c in range(half):
+        a, b = blocks[c][8:], blocks[half + c][8:]
+        tiles.append(jnp.where(sub < 4, a, pltpu.roll(b, 4, 0)))
+    for t, tile in enumerate(tiles):
+        state_out[t // STATE_TILES, t % STATE_TILES] = tile.astype(bf16)
     for t, tile in enumerate(halves[0] + halves[1]):
         packed = tile.astype(bf16)
         for z in range(NZ):
@@ -86,8 +96,11 @@
     return pl.pallas_call(
         project_kernel,
         in_specs=[SMEM] * 2 + [VMEM] * 4,
-        out_specs=VMEM,
-        out_shape=jax.ShapeDtypeStruct((NZ, LOW_TILE + 1 + HALF_TILES, 8, HD), bf16),
+        out_specs=[VMEM] * 2,
+        out_shape=[
+            jax.ShapeDtypeStruct((NZ, LOW_TILE + 1 + HALF_TILES, 8, HD), bf16),
+            jax.ShapeDtypeStruct((NZ, STATE_TILES, 8, HD), bf16),
+        ],
         name="project",
     )(counts, docs, state, down_t, up, frozen)
 
@@ -257,7 +270,6 @@
     def _():
         lane = lax.broadcasted_iota(jnp.int32, (8, HD), 1)
         for b in range(NX):
-            x = lax.rem(place[1] - b + NX, NX)
             for z in range(NZ):
                 at = b * 64 + z * 8
                 head = low_total[at : at + 8, :]
@@ -265,7 +277,7 @@
                 tail = low_total[at : at + 8, :]
                 if z % 2:
                     tail = pltpu.roll(tail, 4, 0)
-                low_part[z, x] = jnp.where(lane < UPDATE_RANK, head, tail).astype(bf16)
+                low_part[z, b] = jnp.where(lane < UPDATE_RANK, head, tail).astype(bf16)
 
 
 def first_kernel(*refs):
@@ -282,7 +294,7 @@
 def second_kernel(*refs):
     (place, query, key, value, grad, up_key, up_value, *boxes) = refs[:11]
     bias, low_all, low_before = refs[11:14]
-    (attended, grad_query, grad_key, grad_value, *rest) = refs[18:]
+    (attended, grad_query, grad_key, grad_value, *rest) = refs[22:]
     outs, (up_k, up_v, low_part, low_total) = rest[:4], rest[4:]
     attend_kernel(
         place, None, None, query, key, value, grad, up_key, up_value, *boxes,
@@ -296,14 +308,14 @@
     wide = pl.BlockSpec((2, SPAN, GROUP * HD), lambda g: (0, 0, g + at))
     narrow = pl.BlockSpec((2, SPAN, HD), lambda g: (0, 0, g + at))
     whole = pl.BlockSpec(boxes[0].shape, lambda g: (0, 0, 0, 0))
-    part = pl.BlockSpec((NZ, 3, 1, 8, HD), lambda g: (0, 0, g, 0, 0))
+    part = pl.BlockSpec((NZ, 3, 1, 8, HD), lambda g: (0, half, g, 0, 0))
     up_key = pl.BlockSpec((UPDATE_RANK, HD), lambda g: (0, g + at))
     up_value = pl.BlockSpec((UPDATE_RANK, HD), lambda g: (0, KVH + g + at))
     up_part = pl.BlockSpec((UPDATE_RANK, HD), lambda g: (0, g))
     low_part = pl.BlockSpec((NZ, NX, 8, HD), lambda g: (0, 0, 0, 0))
     wide_shape = jax.ShapeDtypeStruct((2, SPAN, QW), bf16)
     narrow_shape = jax.ShapeDtypeStruct((2, SPAN, KEY_FEATURES), bf16)
-    part_shape = jax.ShapeDtypeStruct((NZ, 3, HEADS, 8, HD), bf16)
+    part_shape = jax.ShapeDtypeStruct((NZ, 2 * 3, HEADS, 8, HD), bf16)
     up_shape = jax.ShapeDtypeStruct((UPDATE_RANK, HEADS * HD), f32)
     kept = [
         jax.ShapeDtypeStruct((FAR, HD), f32),
@@ -320,11 +332,11 @@
         out_specs += kept_specs
         out_shape += kept
     else:
-        in_specs += kept_specs[1:] + kept_specs[:1] + [pl.BlockSpec(memory_space=pl.ANY)] * 4
+        in_specs += kept_specs[1:] + kept_specs[:1] + [pl.BlockSpec(memory_space=pl.ANY)] * 8
         out_specs.append(low_part)
         out_shape.append(jax.ShapeDtypeStruct((NZ, NX, 8, HD), bf16))
         scratch = [pltpu.VMEM((FAR, HD), f32)]
-        aliases = {len(in_specs) - 4 + i: i for i in range(4)}
+        aliases = {len(in_specs) - 8 + i: i for i in range(8)}
     return pl.pallas_call(
         (first_kernel, second_kernel)[half],
         grid=(HEADS,),
@@ -347,12 +359,23 @@
 HALF = CHUNKS * CHUNK
 
 
-def factor_kernel(place, counts, low_parts, state, key_a, value_a, key_b, value_b, keep, send):
-    pick = selection(counts[0, 0, 0], counts[0, 0, 1])
+def factor_kernel(
+    place, low_parts, box0, box1, box2, box3, key_a, value_a, key_b, value_b, keep, send
+):
     total = jnp.sum(low_parts[...].astype(f32), axis=0)
-    compact = jnp.concatenate([total, pltpu.roll(total, UPDATE_RANK, 1)], axis=0).astype(bf16)
-    low_grad = dot(pick.astype(bf16), compact, ((0,), (0,))).astype(bf16)
-    down_piece = dot(low_grad, state[...], ((0,), (0,)))
+    sub = lax.broadcasted_iota(jnp.int32, (8, HD), 0)
+    half = MODEL_WIDTH // HD // 2
+    lows, states = [], []
+    for b, box in enumerate((box0, box1, box2, box3)):
+        tiles = [
+            box[t // STATE_TILES, HALF_TILES + t % STATE_TILES].astype(f32) for t in range(3 * half)
+        ]
+        lows += [total[b], jnp.where(sub < 4, pltpu.roll(total[b], UPDATE_RANK, 1), 0.0)]
+        states.append(jnp.concatenate(tiles[: 2 * half], axis=1))
+        tails = tiles[2 * half :]
+        states.append(jnp.concatenate(tails + [pltpu.roll(t, 4, 0) for t in tails], axis=1))
+    low_grad = jnp.concatenate(lows, axis=0).astype(bf16)
+    down_piece = dot(low_grad, jnp.concatenate(states, axis=0).astype(bf16), ((0,), (0,)))
     wide = MODEL_WIDTH // HD
     ups = (key_a, key_b, value_a, value_b)
 
@@ -371,28 +394,26 @@
         send[t // CHUNK, t % CHUNK] = jnp.where(lower, b, a).astype(bf16)
 
 
-def factor(place, counts, low_parts, state, ups):
+def factor(place, low_parts, boxes, ups):
     return pl.pallas_call(
         factor_kernel,
-        in_specs=[SMEM] * 2 + [VMEM] * 6,
+        in_specs=[SMEM] + [VMEM] * 9,
         out_specs=[VMEM] * 2,
         out_shape=[jax.ShapeDtypeStruct((CHUNKS, CHUNK, 8, HD), bf16)] * 2,
         compiler_params=SMALL,
         name="factor",
-    )(place, counts, low_parts, state, *ups)
+    )(place, low_parts, *boxes, *ups)
 
 
 def middle_kernel(pieces, *refs):
     out = refs[-1]
     chunk = jnp.sum(pieces[...].astype(f32), axis=0).astype(bf16)
+    a, b, c, d = refs[:-1]
     for z in range(NZ):
         out[z, :CHUNK] = chunk
-        for half in range(2):
-            a, b, c, d = refs[half * NX : half * NX + NX]
-            at = CHUNK + half * HALF_TILES
-            out[z, at : at + HALF_TILES] = (
-                (a[z].astype(f32) + b[z].astype(f32)) + (c[z].astype(f32) + d[z].astype(f32))
-            ).astype(bf16)
+        out[z, CHUNK:] = (
+            (a[z].astype(f32) + b[z].astype(f32)) + (c[z].astype(f32) + d[z].astype(f32))
+        ).astype(bf16)
 
 
 def middle(pieces, parts):
@@ -483,7 +504,7 @@
 
 
 def collect(parts):
-    parts = [p.reshape(NZ, HALF_TILES, 8, HD) for p in parts]
+    parts = [p.reshape(NZ, 2 * HALF_TILES, 8, HD) for p in parts]
     return [parts[0], shift(parts[1], -1), shift(parts[2], -2), shift(parts[3], -3)]
 
 
@@ -495,25 +516,25 @@
     state = beacon_slot_state[0, 0].reshape(2 * MAX_BEACONS, MODEL_WIDTH)
     frozen = frozen_beacon_cache[0, 0].reshape(2 * MAX_BEACONS, 2 * KEY_FEATURES)
 
-    message = project(
+    message, state_tiles = project(
         span_beacon_count, span_document, state, adapter_down_weight.T, adapter_up_weight, frozen
     )
-    arrays = (query[0, 0], key[0, 0], value[0, 0], output_cotangent[0, 0], adapter_up_weight)
+    arrays = (query[0, 0], key[0, 0], value[0, 0], output_cotangent[0, 0])
+    arrays = [pltpu.with_memory_space_constraint(x, pltpu.HBM) for x in arrays]
+    arrays.append(adapter_up_weight)
     column = exchange(message, "z")
     boxes_a = spread(column[:, : LOW_TILE + 1])
-    boxes_b = spread(column[:, LOW_TILE + 1 :])
+    boxes_b = spread(jnp.concatenate([column[:, LOW_TILE + 1 :], state_tiles], axis=1))
     first = attend(0, (place, span_document, boundary), *arrays, boxes_a)
     low_total, bias, low_all = first[10:]
-    parts_a = collect(first[4:8])
-    second = attend(1, (place,), *arrays, boxes_b, (bias, low_all, low_total), first[:4])
-    parts_b = collect(second[4:8])
+    second = attend(1, (place,), *arrays, boxes_b, (bias, low_all, low_total), first[:8])
     attended, grad_query, grad_key, grad_value = second[:4]
-    low_part, parts_a = lax.optimization_barrier((second[10], parts_a))
-    low_parts = exchange(low_part.reshape(NZ * NX, 8, HD), ("z", "x"))
-    low_parts, parts_b = lax.optimization_barrier((low_parts, parts_b))
-    keep, send = factor(place, span_beacon_count, low_parts, state, first[8:10] + second[8:10])
+    parts = collect(second[4:8])
+    low_parts = exchange(second[10], "z")
+    keep, send = factor(place, low_parts, boxes_b, first[8:10] + second[8:10])
+    send, parts = lax.optimization_barrier((send, parts))
     pieces = (keep.astype(f32) + swap(send).astype(f32)).astype(bf16)
-    both = exchange(middle(exchange(pieces, PLANE), parts_a + parts_b), "z")
+    both = exchange(middle(exchange(pieces, PLANE), parts), "z")
     cache_gradient, chunk = close(span_beacon_count, both)
     mine = exchange(chunk, PLANE)
     adapter_gradient = unpack(place, mine, swap(mine))

time: 143 us -> 141 us (0.986)
  waiting for transfers between devices: 20.1 us -> 39.2 us
  blocking collectives: 67.5 us -> 54 us
  starting transfers between devices: 27.1 us -> 22.5 us
  local copies, waits for them, and re-layouts: 3.84 us -> 0.05 us
    all_to_all x4, blocking collectives: 67.5 us -> 54 us  [exchange(): return lax.all_to_all(x, axes, 0, 0, tiled=True)]
    ppermute x12 -> x9, waiting for transfers between devices: 9.32 us -> 21.8 us  [shift(): return lax.ppermute(x, 'x', [(i, (i + by) % NX) for i in range(NX)])]
    all_to_all x1, waiting for transfers between devices: 8.1 us -> 14.7 us  [exchange(): return lax.all_to_all(x, axes, 0, 0, tiled=True)]
    ppermute x12 -> x9, starting transfers between devices: 13.1 us -> 8.6 us  [shift(): return lax.ppermute(x, 'x', [(i, (i + by) % NX) for i in range(NX)])]
    ppermute x2, starting transfers between devices: 8.51 us -> 4.79 us  [swap(): return lax.ppermute(x, 'core', [(0, 1), (1, 0)])]
    all_to_all x1, starting transfers between devices: 5.57 us -> 9.15 us  [exchange(): return lax.all_to_all(x, axes, 0, 0, tiled=True)]
    unnamed x28 -> x10, local copies, waits for them, and re-layouts: 2.89 us -> 0.02 us
  transfers between devices with their start and end apart: 15 -> 12, of which waited for: 6 -> 7; matrix products, arithmetic and copies ran while one was open for 1% -> 0% of each run, Pallas kernels for 11% -> 7%
where the time goes in v6:
time: 141 us; the launch traced here: 140 us
  blocking collectives  54 us (38%)
  waiting for transfers between devices  39.2 us (28%)
  Pallas kernels  23.6 us (17%)
  starting transfers between devices  22.5 us (16%)
    all_to_all x4, blocking collectives, exchange(): return lax.all_to_all(x, axes, 0, 0, tiled=True)  54 us
    ppermute x9, waiting for transfers between devices, shift(): return lax.ppermute(x, 'x', [(i, (i + by) % NX) for i in range(NX)])  21.8 us
    pallas_call x2, Pallas kernels, attend(): pl.pallas_call((first_kernel, second_kernel)[half], grid=(HEADS,), in_spe...  16.3 us
    all_to_all x1, waiting for transfers between devices, exchange(): return lax.all_to_all(x, axes, 0, 0, tiled=True)  14.7 us
    all_to_all x1, starting transfers between devices, exchange(): return lax.all_to_all(x, axes, 0, 0, tiled=True)  9.15 us
    ppermute x9, starting transfers between devices, shift(): return lax.ppermute(x, 'x', [(i, (i + by) % NX) for i in range(NX)])  8.6 us
    ppermute x2, starting transfers between devices, swap(): return lax.ppermute(x, 'core', [(0, 1), (1, 0)])  4.79 us
  transfers between devices with their start and end apart: 12, of which 7 were waited for; matrix products, arithmetic and copies ran while one was open for 0% of the time, Pallas kernels for 7%

profile of v6, /device:TPU:1, one launch (start us, length us, event | category | flops | bytes accessed | tf_op | source)
XLA Modules:
  0.0 140.4 jit_solution(3463841710034350359)
XLA Ops:
  0.7 2.8 %project.1 = (bf16[8,25,8,128]{3,2,1,0:T(8,128)(2,1)}, bf16[8,6,8,128]{3,2,1,0:T(8,128)(2,1)}) custom-call(s32[1,1,2]{2,1,0:T(1,128)} %counts.3, s32[1,1,2]{2,1,0:T(1,128)} %refs_1_.1, bf16[16,4096]{1,0:T(8,128)(2,1)} %bitcast.24, bf16[64,4096]{1,0:T(8,128)(2,1)} %bitcast.23, bf16[64,2048]{1,0:T(8,128)(2,1)} %refs_6_.1, bf16[16,2048]{1,0:T(8,128)(2,1)} %bitcast.25), custom_call_target="tpu_custom_call" | custom-call | tf_op jit(solution)/shard_map/project/pallas_call | solution.py:96
  3.4 9.1 %all-to-all-start = ((bf16[8,25,8,128]{3,2,1,0:T(8,128)(2,1)}), bf16[8,25,8,128]{3,2,1,0:T(8,128)(2,1)S(1)}, u32[]{:S(2)}, u32[]{:S(2)}) async-start(bf16[8,25,8,128]{3,2,1,0:T(8,128)(2,1)} %get-tuple-element.41), calls=%async_computation | async-start | bytes 819200 | tf_op jit(solution)/shard_map/all_to_all | solution.py:491
  12.6 14.7 %all-to-all-done = bf16[8,25,8,128]{3,2,1,0:T(8,128)(2,1)S(1)} async-done(((bf16[8,25,8,128]{3,2,1,0:T(8,128)(2,1)}), bf16[8,25,8,128]{3,2,1,0:T(8,128)(2,1)S(1)}, u32[]{:S(2)}, u32[]{:S(2)}) %all-to-all-start) | async-done | bytes 409632 | tf_op jit(solution)/shard_map/all_to_all | solution.py:491
  27.3 2.6 %collective-permute-start.5 = (bf16[8,13,8,128]{3,2,1,0:T(8,128)(2,1)S(1)}, bf16[8,13,8,128]{3,2,1,0:T(8,128)(2,1)S(1)}, u32[]{:S(2)}, u32[]{:S(2)}) collective-permute-start(bf16[8,13,8,128]{3,2,1,0:T(8,128)(2,1)S(1)} %slice.9.refs_9_), channel_id=1, source_target_pairs={{0,24},{8,0},{16,8},{24,16},{1,25},{9,1},{17,9},{25,17},{2,26},{10... | collective-permute-start | bytes 638984 | tf_op jit(solution)/shard_map/ppermute | solution.py:495
  30.4 0.6 collective-permute-start.3
  31.1 2.1 %collective-permute-start.2 = (bf16[8,18,8,128]{3,2,1,0:T(8,128)(2,1)S(1)}, bf16[8,18,8,128]{3,2,1,0:T(8,128)(2,1)S(1)}, u32[]{:S(2)}, u32[]{:S(2)}) collective-permute-start(bf16[8,18,8,128]{3,2,1,0:T(8,128)(2,1)S(1)} %pad_maximum_fusion.refs_7_.box0), channel_id=1, source_target_pairs={{0,24},{8,0},{16,8},{24,16},{1,25},{9,1},{17,9},{25,17},{2,26},{10... | collective-permute-start | bytes 884744 | tf_op jit(solution)/shard_map/ppermute | solution.py:495
  33.3 1.2 collective-permute-start.1
  34.5 2.1 %collective-permute-done.4.refs_11_ = bf16[8,13,8,128]{3,2,1,0:T(8,128)(2,1)S(1)} collective-permute-done((bf16[8,13,8,128]{3,2,1,0:T(8,128)(2,1)S(1)}, bf16[8,13,8,128]{3,2,1,0:T(8,128)(2,1)S(1)}, u32[]{:S(2)}, u32[]{:S(2)}) %collective-permute-start.4) | collective-permute-done | bytes 213024 | tf_op jit(solution)/shard_map/ppermute | solution.py:495
  36.6 8.4 %collective-permute-done.3.refs_10_ = bf16[8,13,8,128]{3,2,1,0:T(8,128)(2,1)S(1)} collective-permute-done((bf16[8,13,8,128]{3,2,1,0:T(8,128)(2,1)S(1)}, bf16[8,13,8,128]{3,2,1,0:T(8,128)(2,1)S(1)}, u32[]{:S(2)}, u32[]{:S(2)}) %collective-permute-start.3) | collective-permute-done | bytes 213024 | tf_op jit(solution)/shard_map/ppermute | solution.py:495
  45.0 8.3 %attend_first.1 = (bf16[2,64,4096]{2,1,0:T(8,128)(2,1)}, bf16[2,64,4096]{2,1,0:T(8,128)(2,1)}, bf16[2,64,1024]{2,1,0:T(8,128)(2,1)}, bf16[2,64,1024]{2,1,0:T(8,1...) custom-call(s32[3]{0:T(128)S(1)} %pad_add_fusion.refs_0_.place, ...), custom_call_target="tpu_custom_call" | custom-call | flops 6000000000 | bytes 4194304 | tf_op jit(solution)/shard_map/attend_first/pallas_call | solution.py:340
  53.3 2.4 %collective-permute-done.refs_8_.box1 = bf16[8,18,8,128]{3,2,1,0:T(8,128)(2,1)S(1)} collective-permute-done((bf16[8,18,8,128]{3,2,1,0:T(8,128)(2,1)S(1)}, bf16[8,18,8,128]{3,2,1,0:T(8,128)(2,1)S(1)}, u32[]{:S(2)}, u32[]{:S(2)}) %collective-permute-start) | collective-permute-done | bytes 294944 | tf_op jit(solution)/shard_map/ppermute | solution.py:495
  55.7 8.1 %attend_second.1 = (bf16[2,64,4096]{2,1,0:T(8,128)(2,1)}, bf16[2,64,4096]{2,1,0:T(8,128)(2,1)}, bf16[2,64,1024]{2,1,0:T(8,128)(2,1)}, bf16[2,64,1024]{2,1,0:T(8,...) custom-call(s32[3]{0:T(128)S(1)} %pad_add_fusion.refs_0_.place, ...), custom_call_target="tpu_custom_call", output_to_operand_aliasing={{0}: (14, {}), {1}: (15, {}), {2}: (16, {}), {3}: (17, {}),... | custom-call | flops 6000000000 | bytes 4194304 | tf_op jit(solution)/shard_map/attend_second/pallas_call | solution.py:340
  64.2 1.1 collective-permute-start.8
  65.3 9.6 %all_to_all.25.low_parts = bf16[8,4,8,128]{3,2,1,0:T(8,128)(2,1)S(1)} all-to-all(bf16[8,4,8,128]{3,2,1,0:T(8,128)(2,1)S(1)} %get-tuple-element.58), channel_id=1, replica_groups=mesh['z'=8,'x'=4,'y'=4,'core'=2] {'z'}, dimensions={0} | all-to-all | bytes 131072 | tf_op jit(solution)/shard_map/all_to_all | solution.py:491
  74.9 1.1 factor.1
  76.0 8.9 %collective-permute-done.8.refs_3_ = bf16[8,24,8,128]{3,2,1,0:T(8,128)(2,1)S(1)} collective-permute-done((bf16[8,24,8,128]{3,2,1,0:T(8,128)(2,1)S(1)}, bf16[8,24,8,128]{3,2,1,0:T(8,128)(2,1)S(1)}, u32[]{:S(2)}, u32[]{:S(2)}) %collective-permute-start.8) | collective-permute-done | bytes 393248 | tf_op jit(solution)/shard_map/ppermute | solution.py:495
  85.4 1.3 collective-permute-done.9
  86.9 13.8 %all_to_all.26.pieces = bf16[16,12,8,128]{3,2,1,0:T(8,128)(2,1)S(1)} all-to-all(bf16[16,12,8,128]{3,2,1,0:T(8,128)(2,1)S(1)} %add_convert_fusion), channel_id=1, replica_groups=mesh['z'=8,'x'=4,'y'=4,'core'=2] {'x','y'}, dimensions={0} | all-to-all | bytes 786432 | tf_op jit(solution)/shard_map/all_to_all | solution.py:491
  101.0 19.3 %all_to_all.27.parts = bf16[8,36,8,128]{3,2,1,0:T(8,128)(2,1)S(1)} all-to-all(bf16[8,36,8,128]{3,2,1,0:T(8,128)(2,1)S(1)} %middle.1), channel_id=1, replica_groups=mesh['z'=8,'x'=4,'y'=4,'core'=2] {'z'}, dimensions={0} | all-to-all | bytes 1179648 | tf_op jit(solution)/shard_map/all_to_all | solution.py:491
  120.2 1.4 close.1
  121.6 11.3 %all_to_all.28.mine = bf16[16,12,8,128]{3,2,1,0:T(8,128)(2,1)S(1)} all-to-all(bf16[16,12,8,128]{3,2,1,0:T(8,128)(2,1)S(1)} %get-tuple-element.75), channel_id=1, replica_groups=mesh['z'=8,'x'=4,'y'=4,'core'=2] {'x','y'}, dimensions={0} | all-to-all | bytes 786432 | tf_op jit(solution)/shard_map/all_to_all | solution.py:491
  132.9 4.3 %collective-permute-start.10 = (bf16[16,12,8,128]{3,2,1,0:T(8,128)(2,1)S(1)}, bf16[16,12,8,128]{3,2,1,0:T(8,128)(2,1)S(1)}, u32[]{:S(2)}, u32[]{:S(2)}) collective-permute-start(bf16[16,12,8,128]{3,2,1,0:T(8,128)(2,1)S(1)} %all_to_all.28.mine), channel_id=1, source_target_pairs={{0,1},{1,0},{2,3},{3,2},{4,5},{5,4},{6,7},{7,6},{8,9},{9,8},{10,11... | collective-permute-start | bytes 1179656 | tf_op jit(solution)/shard_map/ppermute | solution.py:499
  137.2 1.3 collective-permute-done.10.other
  138.6 1.8 %unpack.1 = f32[64,6144]{1,0:T(8,128)} custom-call(s32[3]{0:T(128)S(1)} %pad_add_fusion.refs_0_.place, bf16[16,12,8,128]{3,2,1,0:T(8,128)(2,1)S(1)} %all_to_all.28.mine, bf16[16,12,8,128]{3,2,1,0:T(8,128)(2,1)S(1)} %collective-permute-done.10.other), custom_call_target="tpu_custom_call" | custom-call | tf_op jit(solution)/shard_map/unpack/pallas_call | solution.py:480
  (26 shorter events, 1.9 us)
Async XLA Ops:
  0.6 44.4 %copy-start = (bf16[64,2048]{1,0:T(8,128)(2,1)S(1)}, bf16[64,2048]{1,0:T(8,128)(2,1)}, u32[]{:S(2)}) copy-start(bf16[64,2048]{1,0:T(8,128)(2,1)} %refs_6_.1) | copy-start | bytes 786436
  0.6 44.4 %copy-start.2 = (s32[1,1,2]{2,1,0:T(1,128)S(1)}, s32[1,1,2]{2,1,0:T(1,128)}, u32[]{:S(2)}) copy-start(s32[1,1,2]{2,1,0:T(1,128)} %refs_1_.1) | copy-start | bytes 28
  0.7 44.4 %copy-start.3 = (s32[1,1,2]{2,1,0:T(1,128)S(1)}, s32[1,1,2]{2,1,0:T(1,128)}, u32[]{:S(2)}) copy-start(s32[1,1,2]{2,1,0:T(1,128)} %refs_2_.1) | copy-start | bytes 28
  3.4 27.7 %copy-start.4 = (bf16[8,6,8,128]{3,2,1,0:T(8,128)(2,1)S(1)}, bf16[8,6,8,128]{3,2,1,0:T(8,128)(2,1)}, u32[]{:S(2)}) copy-start(bf16[8,6,8,128]{3,2,1,0:T(8,128)(2,1)} %get-tuple-element.42) | copy-start | bytes 294916
  3.4 23.9 %all-to-all-start = ((bf16[8,25,8,128]{3,2,1,0:T(8,128)(2,1)}), bf16[8,25,8,128]{3,2,1,0:T(8,128)(2,1)S(1)}, u32[]{:S(2)}, u32[]{:S(2)}) async-start(bf16[8,25,8,128]{3,2,1,0:T(8,128)(2,1)} %get-tuple-element.41), calls=%async_computation | async-start | bytes 819200 | tf_op jit(solution)/shard_map/all_to_all | solution.py:491
  27.3 7.2 %collective-permute-start.5 = (bf16[8,13,8,128]{3,2,1,0:T(8,128)(2,1)S(1)}, bf16[8,13,8,128]{3,2,1,0:T(8,128)(2,1)S(1)}, u32[]{:S(2)}, u32[]{:S(2)}) collective-permute-start(bf16[8,13,8,128]{3,2,1,0:T(8,128)(2,1)S(1)} %slice.9.refs_9_), channel_id=1, source_target_pairs={{0,24},{8,0},{16,8},{24,16},{1,25},{9,1},{17,9},{25,17},{2,26},{10... | collective-permute-start | bytes 638984 | tf_op jit(solution)/shard_map/ppermute | solution.py:495
  29.9 6.8 %collective-permute-start.4 = (bf16[8,13,8,128]{3,2,1,0:T(8,128)(2,1)S(1)}, bf16[8,13,8,128]{3,2,1,0:T(8,128)(2,1)S(1)}, u32[]{:S(2)}, u32[]{:S(2)}) collective-permute-start(bf16[8,13,8,128]{3,2,1,0:T(8,128)(2,1)S(1)} %slice.9.refs_9_), channel_id=1, source_target_pairs={{0,16},{8,24},{16,0},{24,8},{1,17},{9,25},{17,1},{25,9},{2,18},{10... | collective-permute-start | bytes 638984 | tf_op jit(solution)/shard_map/ppermute | solution.py:495
  30.4 14.6 %collective-permute-start.3 = (bf16[8,13,8,128]{3,2,1,0:T(8,128)(2,1)S(1)}, bf16[8,13,8,128]{3,2,1,0:T(8,128)(2,1)S(1)}, u32[]{:S(2)}, u32[]{:S(2)}) collective-permute-start(bf16[8,13,8,128]{3,2,1,0:T(8,128)(2,1)S(1)} %slice.9.refs_9_), channel_id=1, source_target_pairs={{0,8},{8,16},{16,24},{24,0},{1,9},{9,17},{17,25},{25,1},{2,10},{10... | collective-permute-start | bytes 638984 | tf_op jit(solution)/shard_map/ppermute | solution.py:495
  31.1 22.2 %collective-permute-start.2 = (bf16[8,18,8,128]{3,2,1,0:T(8,128)(2,1)S(1)}, bf16[8,18,8,128]{3,2,1,0:T(8,128)(2,1)S(1)}, u32[]{:S(2)}, u32[]{:S(2)}) collective-permute-start(bf16[8,18,8,128]{3,2,1,0:T(8,128)(2,1)S(1)} %pad_maximum_fusion.refs_7_.box0), channel_id=1, source_target_pairs={{0,24},{8,0},{16,8},{24,16},{1,25},{9,1},{17,9},{25,17},{2,26},{10... | collective-permute-start | bytes 884744 | tf_op jit(solution)/shard_map/ppermute | solution.py:495
  33.3 20.0 %collective-permute-start.1 = (bf16[8,18,8,128]{3,2,1,0:T(8,128)(2,1)S(1)}, bf16[8,18,8,128]{3,2,1,0:T(8,128)(2,1)S(1)}, u32[]{:S(2)}, u32[]{:S(2)}) collective-permute-start(bf16[8,18,8,128]{3,2,1,0:T(8,128)(2,1)S(1)} %pad_maximum_fusion.refs_7_.box0), channel_id=1, source_target_pairs={{0,16},{8,24},{16,0},{24,8},{1,17},{9,25},{17,1},{25,9},{2,18},{10... | collective-permute-start | bytes 884744 | tf_op jit(solution)/shard_map/ppermute | solution.py:495
  34.5 21.2 %collective-permute-start = (bf16[8,18,8,128]{3,2,1,0:T(8,128)(2,1)S(1)}, bf16[8,18,8,128]{3,2,1,0:T(8,128)(2,1)S(1)}, u32[]{:S(2)}, u32[]{:S(2)}) collective-permute-start(bf16[8,18,8,128]{3,2,1,0:T(8,128)(2,1)S(1)} %pad_maximum_fusion.refs_7_.box0), channel_id=1, source_target_pairs={{0,8},{8,16},{16,24},{24,0},{1,9},{9,17},{17,25},{25,1},{2,10},{10... | collective-permute-start | bytes 884744 | tf_op jit(solution)/shard_map/ppermute | solution.py:495
  63.8 12.2 %collective-permute-start.6 = (bf16[8,24,8,128]{3,2,1,0:T(8,128)(2,1)S(1)}, bf16[8,24,8,128]{3,2,1,0:T(8,128)(2,1)S(1)}, u32[]{:S(2)}, u32[]{:S(2)}) collective-permute-start(bf16[8,24,8,128]{3,2,1,0:T(8,128)(2,1)S(1)} %bitcast.20), channel_id=1, source_target_pairs={{0,24},{8,0},{16,8},{24,16},{1,25},{9,1},{17,9},{25,17},{2,26},{10... | collective-permute-start | bytes 1179656 | tf_op jit(solution)/shard_map/ppermute | solution.py:495
  63.8 12.1 %collective-permute-start.7 = (bf16[8,24,8,128]{3,2,1,0:T(8,128)(2,1)S(1)}, bf16[8,24,8,128]{3,2,1,0:T(8,128)(2,1)S(1)}, u32[]{:S(2)}, u32[]{:S(2)}) collective-permute-start(bf16[8,24,8,128]{3,2,1,0:T(8,128)(2,1)S(1)} %bitcast.21), channel_id=1, source_target_pairs={{0,16},{8,24},{16,0},{24,8},{1,17},{9,25},{17,1},{25,9},{2,18},{10... | collective-permute-start | bytes 1179656 | tf_op jit(solution)/shard_map/ppermute | solution.py:495
  64.2 20.7 %collective-permute-start.8 = (bf16[8,24,8,128]{3,2,1,0:T(8,128)(2,1)S(1)}, bf16[8,24,8,128]{3,2,1,0:T(8,128)(2,1)S(1)}, u32[]{:S(2)}, u32[]{:S(2)}) collective-permute-start(bf16[8,24,8,128]{3,2,1,0:T(8,128)(2,1)S(1)} %bitcast.22), channel_id=1, source_target_pairs={{0,8},{8,16},{16,24},{24,0},{1,9},{9,17},{17,25},{25,1},{2,10},{10... | collective-permute-start | bytes 1179656 | tf_op jit(solution)/shard_map/ppermute | solution.py:495
  84.9 1.8 %collective-permute-start.9 = (bf16[16,12,8,128]{3,2,1,0:T(8,128)(2,1)S(1)}, bf16[16,12,8,128]{3,2,1,0:T(8,128)(2,1)S(1)}, u32[]{:S(2)}, u32[]{:S(2)}) collective-permute-start(bf16[16,12,8,128]{3,2,1,0:T(8,128)(2,1)S(1)} %get-tuple-element.69), channel_id=1, source_target_pairs={{0,1},{1,0},{2,3},{3,2},{4,5},{5,4},{6,7},{7,6},{8,9},{9,8},{10,11... | collective-permute-start | bytes 1179656 | tf_op jit(solution)/shard_map/ppermute | solution.py:499
  100.7 19.5 %copy-start.1 = (s32[1,1,2]{2,1,0:T(1,128)S(1)}, s32[1,1,2]{2,1,0:T(1,128)}, u32[]{:S(2)}) copy-start(s32[1,1,2]{2,1,0:T(1,128)} %counts.3) | copy-start | bytes 28
  132.9 5.6 %collective-permute-start.10 = (bf16[16,12,8,128]{3,2,1,0:T(8,128)(2,1)S(1)}, bf16[16,12,8,128]{3,2,1,0:T(8,128)(2,1)S(1)}, u32[]{:S(2)}, u32[]{:S(2)}) collective-permute-start(bf16[16,12,8,128]{3,2,1,0:T(8,128)(2,1)S(1)} %all_to_all.28.mine), channel_id=1, source_target_pairs={{0,1},{1,0},{2,3},{3,2},{4,5},{5,4},{6,7},{7,6},{8,9},{9,8},{10,11... | collective-permute-start | bytes 1179656 | tf_op jit(solution)/shard_map/ppermute | solution.py:499

commit v7 on v5

--- a/solution.py
+++ b/solution.py
@@ -23,6 +23,7 @@
 PLANE = ("x", "y")
 
 HEADS = 4
+STEP = 2
 HALF_TILES = 3 * HEADS
 LOW_TILE = HALF_TILES
 FAR = 384
@@ -175,8 +176,8 @@
 
     sub = lax.broadcasted_iota(jnp.int32, (NZ // 2, 8, HD), 1)
 
-    def stack(ref):
-        whole = ref[...].reshape(2 * SPAN, GROUP * HD)
+    def stack(ref, n):
+        whole = ref[:, :, n * GROUP * HD : (n + 1) * GROUP * HD].reshape(2 * SPAN, GROUP * HD)
         return jnp.concatenate(
             [whole[:, m * HD : (m + 1) * HD] for m in range(GROUP)], axis=0
         )
@@ -184,76 +185,92 @@
     def far_rows(tile):
         return [box[:, tile].astype(f32).reshape(8 * NZ, HD) for box in boxes]
 
-    extra_keys, extra_values = [], []
-    for box in boxes:
-        both = box[:, 2 * HEADS + g].astype(f32).reshape(NZ // 2, 2, 8, HD)
-        even, odd = both[:, 0], both[:, 1]
-        extra_keys.append(jnp.where(sub < 4, even, pltpu.roll(odd, 4, 1)).reshape(4 * NZ, HD))
-        extra_values.append(jnp.where(sub < 4, pltpu.roll(even, 4, 1), odd).reshape(4 * NZ, HD))
-    keys = jnp.concatenate(
-        [key[...].reshape(NEAR, HD).astype(f32)] + far_rows(g) + extra_keys, axis=0
-    )
-    values = jnp.concatenate(
-        [value[...].reshape(NEAR, HD).astype(f32)] + far_rows(HEADS + g) + extra_values, axis=0
-    )
-    keys = keys.astype(bf16)
-    values = values.astype(bf16)
-    keys_t = keys.T
-    values_t = values.T
-    queries = stack(query)
-    grads = stack(grad)
-    grads_t = grads.T
-
-    scores = dot(keys, queries, ((1,), (1,))) * (SCORE_SCALE * LOG2E)
-    scores = scores + jnp.tile(bias[...], (1, GROUP))
-    top = jnp.max(scores, axis=0, keepdims=True)
-    weights = jnp.exp2(scores - top)
-    total = jnp.sum(weights, axis=0, keepdims=True)
-    exact = weights * (1.0 / total)
-    probs = exact.astype(bf16)
-    summed_t = dot(values_t, probs)
-    rounded_t = summed_t.astype(bf16)
-    summed = rounded_t.T
-    delta = jnp.sum(grads_t.astype(f32) * rounded_t.astype(f32), axis=0, keepdims=True)
-    grad_probs = dot(values, grads_t)
-    grad_scores = (exact * (grad_probs - delta)).astype(bf16)
-    query_grad = (dot(keys_t, grad_scores) * SCORE_SCALE).astype(bf16).T
-    key_grad = dot(grad_scores, queries) * SCORE_SCALE
-    value_grad = dot(probs, grads)
-
-    for m in range(GROUP):
-        at = slice(m * 2 * SPAN, (m + 1) * 2 * SPAN)
-        cols = slice(m * HD, (m + 1) * HD)
-        attended[:, :, cols] = summed[at].reshape(2, SPAN, HD)
-        grad_query[:, :, cols] = query_grad[at].reshape(2, SPAN, HD)
-    grad_key[...] = key_grad[:NEAR].astype(bf16).reshape(2, SPAN, HD)
-    grad_value[...] = value_grad[:NEAR].astype(bf16).reshape(2, SPAN, HD)
-    for b, out in enumerate(outs):
-        at = NEAR + b * 64
-        out[:, 0, 0] = key_grad[at : at + 64].reshape(NZ, 8, HD).astype(bf16)
-        out[:, 1, 0] = value_grad[at : at + 64].reshape(NZ, 8, HD).astype(bf16)
-        at = NEAR + 256 + b * 32
-        k = key_grad[at : at + 32].reshape(NZ // 2, 8, HD)
-        v = value_grad[at : at + 32].reshape(NZ // 2, 8, HD)
-        even = jnp.where(sub < 4, k, pltpu.roll(v, 4, 1)).astype(bf16)
-        odd = jnp.where(sub < 4, pltpu.roll(k, 4, 1), v).astype(bf16)
-        for i in range(NZ // 2):
-            out[2 * i, 2, 0] = even[i]
-            out[2 * i + 1, 2, 0] = odd[i]
-
-    far_keys = key_grad[NEAR:].astype(bf16)
-    far_values = value_grad[NEAR:].astype(bf16)
-    far = jnp.concatenate([far_keys, far_values], axis=1)
-    up_part = dot(low_all[...], far)
-    up_key_part[...] = up_part[:, :HD]
-    up_value_part[...] = up_part[:, HD:]
-    up_both = jnp.concatenate([up_key[...], up_value[...]], axis=1)
-    low_total[...] += dot(far, jnp.concatenate([up_both, up_both], axis=0), ((1,), (1,)))
+    def own(ref, n):
+        return ref[:, :, n * HD : (n + 1) * HD].reshape(NEAR, HD).astype(f32)
+
+    def load(n):
+        h = g * STEP + n
+        extra_keys, extra_values = [], []
+        for box in boxes:
+            both = box[:, 2 * HEADS + h].astype(f32).reshape(NZ // 2, 2, 8, HD)
+            even, odd = both[:, 0], both[:, 1]
+            extra_keys.append(jnp.where(sub < 4, even, pltpu.roll(odd, 4, 1)).reshape(4 * NZ, HD))
+            extra_values.append(
+                jnp.where(sub < 4, pltpu.roll(even, 4, 1), odd).reshape(4 * NZ, HD)
+            )
+        keys = jnp.concatenate([own(key, n)] + far_rows(h) + extra_keys, axis=0)
+        values = jnp.concatenate([own(value, n)] + far_rows(HEADS + h) + extra_values, axis=0)
+        keys, values = keys.astype(bf16), values.astype(bf16)
+        queries, grads = stack(query, n), stack(grad, n)
+        return keys, values, queries, grads, grads.T
+
+    def scored(keys, values, queries, grads, grads_t):
+        return dot(keys, queries, ((1,), (1,))), dot(values, grads_t)
+
+    def soften(scores):
+        scores = scores * (SCORE_SCALE * LOG2E) + jnp.tile(bias[...], (1, GROUP))
+        top = jnp.max(scores, axis=0, keepdims=True)
+        weights = jnp.exp2(scores - top)
+        total = jnp.sum(weights, axis=0, keepdims=True)
+        return weights * (1.0 / total)
+
+    def forward(values, exact):
+        probs = exact.astype(bf16)
+        return probs, dot(values.T, probs).astype(bf16)
+
+    def backward(keys, queries, grads, grads_t, exact, probs, rounded_t, grad_probs):
+        delta = jnp.sum(grads_t.astype(f32) * rounded_t.astype(f32), axis=0, keepdims=True)
+        grad_scores = (exact * (grad_probs - delta)).astype(bf16)
+        query_grad = (dot(keys.T, grad_scores) * SCORE_SCALE).astype(bf16).T
+        key_grad = dot(grad_scores, queries) * SCORE_SCALE
+        value_grad = dot(probs, grads)
+        return rounded_t.T, query_grad, key_grad, value_grad
+
+    def emit(n, summed, query_grad, key_grad, value_grad):
+        for m in range(GROUP):
+            at = slice(m * 2 * SPAN, (m + 1) * 2 * SPAN)
+            cols = slice((n * GROUP + m) * HD, (n * GROUP + m + 1) * HD)
+            attended[:, :, cols] = summed[at].reshape(2, SPAN, HD)
+            grad_query[:, :, cols] = query_grad[at].reshape(2, SPAN, HD)
+        cols = slice(n * HD, (n + 1) * HD)
+        grad_key[:, :, cols] = key_grad[:NEAR].astype(bf16).reshape(2, SPAN, HD)
+        grad_value[:, :, cols] = value_grad[:NEAR].astype(bf16).reshape(2, SPAN, HD)
+        for b, out in enumerate(outs):
+            at = NEAR + b * 64
+            out[:, 0, n] = key_grad[at : at + 64].reshape(NZ, 8, HD).astype(bf16)
+            out[:, 1, n] = value_grad[at : at + 64].reshape(NZ, 8, HD).astype(bf16)
+            at = NEAR + 256 + b * 32
+            k = key_grad[at : at + 32].reshape(NZ // 2, 8, HD)
+            v = value_grad[at : at + 32].reshape(NZ // 2, 8, HD)
+            even = jnp.where(sub < 4, k, pltpu.roll(v, 4, 1)).astype(bf16)
+            odd = jnp.where(sub < 4, pltpu.roll(k, 4, 1), v).astype(bf16)
+            for i in range(NZ // 2):
+                out[2 * i, 2, n] = even[i]
+                out[2 * i + 1, 2, n] = odd[i]
+        far_keys = key_grad[NEAR:].astype(bf16)
+        far_values = value_grad[NEAR:].astype(bf16)
+        far = jnp.concatenate([far_keys, far_values], axis=1)
+        up_part = dot(low_all[...], far)
+        up_key_part[:, cols] = up_part[:, :HD]
+        up_value_part[:, cols] = up_part[:, HD:]
+        up_both = jnp.concatenate([up_key[:, cols], up_value[:, cols]], axis=1)
+        low_total[...] += dot(far, jnp.concatenate([up_both, up_both], axis=0), ((1,), (1,)))
+
+    ns = range(STEP)
+    loaded = [load(n) for n in ns]
+    raw = [scored(*loaded[n]) for n in ns]
+    exact, ahead = [], []
+    for n in ns:
+        exact.append(soften(raw[n][0]))
+        ahead.append(forward(loaded[n][1], exact[n]))
+    for n in ns:
+        keys, values, queries, grads, grads_t = loaded[n]
+        emit(n, *backward(keys, queries, grads, grads_t, exact[n], *ahead[n], raw[n][1]))
 
     if not last:
         return
 
-    @pl.when(g == HEADS - 1)
+    @pl.when(g == HEADS // STEP - 1)
     def _():
         lane = lax.broadcasted_iota(jnp.int32, (8, HD), 1)
         for b in range(NX):
@@ -282,7 +299,7 @@
 def second_kernel(*refs):
     (place, query, key, value, grad, up_key, up_value, *boxes) = refs[:11]
     bias, low_all, low_before = refs[11:14]
-    (attended, grad_query, grad_key, grad_value, *rest) = refs[18:]
+    (attended, grad_query, grad_key, grad_value, *rest) = refs[22:]
     outs, (up_k, up_v, low_part, low_total) = rest[:4], rest[4:]
     attend_kernel(
         place, None, None, query, key, value, grad, up_key, up_value, *boxes,
@@ -292,18 +309,18 @@
 
 
 def attend(half, small, query, key, value, grad, up, boxes, carried=(), filled=()):
-    at = half * HEADS
-    wide = pl.BlockSpec((2, SPAN, GROUP * HD), lambda g: (0, 0, g + at))
-    narrow = pl.BlockSpec((2, SPAN, HD), lambda g: (0, 0, g + at))
+    at = half * HEADS // STEP
+    wide = pl.BlockSpec((2, SPAN, STEP * GROUP * HD), lambda g: (0, 0, g + at))
+    narrow = pl.BlockSpec((2, SPAN, STEP * HD), lambda g: (0, 0, g + at))
     whole = pl.BlockSpec(boxes[0].shape, lambda g: (0, 0, 0, 0))
-    part = pl.BlockSpec((NZ, 3, 1, 8, HD), lambda g: (0, 0, g, 0, 0))
-    up_key = pl.BlockSpec((UPDATE_RANK, HD), lambda g: (0, g + at))
-    up_value = pl.BlockSpec((UPDATE_RANK, HD), lambda g: (0, KVH + g + at))
-    up_part = pl.BlockSpec((UPDATE_RANK, HD), lambda g: (0, g))
+    part = pl.BlockSpec((NZ, 3, STEP, 8, HD), lambda g: (0, half, g, 0, 0))
+    up_key = pl.BlockSpec((UPDATE_RANK, STEP * HD), lambda g: (0, g + at))
+    up_value = pl.BlockSpec((UPDATE_RANK, STEP * HD), lambda g: (0, KVH // STEP + g + at))
+    up_part = pl.BlockSpec((UPDATE_RANK, STEP * HD), lambda g: (0, g))
     low_part = pl.BlockSpec((NZ, NX, 8, HD), lambda g: (0, 0, 0, 0))
     wide_shape = jax.ShapeDtypeStruct((2, SPAN, QW), bf16)
     narrow_shape = jax.ShapeDtypeStruct((2, SPAN, KEY_FEATURES), bf16)
-    part_shape = jax.ShapeDtypeStruct((NZ, 3, HEADS, 8, HD), bf16)
+    part_shape = jax.ShapeDtypeStruct((NZ, 2 * 3, HEADS, 8, HD), bf16)
     up_shape = jax.ShapeDtypeStruct((UPDATE_RANK, HEADS * HD), f32)
     kept = [
         jax.ShapeDtypeStruct((FAR, HD), f32),
@@ -320,20 +337,20 @@
         out_specs += kept_specs
         out_shape += kept
     else:
-        in_specs += kept_specs[1:] + kept_specs[:1] + [pl.BlockSpec(memory_space=pl.ANY)] * 4
+        in_specs += kept_specs[1:] + kept_specs[:1] + [pl.BlockSpec(memory_space=pl.ANY)] * 8
         out_specs.append(low_part)
         out_shape.append(jax.ShapeDtypeStruct((NZ, NX, 8, HD), bf16))
         scratch = [pltpu.VMEM((FAR, HD), f32)]
-        aliases = {len(in_specs) - 4 + i: i for i in range(4)}
+        aliases = {len(in_specs) - 8 + i: i for i in range(8)}
     return pl.pallas_call(
         (first_kernel, second_kernel)[half],
-        grid=(HEADS,),
+        grid=(HEADS // STEP,),
         in_specs=in_specs,
         out_specs=out_specs,
         out_shape=out_shape,
         scratch_shapes=scratch,
         input_output_aliases=aliases,
-        compiler_params=pltpu.CompilerParams(vmem_limit_bytes=20 * 1024 * 1024),
+        compiler_params=pltpu.CompilerParams(vmem_limit_bytes=28 * 1024 * 1024),
         cost_estimate=pl.CostEstimate(
             flops=6 * 10**9, bytes_accessed=4 * 2**20, transcendentals=HEADS * KEYS * ROWS
         ),
@@ -385,14 +402,12 @@
 def middle_kernel(pieces, *refs):
     out = refs[-1]
     chunk = jnp.sum(pieces[...].astype(f32), axis=0).astype(bf16)
+    a, b, c, d = refs[:-1]
     for z in range(NZ):
         out[z, :CHUNK] = chunk
-        for half in range(2):
-            a, b, c, d = refs[half * NX : half * NX + NX]
-            at = CHUNK + half * HALF_TILES
-            out[z, at : at + HALF_TILES] = (
-                (a[z].astype(f32) + b[z].astype(f32)) + (c[z].astype(f32) + d[z].astype(f32))
-            ).astype(bf16)
+        out[z, CHUNK:] = (
+            (a[z].astype(f32) + b[z].astype(f32)) + (c[z].astype(f32) + d[z].astype(f32))
+        ).astype(bf16)
 
 
 def middle(pieces, parts):
@@ -483,7 +498,7 @@
 
 
 def collect(parts):
-    parts = [p.reshape(NZ, HALF_TILES, 8, HD) for p in parts]
+    parts = [p.reshape(NZ, 2 * HALF_TILES, 8, HD) for p in parts]
     return [parts[0], shift(parts[1], -1), shift(parts[2], -2), shift(parts[3], -3)]
 
 
@@ -498,22 +513,22 @@
     message = project(
         span_beacon_count, span_document, state, adapter_down_weight.T, adapter_up_weight, frozen
     )
-    arrays = (query[0, 0], key[0, 0], value[0, 0], output_cotangent[0, 0], adapter_up_weight)
+    arrays = (query[0, 0], key[0, 0], value[0, 0], output_cotangent[0, 0])
+    arrays = [pltpu.with_memory_space_constraint(x, pltpu.HBM) for x in arrays]
+    arrays.append(adapter_up_weight)
     column = exchange(message, "z")
     boxes_a = spread(column[:, : LOW_TILE + 1])
     boxes_b = spread(column[:, LOW_TILE + 1 :])
     first = attend(0, (place, span_document, boundary), *arrays, boxes_a)
     low_total, bias, low_all = first[10:]
-    parts_a = collect(first[4:8])
-    second = attend(1, (place,), *arrays, boxes_b, (bias, low_all, low_total), first[:4])
-    parts_b = collect(second[4:8])
+    second = attend(1, (place,), *arrays, boxes_b, (bias, low_all, low_total), first[:8])
     attended, grad_query, grad_key, grad_value = second[:4]
-    low_part, parts_a = lax.optimization_barrier((second[10], parts_a))
-    low_parts = exchange(low_part.reshape(NZ * NX, 8, HD), ("z", "x"))
-    low_parts, parts_b = lax.optimization_barrier((low_parts, parts_b))
+    parts = collect(second[4:8])
+    low_parts = exchange(second[10].reshape(NZ * NX, 8, HD), ("z", "x"))
     keep, send = factor(place, span_beacon_count, low_parts, state, first[8:10] + second[8:10])
+    send, parts = lax.optimization_barrier((send, parts))
     pieces = (keep.astype(f32) + swap(send).astype(f32)).astype(bf16)
-    both = exchange(middle(exchange(pieces, PLANE), parts_a + parts_b), "z")
+    both = exchange(middle(exchange(pieces, PLANE), parts), "z")
     cache_gradient, chunk = close(span_beacon_count, both)
     mine = exchange(chunk, PLANE)
     adapter_gradient = unpack(place, mine, swap(mine))

time: 143 us -> 138 us (0.965)
  blocking collectives: 67.5 us -> 87.6 us
  starting transfers between devices: 27.1 us -> 14.2 us
  waiting for transfers between devices: 20.1 us -> 12.3 us
  local copies, waits for them, and re-layouts: 3.84 us -> 0.06 us
    all_to_all x4 -> x5, blocking collectives: 67.5 us -> 87.6 us  [exchange(): return lax.all_to_all(x, axes, 0, 0, tiled=True)]
    all_to_all x1 -> x0, waiting for transfers between devices: 8.1 us -> none  [exchange(): return lax.all_to_all(x, axes, 0, 0, tiled=True)]
    all_to_all x1 -> x0, starting transfers between devices: 5.57 us -> none  [exchange(): return lax.all_to_all(x, axes, 0, 0, tiled=True)]
    ppermute x12 -> x9, starting transfers between devices: 13.1 us -> 8.58 us  [shift(): return lax.ppermute(x, 'x', [(i, (i + by) % NX) for i in range(NX)])]
    ppermute x2, starting transfers between devices: 8.51 us -> 5.63 us  [swap(): return lax.ppermute(x, 'core', [(0, 1), (1, 0)])]
    unnamed x28 -> x10, local copies, waits for them, and re-layouts: 2.89 us -> 0.03 us
    ppermute x12 -> x9, waiting for transfers between devices: 9.32 us -> 9.62 us  [shift(): return lax.ppermute(x, 'x', [(i, (i + by) % NX) for i in range(NX)])]
  transfers between devices with their start and end apart: 15 -> 11, of which waited for: 6 -> 5; matrix products, arithmetic and copies ran while one was open for 1% -> 0% of each run, Pallas kernels for 11% -> 6%
where the time goes in v7:
time: 138 us; the launch traced here: 137 us
  blocking collectives  87.6 us (63%)
  Pallas kernels  22.1 us (16%)
  starting transfers between devices  14.2 us (10%)
  waiting for transfers between devices  12.3 us (9%)
    all_to_all x5, blocking collectives, exchange(): return lax.all_to_all(x, axes, 0, 0, tiled=True)  87.6 us
    pallas_call x2, Pallas kernels, attend(): pl.pallas_call((first_kernel, second_kernel)[half], grid=(HEADS // STEP,)...  14.8 us
    ppermute x9, waiting for transfers between devices, shift(): return lax.ppermute(x, 'x', [(i, (i + by) % NX) for i in range(NX)])  9.62 us
    ppermute x9, starting transfers between devices, shift(): return lax.ppermute(x, 'x', [(i, (i + by) % NX) for i in range(NX)])  8.58 us
    ppermute x2, starting transfers between devices, swap(): return lax.ppermute(x, 'core', [(0, 1), (1, 0)])  5.63 us
  transfers between devices with their start and end apart: 11, of which 5 were waited for; matrix products, arithmetic and copies ran while one was open for 0% of the time, Pallas kernels for 6%

profile of v7, /device:TPU:1, one launch (start us, length us, event | category | flops | bytes accessed | tf_op | source)
XLA Modules:
  0.0 137.3 jit_solution(5965661040949321047)
XLA Ops:
  0.7 2.7 %project.1 = bf16[8,25,8,128]{3,2,1,0:T(8,128)(2,1)} custom-call(s32[1,1,2]{2,1,0:T(1,128)} %counts.5, s32[1,1,2]{2,1,0:T(1,128)} %refs_1_.1, bf16[16,4096]{1,0:T(8,128)(2,1)} %bitcast.20, bf16[64,4096]{1,0:T(8,128)(2,1)} %bitcast.27, bf16[64,2048]{1,0:T(8,128)(2,1)} %refs_6_.1, bf16[16,2048]{1,0:T(8,128)(2,1)} %bitcast.28), custom_call_target="tpu_custom_call" | custom-call | tf_op jit(solution)/shard_map/project/pallas_call | solution.py:87
  3.4 22.8 %all_to_all.25 = bf16[8,25,8,128]{3,2,1,0:T(8,128)(2,1)S(1)} all-to-all(bf16[8,25,8,128]{3,2,1,0:T(8,128)(2,1)} %project.1), channel_id=1, replica_groups=mesh['z'=8,'x'=4,'y'=4,'core'=2] {'z'}, dimensions={0} | all-to-all | bytes 819200 | tf_op jit(solution)/shard_map/all_to_all | solution.py:485
  26.2 2.6 %collective-permute-start.5 = (bf16[8,13,8,128]{3,2,1,0:T(8,128)(2,1)S(1)}, bf16[8,13,8,128]{3,2,1,0:T(8,128)(2,1)S(1)}, u32[]{:S(2)}, u32[]{:S(2)}) collective-permute-start(bf16[8,13,8,128]{3,2,1,0:T(8,128)(2,1)S(1)} %slice.9.refs_9_), channel_id=1, source_target_pairs={{0,24},{8,0},{16,8},{24,16},{1,25},{9,1},{17,9},{25,17},{2,26},{10... | collective-permute-start | bytes 638984 | tf_op jit(solution)/shard_map/ppermute | solution.py:489
  28.7 0.5 collective-permute-start.4
  29.2 0.6 collective-permute-start.3
  29.9 2.1 %collective-permute-start.2 = (bf16[8,12,8,128]{3,2,1,0:T(8,128)(2,1)S(1)}, bf16[8,12,8,128]{3,2,1,0:T(8,128)(2,1)S(1)}, u32[]{:S(2)}, u32[]{:S(2)}) collective-permute-start(bf16[8,12,8,128]{3,2,1,0:T(8,128)(2,1)S(1)} %slice.8.refs_7_), channel_id=1, source_target_pairs={{0,24},{8,0},{16,8},{24,16},{1,25},{9,1},{17,9},{25,17},{2,26},{10... | collective-permute-start | bytes 589832 | tf_op jit(solution)/shard_map/ppermute | solution.py:489
  32.1 1.2 collective-permute-start.1
  33.3 0.7 collective-permute-done.5.refs_12_
  34.0 1.0 collective-permute-done.4.refs_11_
  35.0 7.9 %collective-permute-done.3.refs_10_ = bf16[8,13,8,128]{3,2,1,0:T(8,128)(2,1)S(1)} collective-permute-done((bf16[8,13,8,128]{3,2,1,0:T(8,128)(2,1)S(1)}, bf16[8,13,8,128]{3,2,1,0:T(8,128)(2,1)S(1)}, u32[]{:S(2)}, u32[]{:S(2)}) %collective-permute-start.3) | collective-permute-done | bytes 213024 | tf_op jit(solution)/shard_map/ppermute | solution.py:489
  42.9 7.5 %attend_first.1 = (bf16[2,64,4096]{2,1,0:T(8,128)(2,1)}, bf16[2,64,4096]{2,1,0:T(8,128)(2,1)}, bf16[2,64,1024]{2,1,0:T(8,128)(2,1)}, bf16[2,64,1024]{2,1,0:T(8,1...) custom-call(s32[3]{0:T(128)S(1)} %pad_add_fusion.refs_0_.place, ...), custom_call_target="tpu_custom_call" | custom-call | flops 6000000000 | bytes 4194304 | tf_op jit(solution)/shard_map/attend_first/pallas_call | solution.py:345
  50.5 7.3 %attend_second.1 = (bf16[2,64,4096]{2,1,0:T(8,128)(2,1)}, bf16[2,64,4096]{2,1,0:T(8,128)(2,1)}, bf16[2,64,1024]{2,1,0:T(8,128)(2,1)}, bf16[2,64,1024]{2,1,0:T(8,...) custom-call(s32[3]{0:T(128)S(1)} %pad_add_fusion.refs_0_.place, ...), custom_call_target="tpu_custom_call", output_to_operand_aliasing={{0}: (14, {}), {1}: (15, {}), {2}: (16, {}), {3}: (17, {}),... | custom-call | flops 6000000000 | bytes 4194304 | tf_op jit(solution)/shard_map/attend_second/pallas_call | solution.py:345
  58.0 1.4 collective-permute-start.8
  59.3 20.3 %all_to_all.26.low_parts = bf16[32,8,128]{2,1,0:T(8,128)(2,1)S(1)} all-to-all(bf16[32,8,128]{2,1,0:T(8,128)(2,1)S(1)} %bitcast.23), channel_id=1, replica_groups=mesh['z'=8,'x'=4,'y'=4,'core'=2] {'z','x'}, dimensions={0} | all-to-all | bytes 131072 | tf_op jit(solution)/shard_map/all_to_all | solution.py:485
  79.6 1.2 factor.1
  80.9 0.6 collective-permute-start.9
  81.5 1.3 collective-permute-done.9
  83.0 13.8 %all_to_all.27.pieces = bf16[16,12,8,128]{3,2,1,0:T(8,128)(2,1)S(1)} all-to-all(bf16[16,12,8,128]{3,2,1,0:T(8,128)(2,1)S(1)} %add_convert_fusion), channel_id=1, replica_groups=mesh['z'=8,'x'=4,'y'=4,'core'=2] {'x','y'}, dimensions={0} | all-to-all | bytes 786432 | tf_op jit(solution)/shard_map/all_to_all | solution.py:485
  97.0 19.2 %all_to_all.28.parts = bf16[8,36,8,128]{3,2,1,0:T(8,128)(2,1)S(1)} all-to-all(bf16[8,36,8,128]{3,2,1,0:T(8,128)(2,1)S(1)} %middle.1), channel_id=1, replica_groups=mesh['z'=8,'x'=4,'y'=4,'core'=2] {'z'}, dimensions={0} | all-to-all | bytes 1179648 | tf_op jit(solution)/shard_map/all_to_all | solution.py:485
  116.2 1.4 %close.1 = (bf16[16,2048]{1,0:T(8,128)(2,1)}, bf16[16,12,8,128]{3,2,1,0:T(8,128)(2,1)S(1)}) custom-call(s32[1,1,2]{2,1,0:T(1,128)S(1)} %copy-done.2, bf16[8,36,8,128]{3,2,1,0:T(8,128)(2,1)S(1)} %all_to_all.28.parts), custom_call_target="tpu_custom_call" | custom-call | tf_op jit(solution)/shard_map/close/pallas_call | solution.py:450
  117.6 11.6 %all_to_all.29.mine = bf16[16,12,8,128]{3,2,1,0:T(8,128)(2,1)S(1)} all-to-all(bf16[16,12,8,128]{3,2,1,0:T(8,128)(2,1)S(1)} %get-tuple-element.71), channel_id=1, replica_groups=mesh['z'=8,'x'=4,'y'=4,'core'=2] {'x','y'}, dimensions={0} | all-to-all | bytes 786432 | tf_op jit(solution)/shard_map/all_to_all | solution.py:485
  129.2 5.0 %collective-permute-start.10 = (bf16[16,12,8,128]{3,2,1,0:T(8,128)(2,1)S(1)}, bf16[16,12,8,128]{3,2,1,0:T(8,128)(2,1)S(1)}, u32[]{:S(2)}, u32[]{:S(2)}) collective-permute-start(bf16[16,12,8,128]{3,2,1,0:T(8,128)(2,1)S(1)} %all_to_all.29.mine), channel_id=1, source_target_pairs={{0,1},{1,0},{2,3},{3,2},{4,5},{5,4},{6,7},{7,6},{8,9},{9,8},{10,11... | collective-permute-start | bytes 1179656 | tf_op jit(solution)/shard_map/ppermute | solution.py:493
  134.2 1.3 collective-permute-done.10.other
  135.5 1.8 %unpack.1 = f32[64,6144]{1,0:T(8,128)} custom-call(s32[3]{0:T(128)S(1)} %pad_add_fusion.refs_0_.place, bf16[16,12,8,128]{3,2,1,0:T(8,128)(2,1)S(1)} %all_to_all.29.mine, bf16[16,12,8,128]{3,2,1,0:T(8,128)(2,1)S(1)} %collective-permute-done.10.other), custom_call_target="tpu_custom_call" | custom-call | tf_op jit(solution)/shard_map/unpack/pallas_call | solution.py:474
  (24 shorter events, 0.7 us)
Async XLA Ops:
  0.6 42.3 %copy-start.1 = (bf16[64,2048]{1,0:T(8,128)(2,1)S(1)}, bf16[64,2048]{1,0:T(8,128)(2,1)}, u32[]{:S(2)}) copy-start(bf16[64,2048]{1,0:T(8,128)(2,1)} %refs_6_.1) | copy-start | bytes 786436
  0.6 42.3 %copy-start.3 = (s32[1,1,2]{2,1,0:T(1,128)S(1)}, s32[1,1,2]{2,1,0:T(1,128)}, u32[]{:S(2)}) copy-start(s32[1,1,2]{2,1,0:T(1,128)} %refs_1_.1) | copy-start | bytes 28
  0.7 42.3 %copy-start.4 = (s32[1,1,2]{2,1,0:T(1,128)S(1)}, s32[1,1,2]{2,1,0:T(1,128)}, u32[]{:S(2)}) copy-start(s32[1,1,2]{2,1,0:T(1,128)} %refs_2_.1) | copy-start | bytes 28
  26.2 7.8 %collective-permute-start.5 = (bf16[8,13,8,128]{3,2,1,0:T(8,128)(2,1)S(1)}, bf16[8,13,8,128]{3,2,1,0:T(8,128)(2,1)S(1)}, u32[]{:S(2)}, u32[]{:S(2)}) collective-permute-start(bf16[8,13,8,128]{3,2,1,0:T(8,128)(2,1)S(1)} %slice.9.refs_9_), channel_id=1, source_target_pairs={{0,24},{8,0},{16,8},{24,16},{1,25},{9,1},{17,9},{25,17},{2,26},{10... | collective-permute-start | bytes 638984 | tf_op jit(solution)/shard_map/ppermute | solution.py:489
  28.7 6.3 %collective-permute-start.4 = (bf16[8,13,8,128]{3,2,1,0:T(8,128)(2,1)S(1)}, bf16[8,13,8,128]{3,2,1,0:T(8,128)(2,1)S(1)}, u32[]{:S(2)}, u32[]{:S(2)}) collective-permute-start(bf16[8,13,8,128]{3,2,1,0:T(8,128)(2,1)S(1)} %slice.9.refs_9_), channel_id=1, source_target_pairs={{0,16},{8,24},{16,0},{24,8},{1,17},{9,25},{17,1},{25,9},{2,18},{10... | collective-permute-start | bytes 638984 | tf_op jit(solution)/shard_map/ppermute | solution.py:489
  29.2 13.7 %collective-permute-start.3 = (bf16[8,13,8,128]{3,2,1,0:T(8,128)(2,1)S(1)}, bf16[8,13,8,128]{3,2,1,0:T(8,128)(2,1)S(1)}, u32[]{:S(2)}, u32[]{:S(2)}) collective-permute-start(bf16[8,13,8,128]{3,2,1,0:T(8,128)(2,1)S(1)} %slice.9.refs_9_), channel_id=1, source_target_pairs={{0,8},{8,16},{16,24},{24,0},{1,9},{9,17},{17,25},{25,1},{2,10},{10... | collective-permute-start | bytes 638984 | tf_op jit(solution)/shard_map/ppermute | solution.py:489
  29.9 20.5 %collective-permute-start.2 = (bf16[8,12,8,128]{3,2,1,0:T(8,128)(2,1)S(1)}, bf16[8,12,8,128]{3,2,1,0:T(8,128)(2,1)S(1)}, u32[]{:S(2)}, u32[]{:S(2)}) collective-permute-start(bf16[8,12,8,128]{3,2,1,0:T(8,128)(2,1)S(1)} %slice.8.refs_7_), channel_id=1, source_target_pairs={{0,24},{8,0},{16,8},{24,16},{1,25},{9,1},{17,9},{25,17},{2,26},{10... | collective-permute-start | bytes 589832 | tf_op jit(solution)/shard_map/ppermute | solution.py:489
  32.1 18.4 %collective-permute-start.1 = (bf16[8,12,8,128]{3,2,1,0:T(8,128)(2,1)S(1)}, bf16[8,12,8,128]{3,2,1,0:T(8,128)(2,1)S(1)}, u32[]{:S(2)}, u32[]{:S(2)}) collective-permute-start(bf16[8,12,8,128]{3,2,1,0:T(8,128)(2,1)S(1)} %slice.8.refs_7_), channel_id=1, source_target_pairs={{0,16},{8,24},{16,0},{24,8},{1,17},{9,25},{17,1},{25,9},{2,18},{10... | collective-permute-start | bytes 589832 | tf_op jit(solution)/shard_map/ppermute | solution.py:489
  34.0 16.5 %collective-permute-start = (bf16[8,12,8,128]{3,2,1,0:T(8,128)(2,1)S(1)}, bf16[8,12,8,128]{3,2,1,0:T(8,128)(2,1)S(1)}, u32[]{:S(2)}, u32[]{:S(2)}) collective-permute-start(bf16[8,12,8,128]{3,2,1,0:T(8,128)(2,1)S(1)} %slice.8.refs_7_), channel_id=1, source_target_pairs={{0,8},{8,16},{16,24},{24,0},{1,9},{9,17},{17,25},{25,1},{2,10},{10... | collective-permute-start | bytes 589832 | tf_op jit(solution)/shard_map/ppermute | solution.py:489
  50.5 29.1 %copy-start = (bf16[1,1,2,8,4096]{4,3,2,1,0:T(8,128)(2,1)S(1)}, bf16[1,1,2,8,4096]{4,3,2,1,0:T(8,128)(2,1)}, u32[]{:S(2)}) copy-start(bf16[1,1,2,8,4096]{4,3,2,1,0:T(8,128)(2,1)} %param.14) | copy-start | bytes 393220
  50.5 29.1 %copy-start.2 = (s32[1,1,2]{2,1,0:T(1,128)S(1)}, s32[1,1,2]{2,1,0:T(1,128)}, u32[]{:S(2)}) copy-start(s32[1,1,2]{2,1,0:T(1,128)} %counts.5) | copy-start | bytes 28
  57.8 23.0 %collective-permute-start.6 = (bf16[8,24,8,128]{3,2,1,0:T(8,128)(2,1)S(1)}, bf16[8,24,8,128]{3,2,1,0:T(8,128)(2,1)S(1)}, u32[]{:S(2)}, u32[]{:S(2)}) collective-permute-start(bf16[8,24,8,128]{3,2,1,0:T(8,128)(2,1)S(1)} %bitcast.24), channel_id=1, source_target_pairs={{0,24},{8,0},{16,8},{24,16},{1,25},{9,1},{17,9},{25,17},{2,26},{10... | collective-permute-start | bytes 1179656 | tf_op jit(solution)/shard_map/ppermute | solution.py:489
  57.9 23.0 %collective-permute-start.7 = (bf16[8,24,8,128]{3,2,1,0:T(8,128)(2,1)S(1)}, bf16[8,24,8,128]{3,2,1,0:T(8,128)(2,1)S(1)}, u32[]{:S(2)}, u32[]{:S(2)}) collective-permute-start(bf16[8,24,8,128]{3,2,1,0:T(8,128)(2,1)S(1)} %bitcast.25), channel_id=1, source_target_pairs={{0,16},{8,24},{16,0},{24,8},{1,17},{9,25},{17,1},{25,9},{2,18},{10... | collective-permute-start | bytes 1179656 | tf_op jit(solution)/shard_map/ppermute | solution.py:489
  58.0 22.9 %collective-permute-start.8 = (bf16[8,24,8,128]{3,2,1,0:T(8,128)(2,1)S(1)}, bf16[8,24,8,128]{3,2,1,0:T(8,128)(2,1)S(1)}, u32[]{:S(2)}, u32[]{:S(2)}) collective-permute-start(bf16[8,24,8,128]{3,2,1,0:T(8,128)(2,1)S(1)} %bitcast.26), channel_id=1, source_target_pairs={{0,8},{8,16},{16,24},{24,0},{1,9},{9,17},{17,25},{25,1},{2,10},{10... | collective-permute-start | bytes 1179656 | tf_op jit(solution)/shard_map/ppermute | solution.py:489
  80.9 2.0 %collective-permute-start.9 = (bf16[16,12,8,128]{3,2,1,0:T(8,128)(2,1)S(1)}, bf16[16,12,8,128]{3,2,1,0:T(8,128)(2,1)S(1)}, u32[]{:S(2)}, u32[]{:S(2)}) collective-permute-start(bf16[16,12,8,128]{3,2,1,0:T(8,128)(2,1)S(1)} %get-tuple-element.65), channel_id=1, source_target_pairs={{0,1},{1,0},{2,3},{3,2},{4,5},{5,4},{6,7},{7,6},{8,9},{9,8},{10,11... | collective-permute-start | bytes 1179656 | tf_op jit(solution)/shard_map/ppermute | solution.py:493
  129.2 6.3 %collective-permute-start.10 = (bf16[16,12,8,128]{3,2,1,0:T(8,128)(2,1)S(1)}, bf16[16,12,8,128]{3,2,1,0:T(8,128)(2,1)S(1)}, u32[]{:S(2)}, u32[]{:S(2)}) collective-permute-start(bf16[16,12,8,128]{3,2,1,0:T(8,128)(2,1)S(1)} %all_to_all.29.mine), channel_id=1, source_target_pairs={{0,1},{1,0},{2,3},{3,2},{4,5},{5,4},{6,7},{7,6},{8,9},{9,8},{10,11... | collective-permute-start | bytes 1179656 | tf_op jit(solution)/shard_map/ppermute | solution.py:493

commit v8 on v7

--- a/solution.py
+++ b/solution.py
@@ -421,16 +421,30 @@
     )(pieces, *parts)
 
 
-def close_kernel(counts, parts, cache_out, out):
-    pick = selection(counts[0, 0, 0], counts[0, 0, 1]).astype(bf16)
-    total = jnp.sum(parts[...].astype(f32), axis=0)
-    chunk = total[:CHUNK].astype(bf16)
+def spread_kernel(parts, out):
+    chunk = jnp.sum(parts[:, :CHUNK].astype(f32), axis=0).astype(bf16)
     for i in range(CHUNKS):
         out[i] = chunk
+
+
+def spread_chunk(parts):
+    return pl.pallas_call(
+        spread_kernel,
+        in_specs=[VMEM],
+        out_specs=VMEM,
+        out_shape=jax.ShapeDtypeStruct((CHUNKS, CHUNK, 8, HD), bf16),
+        compiler_params=SMALL,
+        name="spread_chunk",
+    )(parts)
+
+
+def cache_kernel(counts, parts, cache_out):
+    pick = selection(counts[0, 0, 0], counts[0, 0, 1]).astype(bf16)
+    total = jnp.sum(parts[:, CHUNK:].astype(f32), axis=0)
     sub = lax.broadcasted_iota(jnp.int32, (8, HD), 0)
     top_keys, top_values, rest_keys, rest_values = [], [], [], []
     for h in range(KVH):
-        at = CHUNK + h // HEADS * HALF_TILES + h % HEADS
+        at = h // HEADS * HALF_TILES + h % HEADS
         top_keys.append(total[at])
         top_values.append(total[at + HEADS])
         both = total[at + 2 * HEADS]
@@ -446,17 +460,14 @@
     cache_out[...] = dot(pick, compact, ((0,), (0,))).astype(bf16)
 
 
-def close(counts, parts):
-    return pl.pallas_call(
-        close_kernel,
+def cache(counts, parts):
+    return pl.pallas_call(
+        cache_kernel,
         in_specs=[SMEM, VMEM],
-        out_specs=[VMEM, VMEM],
-        out_shape=[
-            jax.ShapeDtypeStruct((16, 2 * KEY_FEATURES), bf16),
-            jax.ShapeDtypeStruct((CHUNKS, CHUNK, 8, HD), bf16),
-        ],
+        out_specs=VMEM,
+        out_shape=jax.ShapeDtypeStruct((16, 2 * KEY_FEATURES), bf16),
         compiler_params=SMALL,
-        name="close",
+        name="cache",
     )(counts, parts)
 
 
@@ -529,8 +540,8 @@
     send, parts = lax.optimization_barrier((send, parts))
     pieces = (keep.astype(f32) + swap(send).astype(f32)).astype(bf16)
     both = exchange(middle(exchange(pieces, PLANE), parts), "z")
-    cache_gradient, chunk = close(span_beacon_count, both)
-    mine = exchange(chunk, PLANE)
+    mine = exchange(spread_chunk(both), PLANE)
+    cache_gradient = cache(span_beacon_count, both)
     adapter_gradient = unpack(place, mine, swap(mine))
     return (
         attended[None, None],

time: 138 us -> 136 us (0.986)
  transfers between devices with their start and end apart: 11 -> 11, of which waited for: 5 -> 4; matrix products, arithmetic and copies ran while one was open for 0% -> 0% of each run, Pallas kernels for 6% -> 7%
where the time goes in v8:
time: 136 us
  blocking collectives  87.6 us (64%)
  Pallas kernels  22.1 us (16%)
  starting transfers between devices  14.2 us (10%)
  waiting for transfers between devices  11 us (8%)
    all_to_all x5, blocking collectives, exchange(): return lax.all_to_all(x, axes, 0, 0, tiled=True)  87.6 us
    pallas_call x2, Pallas kernels, attend(): pl.pallas_call((first_kernel, second_kernel)[half], grid=(HEADS // STEP,)...  14.8 us
    ppermute x9, waiting for transfers between devices, shift(): return lax.ppermute(x, 'x', [(i, (i + by) % NX) for i in range(NX)])  9.62 us
    ppermute x9, starting transfers between devices, shift(): return lax.ppermute(x, 'x', [(i, (i + by) % NX) for i in range(NX)])  8.58 us
    ppermute x2, starting transfers between devices, swap(): return lax.ppermute(x, 'core', [(0, 1), (1, 0)])  5.63 us
  transfers between devices with their start and end apart: 11, of which 4 were waited for; matrix products, arithmetic and copies ran while one was open for 0% of the time, Pallas kernels for 7%

profile of v8, /device:TPU:1, one launch (start us, length us, event | category | flops | bytes accessed | tf_op | source)
XLA Modules:
  0.0 136.0 jit_solution(8980813837193503684)
XLA Ops:
  0.7 2.7 %project.1 = bf16[8,25,8,128]{3,2,1,0:T(8,128)(2,1)} custom-call(s32[1,1,2]{2,1,0:T(1,128)} %counts.5, s32[1,1,2]{2,1,0:T(1,128)} %refs_1_.1, bf16[16,4096]{1,0:T(8,128)(2,1)} %bitcast.20, bf16[64,4096]{1,0:T(8,128)(2,1)} %bitcast.27, bf16[64,2048]{1,0:T(8,128)(2,1)} %refs_6_.1, bf16[16,2048]{1,0:T(8,128)(2,1)} %bitcast.28), custom_call_target="tpu_custom_call" | custom-call | tf_op jit(solution)/shard_map/project/pallas_call | solution.py:87
  3.4 22.8 %all_to_all.25 = bf16[8,25,8,128]{3,2,1,0:T(8,128)(2,1)S(1)} all-to-all(bf16[8,25,8,128]{3,2,1,0:T(8,128)(2,1)} %project.1), channel_id=1, replica_groups=mesh['z'=8,'x'=4,'y'=4,'core'=2] {'z'}, dimensions={0} | all-to-all | bytes 819200 | tf_op jit(solution)/shard_map/all_to_all | solution.py:496
  26.2 2.6 %collective-permute-start.5 = (bf16[8,13,8,128]{3,2,1,0:T(8,128)(2,1)S(1)}, bf16[8,13,8,128]{3,2,1,0:T(8,128)(2,1)S(1)}, u32[]{:S(2)}, u32[]{:S(2)}) collective-permute-start(bf16[8,13,8,128]{3,2,1,0:T(8,128)(2,1)S(1)} %slice.9.refs_9_), channel_id=1, source_target_pairs={{0,24},{8,0},{16,8},{24,16},{1,25},{9,1},{17,9},{25,17},{2,26},{10... | collective-permute-start | bytes 638984 | tf_op jit(solution)/shard_map/ppermute | solution.py:500
  28.7 0.5 collective-permute-start.4
  29.2 0.6 collective-permute-start.3
  29.9 2.1 %collective-permute-start.2 = (bf16[8,12,8,128]{3,2,1,0:T(8,128)(2,1)S(1)}, bf16[8,12,8,128]{3,2,1,0:T(8,128)(2,1)S(1)}, u32[]{:S(2)}, u32[]{:S(2)}) collective-permute-start(bf16[8,12,8,128]{3,2,1,0:T(8,128)(2,1)S(1)} %slice.8.refs_7_), channel_id=1, source_target_pairs={{0,24},{8,0},{16,8},{24,16},{1,25},{9,1},{17,9},{25,17},{2,26},{10... | collective-permute-start | bytes 589832 | tf_op jit(solution)/shard_map/ppermute | solution.py:500
  32.1 1.2 collective-permute-start.1
  33.3 0.7 collective-permute-done.5.refs_12_
  34.0 1.0 collective-permute-done.4.refs_11_
  35.0 7.9 %collective-permute-done.3.refs_10_ = bf16[8,13,8,128]{3,2,1,0:T(8,128)(2,1)S(1)} collective-permute-done((bf16[8,13,8,128]{3,2,1,0:T(8,128)(2,1)S(1)}, bf16[8,13,8,128]{3,2,1,0:T(8,128)(2,1)S(1)}, u32[]{:S(2)}, u32[]{:S(2)}) %collective-permute-start.3) | collective-permute-done | bytes 213024 | tf_op jit(solution)/shard_map/ppermute | solution.py:500
  42.9 7.5 %attend_first.1 = (bf16[2,64,4096]{2,1,0:T(8,128)(2,1)}, bf16[2,64,4096]{2,1,0:T(8,128)(2,1)}, bf16[2,64,1024]{2,1,0:T(8,128)(2,1)}, bf16[2,64,1024]{2,1,0:T(8,1...) custom-call(s32[3]{0:T(128)S(1)} %pad_add_fusion.refs_0_.place, ...), custom_call_target="tpu_custom_call" | custom-call | flops 6000000000 | bytes 4194304 | tf_op jit(solution)/shard_map/attend_first/pallas_call | solution.py:345
  50.5 7.3 %attend_second.1 = (bf16[2,64,4096]{2,1,0:T(8,128)(2,1)}, bf16[2,64,4096]{2,1,0:T(8,128)(2,1)}, bf16[2,64,1024]{2,1,0:T(8,128)(2,1)}, bf16[2,64,1024]{2,1,0:T(8,...) custom-call(s32[3]{0:T(128)S(1)} %pad_add_fusion.refs_0_.place, ...), custom_call_target="tpu_custom_call", output_to_operand_aliasing={{0}: (14, {}), {1}: (15, {}), {2}: (16, {}), {3}: (17, {}),... | custom-call | flops 6000000000 | bytes 4194304 | tf_op jit(solution)/shard_map/attend_second/pallas_call | solution.py:345
  58.0 1.4 collective-permute-start.8
  59.3 20.3 %all_to_all.26.low_parts = bf16[32,8,128]{2,1,0:T(8,128)(2,1)S(1)} all-to-all(bf16[32,8,128]{2,1,0:T(8,128)(2,1)S(1)} %bitcast.23), channel_id=1, replica_groups=mesh['z'=8,'x'=4,'y'=4,'core'=2] {'z','x'}, dimensions={0} | all-to-all | bytes 131072 | tf_op jit(solution)/shard_map/all_to_all | solution.py:496
  79.6 1.2 factor.1
  80.9 0.6 collective-permute-start.9
  81.5 1.3 collective-permute-done.9
  83.0 13.8 %all_to_all.27.pieces = bf16[16,12,8,128]{3,2,1,0:T(8,128)(2,1)S(1)} all-to-all(bf16[16,12,8,128]{3,2,1,0:T(8,128)(2,1)S(1)} %add_convert_fusion), channel_id=1, replica_groups=mesh['z'=8,'x'=4,'y'=4,'core'=2] {'x','y'}, dimensions={0} | all-to-all | bytes 786432 | tf_op jit(solution)/shard_map/all_to_all | solution.py:496
  96.7 0.2 middle.1
  97.0 19.2 %all_to_all.28.parts = bf16[8,36,8,128]{3,2,1,0:T(8,128)(2,1)S(1)} all-to-all(bf16[8,36,8,128]{3,2,1,0:T(8,128)(2,1)S(1)} %middle.1), channel_id=1, replica_groups=mesh['z'=8,'x'=4,'y'=4,'core'=2] {'z'}, dimensions={0} | all-to-all | bytes 1179648 | tf_op jit(solution)/shard_map/all_to_all | solution.py:496
  116.2 11.6 %all_to_all.29.mine = bf16[16,12,8,128]{3,2,1,0:T(8,128)(2,1)S(1)} all-to-all(bf16[16,12,8,128]{3,2,1,0:T(8,128)(2,1)S(1)} %spread_chunk.1), channel_id=1, replica_groups=mesh['z'=8,'x'=4,'y'=4,'core'=2] {'x','y'}, dimensions={0} | all-to-all | bytes 786432 | tf_op jit(solution)/shard_map/all_to_all | solution.py:496
  127.8 5.0 %collective-permute-start.10 = (bf16[16,12,8,128]{3,2,1,0:T(8,128)(2,1)S(1)}, bf16[16,12,8,128]{3,2,1,0:T(8,128)(2,1)S(1)}, u32[]{:S(2)}, u32[]{:S(2)}) collective-permute-start(bf16[16,12,8,128]{3,2,1,0:T(8,128)(2,1)S(1)} %all_to_all.29.mine), channel_id=1, source_target_pairs={{0,1},{1,0},{2,3},{3,2},{4,5},{5,4},{6,7},{7,6},{8,9},{9,8},{10,11... | collective-permute-start | bytes 1179656 | tf_op jit(solution)/shard_map/ppermute | solution.py:504
  132.8 1.4 %cache.1 = bf16[16,2048]{1,0:T(8,128)(2,1)} custom-call(s32[1,1,2]{2,1,0:T(1,128)S(1)} %copy-done.2, bf16[8,36,8,128]{3,2,1,0:T(8,128)(2,1)S(1)} %all_to_all.28.parts), custom_call_target="tpu_custom_call" | custom-call | tf_op jit(solution)/shard_map/cache/pallas_call | solution.py:464
  134.2 1.8 %unpack.1 = f32[64,6144]{1,0:T(8,128)} custom-call(s32[3]{0:T(128)S(1)} %pad_add_fusion.refs_0_.place, bf16[16,12,8,128]{3,2,1,0:T(8,128)(2,1)S(1)} %all_to_all.29.mine, bf16[16,12,8,128]{3,2,1,0:T(8,128)(2,1)S(1)} %collective-permute-done.10.other), custom_call_target="tpu_custom_call" | custom-call | tf_op jit(solution)/shard_map/unpack/pallas_call | solution.py:485
  (25 shorter events, 0.4 us)
Async XLA Ops:
  0.6 42.3 %copy-start.1 = (bf16[64,2048]{1,0:T(8,128)(2,1)S(1)}, bf16[64,2048]{1,0:T(8,128)(2,1)}, u32[]{:S(2)}) copy-start(bf16[64,2048]{1,0:T(8,128)(2,1)} %refs_6_.1) | copy-start | bytes 786436
  0.6 42.3 %copy-start.3 = (s32[1,1,2]{2,1,0:T(1,128)S(1)}, s32[1,1,2]{2,1,0:T(1,128)}, u32[]{:S(2)}) copy-start(s32[1,1,2]{2,1,0:T(1,128)} %refs_1_.1) | copy-start | bytes 28
  0.7 42.3 %copy-start.4 = (s32[1,1,2]{2,1,0:T(1,128)S(1)}, s32[1,1,2]{2,1,0:T(1,128)}, u32[]{:S(2)}) copy-start(s32[1,1,2]{2,1,0:T(1,128)} %refs_2_.1) | copy-start | bytes 28
  26.2 7.8 %collective-permute-start.5 = (bf16[8,13,8,128]{3,2,1,0:T(8,128)(2,1)S(1)}, bf16[8,13,8,128]{3,2,1,0:T(8,128)(2,1)S(1)}, u32[]{:S(2)}, u32[]{:S(2)}) collective-permute-start(bf16[8,13,8,128]{3,2,1,0:T(8,128)(2,1)S(1)} %slice.9.refs_9_), channel_id=1, source_target_pairs={{0,24},{8,0},{16,8},{24,16},{1,25},{9,1},{17,9},{25,17},{2,26},{10... | collective-permute-start | bytes 638984 | tf_op jit(solution)/shard_map/ppermute | solution.py:500
  28.7 6.3 %collective-permute-start.4 = (bf16[8,13,8,128]{3,2,1,0:T(8,128)(2,1)S(1)}, bf16[8,13,8,128]{3,2,1,0:T(8,128)(2,1)S(1)}, u32[]{:S(2)}, u32[]{:S(2)}) collective-permute-start(bf16[8,13,8,128]{3,2,1,0:T(8,128)(2,1)S(1)} %slice.9.refs_9_), channel_id=1, source_target_pairs={{0,16},{8,24},{16,0},{24,8},{1,17},{9,25},{17,1},{25,9},{2,18},{10... | collective-permute-start | bytes 638984 | tf_op jit(solution)/shard_map/ppermute | solution.py:500
  29.2 13.7 %collective-permute-start.3 = (bf16[8,13,8,128]{3,2,1,0:T(8,128)(2,1)S(1)}, bf16[8,13,8,128]{3,2,1,0:T(8,128)(2,1)S(1)}, u32[]{:S(2)}, u32[]{:S(2)}) collective-permute-start(bf16[8,13,8,128]{3,2,1,0:T(8,128)(2,1)S(1)} %slice.9.refs_9_), channel_id=1, source_target_pairs={{0,8},{8,16},{16,24},{24,0},{1,9},{9,17},{17,25},{25,1},{2,10},{10... | collective-permute-start | bytes 638984 | tf_op jit(solution)/shard_map/ppermute | solution.py:500
  29.9 20.5 %collective-permute-start.2 = (bf16[8,12,8,128]{3,2,1,0:T(8,128)(2,1)S(1)}, bf16[8,12,8,128]{3,2,1,0:T(8,128)(2,1)S(1)}, u32[]{:S(2)}, u32[]{:S(2)}) collective-permute-start(bf16[8,12,8,128]{3,2,1,0:T(8,128)(2,1)S(1)} %slice.8.refs_7_), channel_id=1, source_target_pairs={{0,24},{8,0},{16,8},{24,16},{1,25},{9,1},{17,9},{25,17},{2,26},{10... | collective-permute-start | bytes 589832 | tf_op jit(solution)/shard_map/ppermute | solution.py:500
  32.1 18.4 %collective-permute-start.1 = (bf16[8,12,8,128]{3,2,1,0:T(8,128)(2,1)S(1)}, bf16[8,12,8,128]{3,2,1,0:T(8,128)(2,1)S(1)}, u32[]{:S(2)}, u32[]{:S(2)}) collective-permute-start(bf16[8,12,8,128]{3,2,1,0:T(8,128)(2,1)S(1)} %slice.8.refs_7_), channel_id=1, source_target_pairs={{0,16},{8,24},{16,0},{24,8},{1,17},{9,25},{17,1},{25,9},{2,18},{10... | collective-permute-start | bytes 589832 | tf_op jit(solution)/shard_map/ppermute | solution.py:500
  34.0 16.5 %collective-permute-start = (bf16[8,12,8,128]{3,2,1,0:T(8,128)(2,1)S(1)}, bf16[8,12,8,128]{3,2,1,0:T(8,128)(2,1)S(1)}, u32[]{:S(2)}, u32[]{:S(2)}) collective-permute-start(bf16[8,12,8,128]{3,2,1,0:T(8,128)(2,1)S(1)} %slice.8.refs_7_), channel_id=1, source_target_pairs={{0,8},{8,16},{16,24},{24,0},{1,9},{9,17},{17,25},{25,1},{2,10},{10... | collective-permute-start | bytes 589832 | tf_op jit(solution)/shard_map/ppermute | solution.py:500
  50.5 29.1 %copy-start = (bf16[1,1,2,8,4096]{4,3,2,1,0:T(8,128)(2,1)S(1)}, bf16[1,1,2,8,4096]{4,3,2,1,0:T(8,128)(2,1)}, u32[]{:S(2)}) copy-start(bf16[1,1,2,8,4096]{4,3,2,1,0:T(8,128)(2,1)} %param.14) | copy-start | bytes 393220
  50.5 29.1 %copy-start.2 = (s32[1,1,2]{2,1,0:T(1,128)S(1)}, s32[1,1,2]{2,1,0:T(1,128)}, u32[]{:S(2)}) copy-start(s32[1,1,2]{2,1,0:T(1,128)} %counts.5) | copy-start | bytes 28
  57.8 23.0 %collective-permute-start.6 = (bf16[8,24,8,128]{3,2,1,0:T(8,128)(2,1)S(1)}, bf16[8,24,8,128]{3,2,1,0:T(8,128)(2,1)S(1)}, u32[]{:S(2)}, u32[]{:S(2)}) collective-permute-start(bf16[8,24,8,128]{3,2,1,0:T(8,128)(2,1)S(1)} %bitcast.24), channel_id=1, source_target_pairs={{0,24},{8,0},{16,8},{24,16},{1,25},{9,1},{17,9},{25,17},{2,26},{10... | collective-permute-start | bytes 1179656 | tf_op jit(solution)/shard_map/ppermute | solution.py:500
  57.9 23.0 %collective-permute-start.7 = (bf16[8,24,8,128]{3,2,1,0:T(8,128)(2,1)S(1)}, bf16[8,24,8,128]{3,2,1,0:T(8,128)(2,1)S(1)}, u32[]{:S(2)}, u32[]{:S(2)}) collective-permute-start(bf16[8,24,8,128]{3,2,1,0:T(8,128)(2,1)S(1)} %bitcast.25), channel_id=1, source_target_pairs={{0,16},{8,24},{16,0},{24,8},{1,17},{9,25},{17,1},{25,9},{2,18},{10... | collective-permute-start | bytes 1179656 | tf_op jit(solution)/shard_map/ppermute | solution.py:500
  58.0 22.9 %collective-permute-start.8 = (bf16[8,24,8,128]{3,2,1,0:T(8,128)(2,1)S(1)}, bf16[8,24,8,128]{3,2,1,0:T(8,128)(2,1)S(1)}, u32[]{:S(2)}, u32[]{:S(2)}) collective-permute-start(bf16[8,24,8,128]{3,2,1,0:T(8,128)(2,1)S(1)} %bitcast.26), channel_id=1, source_target_pairs={{0,8},{8,16},{16,24},{24,0},{1,9},{9,17},{17,25},{25,1},{2,10},{10... | collective-permute-start | bytes 1179656 | tf_op jit(solution)/shard_map/ppermute | solution.py:500
  80.9 2.0 %collective-permute-start.9 = (bf16[16,12,8,128]{3,2,1,0:T(8,128)(2,1)S(1)}, bf16[16,12,8,128]{3,2,1,0:T(8,128)(2,1)S(1)}, u32[]{:S(2)}, u32[]{:S(2)}) collective-permute-start(bf16[16,12,8,128]{3,2,1,0:T(8,128)(2,1)S(1)} %get-tuple-element.63), channel_id=1, source_target_pairs={{0,1},{1,0},{2,3},{3,2},{4,5},{5,4},{6,7},{7,6},{8,9},{9,8},{10,11... | collective-permute-start | bytes 1179656 | tf_op jit(solution)/shard_map/ppermute | solution.py:504
  127.8 6.4 %collective-permute-start.10 = (bf16[16,12,8,128]{3,2,1,0:T(8,128)(2,1)S(1)}, bf16[16,12,8,128]{3,2,1,0:T(8,128)(2,1)S(1)}, u32[]{:S(2)}, u32[]{:S(2)}) collective-permute-start(bf16[16,12,8,128]{3,2,1,0:T(8,128)(2,1)S(1)} %all_to_all.29.mine), channel_id=1, source_target_pairs={{0,1},{1,0},{2,3},{3,2},{4,5},{5,4},{6,7},{7,6},{8,9},{9,8},{10,11... | collective-permute-start | bytes 1179656 | tf_op jit(solution)/shard_map/ppermute | solution.py:504

commit v9 on v8

--- a/solution.py
+++ b/solution.py
@@ -235,18 +235,19 @@
         cols = slice(n * HD, (n + 1) * HD)
         grad_key[:, :, cols] = key_grad[:NEAR].astype(bf16).reshape(2, SPAN, HD)
         grad_value[:, :, cols] = value_grad[:NEAR].astype(bf16).reshape(2, SPAN, HD)
+        first, h = (3 if last else 0), g * STEP + n
         for b, out in enumerate(outs):
             at = NEAR + b * 64
-            out[:, 0, n] = key_grad[at : at + 64].reshape(NZ, 8, HD).astype(bf16)
-            out[:, 1, n] = value_grad[at : at + 64].reshape(NZ, 8, HD).astype(bf16)
+            out[:, first, h] = key_grad[at : at + 64].reshape(NZ, 8, HD).astype(bf16)
+            out[:, first + 1, h] = value_grad[at : at + 64].reshape(NZ, 8, HD).astype(bf16)
             at = NEAR + 256 + b * 32
             k = key_grad[at : at + 32].reshape(NZ // 2, 8, HD)
             v = value_grad[at : at + 32].reshape(NZ // 2, 8, HD)
             even = jnp.where(sub < 4, k, pltpu.roll(v, 4, 1)).astype(bf16)
             odd = jnp.where(sub < 4, pltpu.roll(k, 4, 1), v).astype(bf16)
             for i in range(NZ // 2):
-                out[2 * i, 2, n] = even[i]
-                out[2 * i + 1, 2, n] = odd[i]
+                out[2 * i, first + 2, h] = even[i]
+                out[2 * i + 1, first + 2, h] = odd[i]
         far_keys = key_grad[NEAR:].astype(bf16)
         far_values = value_grad[NEAR:].astype(bf16)
         far = jnp.concatenate([far_keys, far_values], axis=1)
@@ -312,8 +313,8 @@
     at = half * HEADS // STEP
     wide = pl.BlockSpec((2, SPAN, STEP * GROUP * HD), lambda g: (0, 0, g + at))
     narrow = pl.BlockSpec((2, SPAN, STEP * HD), lambda g: (0, 0, g + at))
-    whole = pl.BlockSpec(boxes[0].shape, lambda g: (0, 0, 0, 0))
-    part = pl.BlockSpec((NZ, 3, STEP, 8, HD), lambda g: (0, half, g, 0, 0))
+    whole = VMEM
+    part = VMEM
     up_key = pl.BlockSpec((UPDATE_RANK, STEP * HD), lambda g: (0, g + at))
     up_value = pl.BlockSpec((UPDATE_RANK, STEP * HD), lambda g: (0, KVH // STEP + g + at))
     up_part = pl.BlockSpec((UPDATE_RANK, STEP * HD), lambda g: (0, g))
@@ -327,17 +328,16 @@
         jax.ShapeDtypeStruct((KEYS, NEAR), f32),
         jax.ShapeDtypeStruct((UPDATE_RANK, FAR), bf16),
     ]
-    kept_specs = [pl.BlockSpec(k.shape, lambda g: (0, 0)) for k in kept]
     in_specs = [SMEM] * len(small) + [wide, narrow, narrow, wide, up_key, up_value] + [whole] * NX
     out_specs = [wide, wide, narrow, narrow] + [part] * NX + [up_part] * 2
     out_shape = [wide_shape] * 2 + [narrow_shape] * 2
     out_shape += [part_shape] * NX + [up_shape] * 2
     scratch, aliases = [], {}
     if half == 0:
-        out_specs += kept_specs
+        out_specs += [VMEM] * 3
         out_shape += kept
     else:
-        in_specs += kept_specs[1:] + kept_specs[:1] + [pl.BlockSpec(memory_space=pl.ANY)] * 8
+        in_specs += [VMEM] * 3 + [pl.BlockSpec(memory_space=pl.ANY)] * 4 + [VMEM] * 4
         out_specs.append(low_part)
         out_shape.append(jax.ShapeDtypeStruct((NZ, NX, 8, HD), bf16))
         scratch = [pltpu.VMEM((FAR, HD), f32)]
@@ -472,21 +472,22 @@
 
 
 def unpack_kernel(place, mine, other, out):
-    lower = place[2] == 0
+    own = pl.program_id(0) == place[2]
     for t in range(HALF):
-        a = mine[t // CHUNK, t % CHUNK].astype(f32)
-        b = other[t // CHUNK, t % CHUNK].astype(f32)
-        for at, tile in ((t, jnp.where(lower, a, b)), (t + HALF, jnp.where(lower, b, a))):
-            r, c = divmod(at, PER_ROW)
-            out[r * 8 : r * 8 + 8, c * HD : (c + 1) * HD] = tile
+        r, c = divmod(t, PER_ROW)
+        at = t // CHUNK, t % CHUNK
+        tile = jnp.where(own, mine[at].astype(f32), other[at].astype(f32))
+        out[r * 8 : r * 8 + 8, c * HD : (c + 1) * HD] = tile
 
 
 def unpack(place, mine, other):
+    wide = MODEL_WIDTH + 2 * KEY_FEATURES
     return pl.pallas_call(
         unpack_kernel,
+        grid=(NC,),
         in_specs=[SMEM] + [VMEM] * 2,
-        out_specs=VMEM,
-        out_shape=jax.ShapeDtypeStruct((UPDATE_RANK, MODEL_WIDTH + 2 * KEY_FEATURES), f32),
+        out_specs=pl.BlockSpec((UPDATE_RANK // NC, wide), lambda half: (half, 0)),
+        out_shape=jax.ShapeDtypeStruct((UPDATE_RANK, wide), f32),
         compiler_params=SMALL,
         name="unpack",
     )(place, mine, other)

time: 136 us -> 136 us (level)
  no operation moved by 1% of the time
where the time goes in v9:
time: 136 us
  blocking collectives  87.6 us (64%)
  Pallas kernels  22 us (16%)
  starting transfers between devices  14.2 us (10%)
  waiting for transfers between devices  11 us (8%)
    all_to_all x5, blocking collectives, exchange(): return lax.all_to_all(x, axes, 0, 0, tiled=True)  87.6 us
    pallas_call x2, Pallas kernels, attend(): pl.pallas_call((first_kernel, second_kernel)[half], grid=(HEADS // STEP,)...  14.7 us
    ppermute x9, waiting for transfers between devices, shift(): return lax.ppermute(x, 'x', [(i, (i + by) % NX) for i in range(NX)])  9.62 us
    ppermute x9, starting transfers between devices, shift(): return lax.ppermute(x, 'x', [(i, (i + by) % NX) for i in range(NX)])  8.58 us
    ppermute x2, starting transfers between devices, swap(): return lax.ppermute(x, 'core', [(0, 1), (1, 0)])  5.63 us
  transfers between devices with their start and end apart: 11, of which 4 were waited for; matrix products, arithmetic and copies ran while one was open for 0% of the time, Pallas kernels for 7%

profile of v9, /device:TPU:1, one launch (start us, length us, event | category | flops | bytes accessed | tf_op | source)
XLA Modules:
  0.0 135.9 jit_solution(15083864022710762506)
XLA Ops:
  0.7 2.7 %project.1 = bf16[8,25,8,128]{3,2,1,0:T(8,128)(2,1)} custom-call(s32[1,1,2]{2,1,0:T(1,128)} %counts.5, s32[1,1,2]{2,1,0:T(1,128)} %refs_1_.1, bf16[16,4096]{1,0:T(8,128)(2,1)} %bitcast.20, bf16[64,4096]{1,0:T(8,128)(2,1)} %bitcast.27, bf16[64,2048]{1,0:T(8,128)(2,1)} %refs_6_.1, bf16[16,2048]{1,0:T(8,128)(2,1)} %bitcast.28), custom_call_target="tpu_custom_call" | custom-call | tf_op jit(solution)/shard_map/project/pallas_call | solution.py:87
  3.4 22.8 %all_to_all.25 = bf16[8,25,8,128]{3,2,1,0:T(8,128)(2,1)S(1)} all-to-all(bf16[8,25,8,128]{3,2,1,0:T(8,128)(2,1)} %project.1), channel_id=1, replica_groups=mesh['z'=8,'x'=4,'y'=4,'core'=2] {'z'}, dimensions={0} | all-to-all | bytes 819200 | tf_op jit(solution)/shard_map/all_to_all | solution.py:497
  26.2 2.6 %collective-permute-start.5 = (bf16[8,13,8,128]{3,2,1,0:T(8,128)(2,1)S(1)}, bf16[8,13,8,128]{3,2,1,0:T(8,128)(2,1)S(1)}, u32[]{:S(2)}, u32[]{:S(2)}) collective-permute-start(bf16[8,13,8,128]{3,2,1,0:T(8,128)(2,1)S(1)} %slice.9.refs_9_), channel_id=1, source_target_pairs={{0,24},{8,0},{16,8},{24,16},{1,25},{9,1},{17,9},{25,17},{2,26},{10... | collective-permute-start | bytes 638984 | tf_op jit(solution)/shard_map/ppermute | solution.py:501
  28.7 0.5 collective-permute-start.4
  29.2 0.6 collective-permute-start.3
  29.9 2.1 %collective-permute-start.2 = (bf16[8,12,8,128]{3,2,1,0:T(8,128)(2,1)S(1)}, bf16[8,12,8,128]{3,2,1,0:T(8,128)(2,1)S(1)}, u32[]{:S(2)}, u32[]{:S(2)}) collective-permute-start(bf16[8,12,8,128]{3,2,1,0:T(8,128)(2,1)S(1)} %slice.8.refs_7_), channel_id=1, source_target_pairs={{0,24},{8,0},{16,8},{24,16},{1,25},{9,1},{17,9},{25,17},{2,26},{10... | collective-permute-start | bytes 589832 | tf_op jit(solution)/shard_map/ppermute | solution.py:501
  32.1 1.2 collective-permute-start.1
  33.3 0.7 collective-permute-done.5.refs_12_
  34.0 1.0 collective-permute-done.4.refs_11_
  35.0 7.9 %collective-permute-done.3.refs_10_ = bf16[8,13,8,128]{3,2,1,0:T(8,128)(2,1)S(1)} collective-permute-done((bf16[8,13,8,128]{3,2,1,0:T(8,128)(2,1)S(1)}, bf16[8,13,8,128]{3,2,1,0:T(8,128)(2,1)S(1)}, u32[]{:S(2)}, u32[]{:S(2)}) %collective-permute-start.3) | collective-permute-done | bytes 213024 | tf_op jit(solution)/shard_map/ppermute | solution.py:501
  42.9 7.5 %attend_first.1 = (bf16[2,64,4096]{2,1,0:T(8,128)(2,1)}, bf16[2,64,4096]{2,1,0:T(8,128)(2,1)}, bf16[2,64,1024]{2,1,0:T(8,128)(2,1)}, bf16[2,64,1024]{2,1,0:T(8,1...) custom-call(s32[3]{0:T(128)S(1)} %pad_add_fusion.refs_0_.place, ...), custom_call_target="tpu_custom_call" | custom-call | flops 6000000000 | bytes 4194304 | tf_op jit(solution)/shard_map/attend_first/pallas_call | solution.py:345
  50.5 7.2 %attend_second.1 = (bf16[2,64,4096]{2,1,0:T(8,128)(2,1)}, bf16[2,64,4096]{2,1,0:T(8,128)(2,1)}, bf16[2,64,1024]{2,1,0:T(8,128)(2,1)}, bf16[2,64,1024]{2,1,0:T(8,...) custom-call(s32[3]{0:T(128)S(1)} %pad_add_fusion.refs_0_.place, ...), custom_call_target="tpu_custom_call", output_to_operand_aliasing={{0}: (14, {}), {1}: (15, {}), {2}: (16, {}), {3}: (17, {}),... | custom-call | flops 6000000000 | bytes 4194304 | tf_op jit(solution)/shard_map/attend_second/pallas_call | solution.py:345
  57.9 1.4 collective-permute-start.8
  59.2 20.3 %all_to_all.26.low_parts = bf16[32,8,128]{2,1,0:T(8,128)(2,1)S(1)} all-to-all(bf16[32,8,128]{2,1,0:T(8,128)(2,1)S(1)} %bitcast.23), channel_id=1, replica_groups=mesh['z'=8,'x'=4,'y'=4,'core'=2] {'z','x'}, dimensions={0} | all-to-all | bytes 131072 | tf_op jit(solution)/shard_map/all_to_all | solution.py:497
  79.5 1.2 factor.1
  80.8 0.6 collective-permute-start.9
  81.4 1.3 collective-permute-done.9
  82.9 13.8 %all_to_all.27.pieces = bf16[16,12,8,128]{3,2,1,0:T(8,128)(2,1)S(1)} all-to-all(bf16[16,12,8,128]{3,2,1,0:T(8,128)(2,1)S(1)} %add_convert_fusion), channel_id=1, replica_groups=mesh['z'=8,'x'=4,'y'=4,'core'=2] {'x','y'}, dimensions={0} | all-to-all | bytes 786432 | tf_op jit(solution)/shard_map/all_to_all | solution.py:497
  96.6 0.2 middle.1
  96.9 19.2 %all_to_all.28.parts = bf16[8,36,8,128]{3,2,1,0:T(8,128)(2,1)S(1)} all-to-all(bf16[8,36,8,128]{3,2,1,0:T(8,128)(2,1)S(1)} %middle.1), channel_id=1, replica_groups=mesh['z'=8,'x'=4,'y'=4,'core'=2] {'z'}, dimensions={0} | all-to-all | bytes 1179648 | tf_op jit(solution)/shard_map/all_to_all | solution.py:497
  116.1 11.6 %all_to_all.29.mine = bf16[16,12,8,128]{3,2,1,0:T(8,128)(2,1)S(1)} all-to-all(bf16[16,12,8,128]{3,2,1,0:T(8,128)(2,1)S(1)} %spread_chunk.1), channel_id=1, replica_groups=mesh['z'=8,'x'=4,'y'=4,'core'=2] {'x','y'}, dimensions={0} | all-to-all | bytes 786432 | tf_op jit(solution)/shard_map/all_to_all | solution.py:497
  127.7 5.0 %collective-permute-start.10 = (bf16[16,12,8,128]{3,2,1,0:T(8,128)(2,1)S(1)}, bf16[16,12,8,128]{3,2,1,0:T(8,128)(2,1)S(1)}, u32[]{:S(2)}, u32[]{:S(2)}) collective-permute-start(bf16[16,12,8,128]{3,2,1,0:T(8,128)(2,1)S(1)} %all_to_all.29.mine), channel_id=1, source_target_pairs={{0,1},{1,0},{2,3},{3,2},{4,5},{5,4},{6,7},{7,6},{8,9},{9,8},{10,11... | collective-permute-start | bytes 1179656 | tf_op jit(solution)/shard_map/ppermute | solution.py:505
  132.7 1.4 %cache.1 = bf16[16,2048]{1,0:T(8,128)(2,1)} custom-call(s32[1,1,2]{2,1,0:T(1,128)S(1)} %copy-done.2, bf16[8,36,8,128]{3,2,1,0:T(8,128)(2,1)S(1)} %all_to_all.28.parts), custom_call_target="tpu_custom_call" | custom-call | tf_op jit(solution)/shard_map/cache/pallas_call | solution.py:464
  134.1 1.8 %unpack.1 = f32[64,6144]{1,0:T(8,128)} custom-call(s32[3]{0:T(128)S(1)} %pad_add_fusion.refs_0_.place, bf16[16,12,8,128]{3,2,1,0:T(8,128)(2,1)S(1)} %all_to_all.29.mine, bf16[16,12,8,128]{3,2,1,0:T(8,128)(2,1)S(1)} %collective-permute-done.10.other), custom_call_target="tpu_custom_call" | custom-call | tf_op jit(solution)/shard_map/unpack/pallas_call | solution.py:485
  (25 shorter events, 0.4 us)
Async XLA Ops:
  0.6 42.3 %copy-start.1 = (bf16[64,2048]{1,0:T(8,128)(2,1)S(1)}, bf16[64,2048]{1,0:T(8,128)(2,1)}, u32[]{:S(2)}) copy-start(bf16[64,2048]{1,0:T(8,128)(2,1)} %refs_6_.1) | copy-start | bytes 786436
  0.6 42.3 %copy-start.3 = (s32[1,1,2]{2,1,0:T(1,128)S(1)}, s32[1,1,2]{2,1,0:T(1,128)}, u32[]{:S(2)}) copy-start(s32[1,1,2]{2,1,0:T(1,128)} %refs_1_.1) | copy-start | bytes 28
  0.7 42.3 %copy-start.4 = (s32[1,1,2]{2,1,0:T(1,128)S(1)}, s32[1,1,2]{2,1,0:T(1,128)}, u32[]{:S(2)}) copy-start(s32[1,1,2]{2,1,0:T(1,128)} %refs_2_.1) | copy-start | bytes 28
  26.2 7.8 %collective-permute-start.5 = (bf16[8,13,8,128]{3,2,1,0:T(8,128)(2,1)S(1)}, bf16[8,13,8,128]{3,2,1,0:T(8,128)(2,1)S(1)}, u32[]{:S(2)}, u32[]{:S(2)}) collective-permute-start(bf16[8,13,8,128]{3,2,1,0:T(8,128)(2,1)S(1)} %slice.9.refs_9_), channel_id=1, source_target_pairs={{0,24},{8,0},{16,8},{24,16},{1,25},{9,1},{17,9},{25,17},{2,26},{10... | collective-permute-start | bytes 638984 | tf_op jit(solution)/shard_map/ppermute | solution.py:501
  28.7 6.3 %collective-permute-start.4 = (bf16[8,13,8,128]{3,2,1,0:T(8,128)(2,1)S(1)}, bf16[8,13,8,128]{3,2,1,0:T(8,128)(2,1)S(1)}, u32[]{:S(2)}, u32[]{:S(2)}) collective-permute-start(bf16[8,13,8,128]{3,2,1,0:T(8,128)(2,1)S(1)} %slice.9.refs_9_), channel_id=1, source_target_pairs={{0,16},{8,24},{16,0},{24,8},{1,17},{9,25},{17,1},{25,9},{2,18},{10... | collective-permute-start | bytes 638984 | tf_op jit(solution)/shard_map/ppermute | solution.py:501
  29.2 13.7 %collective-permute-start.3 = (bf16[8,13,8,128]{3,2,1,0:T(8,128)(2,1)S(1)}, bf16[8,13,8,128]{3,2,1,0:T(8,128)(2,1)S(1)}, u32[]{:S(2)}, u32[]{:S(2)}) collective-permute-start(bf16[8,13,8,128]{3,2,1,0:T(8,128)(2,1)S(1)} %slice.9.refs_9_), channel_id=1, source_target_pairs={{0,8},{8,16},{16,24},{24,0},{1,9},{9,17},{17,25},{25,1},{2,10},{10... | collective-permute-start | bytes 638984 | tf_op jit(solution)/shard_map/ppermute | solution.py:501
  29.9 20.5 %collective-permute-start.2 = (bf16[8,12,8,128]{3,2,1,0:T(8,128)(2,1)S(1)}, bf16[8,12,8,128]{3,2,1,0:T(8,128)(2,1)S(1)}, u32[]{:S(2)}, u32[]{:S(2)}) collective-permute-start(bf16[8,12,8,128]{3,2,1,0:T(8,128)(2,1)S(1)} %slice.8.refs_7_), channel_id=1, source_target_pairs={{0,24},{8,0},{16,8},{24,16},{1,25},{9,1},{17,9},{25,17},{2,26},{10... | collective-permute-start | bytes 589832 | tf_op jit(solution)/shard_map/ppermute | solution.py:501
  32.1 18.3 %collective-permute-start.1 = (bf16[8,12,8,128]{3,2,1,0:T(8,128)(2,1)S(1)}, bf16[8,12,8,128]{3,2,1,0:T(8,128)(2,1)S(1)}, u32[]{:S(2)}, u32[]{:S(2)}) collective-permute-start(bf16[8,12,8,128]{3,2,1,0:T(8,128)(2,1)S(1)} %slice.8.refs_7_), channel_id=1, source_target_pairs={{0,16},{8,24},{16,0},{24,8},{1,17},{9,25},{17,1},{25,9},{2,18},{10... | collective-permute-start | bytes 589832 | tf_op jit(solution)/shard_map/ppermute | solution.py:501
  34.0 16.4 %collective-permute-start = (bf16[8,12,8,128]{3,2,1,0:T(8,128)(2,1)S(1)}, bf16[8,12,8,128]{3,2,1,0:T(8,128)(2,1)S(1)}, u32[]{:S(2)}, u32[]{:S(2)}) collective-permute-start(bf16[8,12,8,128]{3,2,1,0:T(8,128)(2,1)S(1)} %slice.8.refs_7_), channel_id=1, source_target_pairs={{0,8},{8,16},{16,24},{24,0},{1,9},{9,17},{17,25},{25,1},{2,10},{10... | collective-permute-start | bytes 589832 | tf_op jit(solution)/shard_map/ppermute | solution.py:501
  50.4 29.1 %copy-start = (bf16[1,1,2,8,4096]{4,3,2,1,0:T(8,128)(2,1)S(1)}, bf16[1,1,2,8,4096]{4,3,2,1,0:T(8,128)(2,1)}, u32[]{:S(2)}) copy-start(bf16[1,1,2,8,4096]{4,3,2,1,0:T(8,128)(2,1)} %param.14) | copy-start | bytes 393220
  50.5 29.0 %copy-start.2 = (s32[1,1,2]{2,1,0:T(1,128)S(1)}, s32[1,1,2]{2,1,0:T(1,128)}, u32[]{:S(2)}) copy-start(s32[1,1,2]{2,1,0:T(1,128)} %counts.5) | copy-start | bytes 28
  57.7 23.0 %collective-permute-start.6 = (bf16[8,24,8,128]{3,2,1,0:T(8,128)(2,1)S(1)}, bf16[8,24,8,128]{3,2,1,0:T(8,128)(2,1)S(1)}, u32[]{:S(2)}, u32[]{:S(2)}) collective-permute-start(bf16[8,24,8,128]{3,2,1,0:T(8,128)(2,1)S(1)} %bitcast.24), channel_id=1, source_target_pairs={{0,24},{8,0},{16,8},{24,16},{1,25},{9,1},{17,9},{25,17},{2,26},{10... | collective-permute-start | bytes 1179656 | tf_op jit(solution)/shard_map/ppermute | solution.py:501
  57.8 23.0 %collective-permute-start.7 = (bf16[8,24,8,128]{3,2,1,0:T(8,128)(2,1)S(1)}, bf16[8,24,8,128]{3,2,1,0:T(8,128)(2,1)S(1)}, u32[]{:S(2)}, u32[]{:S(2)}) collective-permute-start(bf16[8,24,8,128]{3,2,1,0:T(8,128)(2,1)S(1)} %bitcast.25), channel_id=1, source_target_pairs={{0,16},{8,24},{16,0},{24,8},{1,17},{9,25},{17,1},{25,9},{2,18},{10... | collective-permute-start | bytes 1179656 | tf_op jit(solution)/shard_map/ppermute | solution.py:501
  57.9 22.9 %collective-permute-start.8 = (bf16[8,24,8,128]{3,2,1,0:T(8,128)(2,1)S(1)}, bf16[8,24,8,128]{3,2,1,0:T(8,128)(2,1)S(1)}, u32[]{:S(2)}, u32[]{:S(2)}) collective-permute-start(bf16[8,24,8,128]{3,2,1,0:T(8,128)(2,1)S(1)} %bitcast.26), channel_id=1, source_target_pairs={{0,8},{8,16},{16,24},{24,0},{1,9},{9,17},{17,25},{25,1},{2,10},{10... | collective-permute-start | bytes 1179656 | tf_op jit(solution)/shard_map/ppermute | solution.py:501
  80.8 2.0 %collective-permute-start.9 = (bf16[16,12,8,128]{3,2,1,0:T(8,128)(2,1)S(1)}, bf16[16,12,8,128]{3,2,1,0:T(8,128)(2,1)S(1)}, u32[]{:S(2)}, u32[]{:S(2)}) collective-permute-start(bf16[16,12,8,128]{3,2,1,0:T(8,128)(2,1)S(1)} %get-tuple-element.63), channel_id=1, source_target_pairs={{0,1},{1,0},{2,3},{3,2},{4,5},{5,4},{6,7},{7,6},{8,9},{9,8},{10,11... | collective-permute-start | bytes 1179656 | tf_op jit(solution)/shard_map/ppermute | solution.py:505
  127.7 6.4 %collective-permute-start.10 = (bf16[16,12,8,128]{3,2,1,0:T(8,128)(2,1)S(1)}, bf16[16,12,8,128]{3,2,1,0:T(8,128)(2,1)S(1)}, u32[]{:S(2)}, u32[]{:S(2)}) collective-permute-start(bf16[16,12,8,128]{3,2,1,0:T(8,128)(2,1)S(1)} %all_to_all.29.mine), channel_id=1, source_target_pairs={{0,1},{1,0},{2,3},{3,2},{4,5},{5,4},{6,7},{7,6},{8,9},{9,8},{10,11... | collective-permute-start | bytes 1179656 | tf_op jit(solution)/shard_map/ppermute | solution.py:505
